TPU v7x, 128 devices: a whole 4x4x4 slice. The times are simulated.
128 devices in a mesh: dp: 16 (over x, y), expert: 8 (over z, core).
Axes of the slice: x: 4, y: 4, z: 4, core: 2. Of those that a mesh axis runs over, the one named last changes fastest.
Arguments:
- tokens: bfloat16 [32768, 1024], P(('dp', 'expert')), may hold values from -6 to 6
- cotangent: bfloat16 [32768, 1024], P(('dp', 'expert')), may hold values from -6 to 6
- segments: int32 [16, 2048], P('dp', 'expert'), may hold values from 0 to 15, never falling along the last dimension, each value on 1 to 1024 neighbouring positions
- routes: int32 [16, 2048], P('dp', 'expert'), may hold values from 0 to 7, as said below
- attngain: bfloat16 [1024], replicated, may hold values from 0.5 to 1.5
- attnshift: bfloat16 [1024], replicated, may hold values from -0.59765625 to 0.59765625
- querymat: bfloat16 [1024, 1024], replicated, may hold values from -0.25 to 0.25
- querybias: bfloat16 [1024], replicated, may hold values from -0.59765625 to 0.59765625
- keymat: bfloat16 [1024, 1024], replicated, may hold values from -0.25 to 0.25
- valuemat: bfloat16 [1024, 1024], replicated, may hold values from -0.1875 to 0.1875
- valuebias: bfloat16 [1024], replicated, may hold values from -0.59765625 to 0.59765625
- outmat: bfloat16 [1024, 1024], replicated, may hold values from -0.75 to 0.75
- outbias: bfloat16 [1024], replicated, may hold values from -0.59765625 to 0.59765625
- frontgain: bfloat16 [8, 1024], P('expert', 'dp'), may hold values from 0.5 to 1.5
- frontshift: bfloat16 [8, 1024], P('expert', 'dp'), may hold values from -0.59765625 to 0.59765625
- frontexpand: bfloat16 [8, 1024, 4096], P('expert', None, 'dp'), may hold values from -0.1875 to 0.1875
- frontlift: bfloat16 [8, 4096], P('expert', 'dp'), may hold values from -0.59765625 to 0.59765625
- frontreduce: bfloat16 [8, 4096, 1024], P('expert', 'dp'), may hold values from -0.125 to 0.125
- frontoffset: bfloat16 [8, 1024], P('expert', 'dp'), may hold values from -0.59765625 to 0.59765625
- backgain: bfloat16 [8, 1024], P('expert', 'dp'), may hold values from 0.5 to 1.5
- backshift: bfloat16 [8, 1024], P('expert', 'dp'), may hold values from -0.59765625 to 0.59765625
- backexpand: bfloat16 [8, 1024, 4096], P('expert', None, 'dp'), may hold values from -0.1875 to 0.1875
- backlift: bfloat16 [8, 4096], P('expert', 'dp'), may hold values from -0.59765625 to 0.59765625
- backreduce: bfloat16 [8, 4096, 1024], P('expert', 'dp'), may hold values from -0.125 to 0.125
- backoffset: bfloat16 [8, 1024], P('expert', 'dp'), may hold values from -0.59765625 to 0.59765625
- centroid: bfloat16 [8, 1024], P('expert', 'dp'), may hold values from -0.125 to 0.125
Outputs:
- result: bfloat16 [32768, 1024], P(('dp', 'expert'))
- tokens_grad: float32 [32768, 1024], P(('dp', 'expert'))
- attngain_grad: float32 [1024], replicated
- attnshift_grad: float32 [1024], replicated
- querymat_grad: float32 [1024, 1024], replicated
- querybias_grad: float32 [1024], replicated
- keymat_grad: float32 [1024, 1024], replicated
- valuemat_grad: float32 [1024, 1024], replicated
- valuebias_grad: float32 [1024], replicated
- outmat_grad: float32 [1024, 1024], replicated
- outbias_grad: float32 [1024], replicated
- frontgain_grad: float32 [8, 1024], P('expert', 'dp')
- frontshift_grad: float32 [8, 1024], P('expert', 'dp')
- frontexpand_grad: float32 [8, 1024, 4096], P('expert', None, 'dp')
- frontlift_grad: float32 [8, 4096], P('expert', 'dp')
- frontreduce_grad: float32 [8, 4096, 1024], P('expert', 'dp')
- frontoffset_grad: float32 [8, 1024], P('expert', 'dp')
- backgain_grad: float32 [8, 1024], P('expert', 'dp')
- backshift_grad: float32 [8, 1024], P('expert', 'dp')
- backexpand_grad: float32 [8, 1024, 4096], P('expert', None, 'dp')
- backlift_grad: float32 [8, 4096], P('expert', 'dp')
- backreduce_grad: float32 [8, 4096, 1024], P('expert', 'dp')
- backoffset_grad: float32 [8, 1024], P('expert', 'dp')
- centroid_grad: float32 [8, 1024], P('expert', 'dp')
Inputs may be any that keep to these rules, and one draw needn't show every extreme that they name: `routes`: every expert gets exactly 256 tokens of each sequence. Among the 256 tokens of one device (tokens d * 256 to (d + 1) * 256 - 1 of a sequence), one expert gets exactly 48, one other gets 2 * 32 - 48, and each remaining expert 256 // 8; which experts and which tokens vary.
All inputs are finite; a program needn't handle non-finite values.
Results may differ from a plain program's by a relative error of at most 0.018.
Values may be sent and summed in bfloat16 or wider, within the bound.
No kernel may reach another device: no remote copies, remote signals or barrier semaphores. Data moves between devices by JAX's collectives and lax.ppermute only.
A program may use at most 256 MiB of HBM per device.

v0:
```python
import jax
import jax.numpy as jnp
from jax import lax
from jax.sharding import PartitionSpec as P

HEADS = 16
HEAD_DIM = 64


epsilon = 1e-05


def norm_rows(stream, gain_vec, shift_vec):
    center = stream - jnp.mean(stream, -1, keepdims=True)
    variance = jnp.mean(center * center, -1, keepdims=True)
    return center * lax.rsqrt(variance + epsilon) * gain_vec + shift_vec


def matmul(left, right):
    return jnp.dot(left, right, preferred_element_type=jnp.float32)


def matmul_left(left, right):
    return lax.dot_general(
        left, right, (((0,), (0,)), ((), ())), preferred_element_type=jnp.float32
    )


def matmul_right(left, right):
    return lax.dot_general(
        left, right, (((1,), (1,)), ((), ())), preferred_element_type=jnp.float32
    )


def gelu_exact(value):
    return jax.nn.gelu(value, approximate=False)


def sublayer(stream, gain_vec, shift_vec, expand, lift, shrink, offset):
    normed_rows = norm_rows(stream, gain_vec, shift_vec).astype(jnp.bfloat16)
    hidden_pre = matmul(normed_rows, expand) + lift
    active = gelu_exact(hidden_pre).astype(jnp.bfloat16)
    branch = matmul(active, shrink) + offset
    return (normed_rows, hidden_pre, active, branch)


def sublayer_back(stream, gain_vec, normed_rows, hidden_pre, active, expand, shrink, branch_grad):
    branch_low = branch_grad.astype(jnp.bfloat16)
    active_grad = matmul_right(branch_low, shrink)
    _, gelu_pull = jax.vjp(gelu_exact, hidden_pre)
    hidden_low = gelu_pull(active_grad)[0].astype(jnp.bfloat16)
    normed_grad = matmul_right(hidden_low, expand)
    _, norm_pull = jax.vjp(norm_rows, stream, gain_vec, jnp.zeros_like(gain_vec))
    stream_grad, gain_grad, shift_grad = norm_pull(normed_grad)
    return (stream_grad, gain_grad, shift_grad, (normed_rows, hidden_low, active, branch_low))


def per_device(
    tokens,
    cotangent,
    segments,
    routes,
    attngain,
    attnshift,
    querymat,
    querybias,
    keymat,
    valuemat,
    valuebias,
    outmat,
    outbias,
    frontgain,
    frontshift,
    frontexpand,
    frontlift,
    frontreduce,
    frontoffset,
    backgain,
    backshift,
    backexpand,
    backlift,
    backreduce,
    backoffset,
    centroid,
):
    wide = jnp.float32
    narrow = jnp.bfloat16
    row_count = tokens.shape[0]
    width = tokens.shape[1]
    experts = lax.axis_size("expert")
    my_expert = lax.axis_index("expert")
    capacity = row_count // experts + row_count // (2 * experts)
    block_heads = 4
    block_width = block_heads * HEAD_DIM
    head_blocks = HEADS // block_heads
    scale = HEAD_DIM ** (-0.5)
    inputs = tokens.astype(wide)
    attn_gain = attngain.astype(wide)
    attn_normed = norm_rows(inputs, attn_gain, attnshift.astype(wide)).astype(narrow)
    queries = (matmul(attn_normed, querymat) + querybias.astype(wide)).astype(narrow)
    keys_own = matmul(attn_normed, keymat).astype(narrow)
    values_own = (matmul(attn_normed, valuemat) + valuebias.astype(wide)).astype(narrow)
    keys_all, values_all = (
        lax.all_gather(keys_own, "expert", axis=0, tiled=True),
        lax.all_gather(values_own, "expert", axis=0, tiled=True),
    )
    seg_all, route_all = (
        lax.all_gather(segments, "expert", axis=1, tiled=True),
        lax.all_gather(routes, "expert", axis=1, tiled=True),
    )
    seg_all = seg_all[0]
    route_all = route_all[0]
    own_seg = segments[0]
    own_route = routes[0]
    length = keys_all.shape[0]
    key_pos = jnp.arange(length)
    query_pos = my_expert * row_count + jnp.arange(row_count)
    allowed = (key_pos[None, :] <= query_pos[:, None]) & (seg_all[None, :] == own_seg[:, None])

    def block_cols(matrix, index):
        sliced = lax.dynamic_slice_in_dim(matrix, index * block_width, block_width, 1)
        return sliced.reshape(matrix.shape[0], block_heads, HEAD_DIM)

    def scores_of(index):
        return (
            jnp.einsum(
                "qhd,khd->hqk",
                block_cols(queries, index),
                block_cols(keys_all, index),
                preferred_element_type=wide,
            )
            * scale
        )

    def forward_block(index):
        scores = scores_of(index)
        masked = jnp.where(allowed[None], scores, -1e30)
        maximum = jnp.max(masked, -1, keepdims=True)
        expo = jnp.where(allowed[None], jnp.exp(masked - maximum), 0.0)
        total = jnp.sum(expo, -1, keepdims=True)
        probs_low = (expo / total).astype(narrow)
        context_blk = jnp.einsum(
            "hqk,khd->qhd", probs_low, block_cols(values_all, index), preferred_element_type=wide
        )
        return (context_blk.reshape(row_count, block_width), maximum + jnp.log(total))

    context_blocks, log_totals = lax.map(forward_block, jnp.arange(head_blocks))
    context = jnp.moveaxis(context_blocks, 0, 1).reshape(row_count, width).astype(narrow)
    hidden = inputs + matmul(context, outmat) + outbias.astype(wide)
    sent = hidden.astype(narrow)
    onehot = (own_route[:, None] == jnp.arange(experts)[None, :]).astype(jnp.int32)
    slot_index = jnp.sum((jnp.cumsum(onehot, 0) - 1) * onehot, 1)
    send_index = own_route * capacity + slot_index
    owned_mask = route_all == my_expert
    rank_list = (
        jnp.cumsum(owned_mask.reshape(experts, row_count).astype(jnp.int32), 1) - 1
    ).reshape(-1)
    chosen = jnp.nonzero(owned_mask, size=row_count)[0]
    recv_index = chosen // row_count * capacity + rank_list[chosen]

    def pack_send(row_data):
        filled = jnp.zeros((experts * capacity, width), row_data.dtype).at[send_index].set(row_data)
        return filled.reshape(experts, capacity, width)

    def pack_recv(row_data):
        filled = jnp.zeros((experts * capacity, width), row_data.dtype).at[recv_index].set(row_data)
        return filled.reshape(experts, capacity, width)

    arrived = lax.all_to_all(pack_send(sent), "expert", split_axis=0, concat_axis=0, tiled=True)
    expert_in = arrived.reshape(experts * capacity, width)[recv_index]
    params = (
        lax.all_gather(frontgain, "dp", axis=1, tiled=True),
        lax.all_gather(frontshift, "dp", axis=1, tiled=True),
        lax.all_gather(frontexpand, "dp", axis=2, tiled=True),
        lax.all_gather(frontlift, "dp", axis=1, tiled=True),
        lax.all_gather(frontreduce, "dp", axis=1, tiled=True),
        lax.all_gather(frontoffset, "dp", axis=1, tiled=True),
        lax.all_gather(backgain, "dp", axis=1, tiled=True),
        lax.all_gather(backshift, "dp", axis=1, tiled=True),
        lax.all_gather(backexpand, "dp", axis=2, tiled=True),
        lax.all_gather(backlift, "dp", axis=1, tiled=True),
        lax.all_gather(backreduce, "dp", axis=1, tiled=True),
        lax.all_gather(backoffset, "dp", axis=1, tiled=True),
        lax.all_gather(centroid, "dp", axis=1, tiled=True),
    )
    front_gain = params[0][0].astype(wide)
    back_gain = params[6][0].astype(wide)
    centre = params[12][0].astype(wide)
    stream_first = expert_in.astype(wide)
    front_normed, front_pre, front_act, front_out = sublayer(
        stream_first,
        front_gain,
        params[1][0].astype(wide),
        params[2][0],
        params[3][0].astype(wide),
        params[4][0],
        params[5][0].astype(wide),
    )
    middle = stream_first + front_out
    back_normed, back_pre, back_act, back_out = sublayer(
        middle,
        back_gain,
        params[7][0].astype(wide),
        params[8][0],
        params[9][0].astype(wide),
        params[10][0],
        params[11][0].astype(wide),
    )
    gate = jax.nn.sigmoid(jnp.sum(stream_first * centre, -1, keepdims=True))
    branches = front_out + back_out
    returned = (gate * branches).astype(narrow)
    came_back = lax.all_to_all(
        pack_recv(returned), "expert", split_axis=0, concat_axis=0, tiled=True
    )
    result = (
        hidden + came_back.reshape(experts * capacity, width)[send_index].astype(wide)
    ).astype(narrow)
    upstream = cotangent.astype(wide)
    ct_arrived = lax.all_to_all(
        pack_send(cotangent), "expert", split_axis=0, concat_axis=0, tiled=True
    )
    ct_rows = ct_arrived.reshape(experts * capacity, width)[recv_index].astype(wide)
    again = (
        lax.all_gather(frontexpand, "dp", axis=2, tiled=True),
        lax.all_gather(frontreduce, "dp", axis=1, tiled=True),
        lax.all_gather(backexpand, "dp", axis=2, tiled=True),
        lax.all_gather(backreduce, "dp", axis=1, tiled=True),
        lax.all_gather(frontgain, "dp", axis=1, tiled=True),
        lax.all_gather(backgain, "dp", axis=1, tiled=True),
        lax.all_gather(centroid, "dp", axis=1, tiled=True),
    )
    front_expand, front_shrink, back_expand, back_shrink = (
        again[0][0],
        again[1][0],
        again[2][0],
        again[3][0],
    )
    front_gain_b, back_gain_b, centre_b = (
        again[4][0].astype(wide),
        again[5][0].astype(wide),
        again[6][0].astype(wide),
    )
    logit_grad = jnp.sum(ct_rows * branches, -1, keepdims=True) * gate * (1.0 - gate)
    centroid_sum = jnp.sum(logit_grad * stream_first, 0)
    middle_grad, back_gain_grad, back_shift_grad, back_pieces = sublayer_back(
        middle,
        back_gain_b,
        back_normed,
        back_pre,
        back_act,
        back_expand,
        back_shrink,
        gate * ct_rows,
    )
    first_grad, front_gain_grad, front_shift_grad, front_pieces = sublayer_back(
        stream_first,
        front_gain_b,
        front_normed,
        front_pre,
        front_act,
        front_expand,
        front_shrink,
        gate * ct_rows + middle_grad,
    )
    sent_grad = (logit_grad * centre_b + middle_grad + first_grad).astype(narrow)
    grad_back = lax.all_to_all(
        pack_recv(sent_grad), "expert", split_axis=0, concat_axis=0, tiled=True
    )
    hidden_grad = upstream + grad_back.reshape(experts * capacity, width)[send_index].astype(wide)

    def full_terms(pieces):
        normed_rows, hidden_low, active, branch_low = pieces
        return (
            matmul_left(normed_rows, hidden_low)[None],
            jnp.sum(hidden_low.astype(wide), 0)[None],
            matmul_left(active, branch_low)[None],
            jnp.sum(branch_low.astype(wide), 0)[None],
        )

    fterms = full_terms(front_pieces)
    bterms = full_terms(back_pieces)
    summed = (
        lax.psum_scatter(
            front_gain_grad[None].astype(jnp.bfloat16), "dp", scatter_dimension=1, tiled=True
        ).astype(jnp.float32),
        lax.psum_scatter(
            front_shift_grad[None].astype(jnp.bfloat16), "dp", scatter_dimension=1, tiled=True
        ).astype(jnp.float32),
        lax.psum_scatter(
            fterms[0].astype(jnp.bfloat16), "dp", scatter_dimension=2, tiled=True
        ).astype(jnp.float32),
        lax.psum_scatter(
            fterms[1].astype(jnp.bfloat16), "dp", scatter_dimension=1, tiled=True
        ).astype(jnp.float32),
        lax.psum_scatter(
            fterms[2].astype(jnp.bfloat16), "dp", scatter_dimension=1, tiled=True
        ).astype(jnp.float32),
        lax.psum_scatter(
            fterms[3].astype(jnp.bfloat16), "dp", scatter_dimension=1, tiled=True
        ).astype(jnp.float32),
        lax.psum_scatter(
            back_gain_grad[None].astype(jnp.bfloat16), "dp", scatter_dimension=1, tiled=True
        ).astype(jnp.float32),
        lax.psum_scatter(
            back_shift_grad[None].astype(jnp.bfloat16), "dp", scatter_dimension=1, tiled=True
        ).astype(jnp.float32),
        lax.psum_scatter(
            bterms[0].astype(jnp.bfloat16), "dp", scatter_dimension=2, tiled=True
        ).astype(jnp.float32),
        lax.psum_scatter(
            bterms[1].astype(jnp.bfloat16), "dp", scatter_dimension=1, tiled=True
        ).astype(jnp.float32),
        lax.psum_scatter(
            bterms[2].astype(jnp.bfloat16), "dp", scatter_dimension=1, tiled=True
        ).astype(jnp.float32),
        lax.psum_scatter(
            bterms[3].astype(jnp.bfloat16), "dp", scatter_dimension=1, tiled=True
        ).astype(jnp.float32),
        lax.psum_scatter(
            centroid_sum[None].astype(jnp.bfloat16), "dp", scatter_dimension=1, tiled=True
        ).astype(jnp.float32),
    )
    out_low = hidden_grad.astype(narrow)
    outmat_grad = matmul_left(context, out_low)
    outbias_grad = jnp.sum(out_low.astype(wide), 0)
    context_grad = matmul_right(out_low, outmat).astype(narrow)

    def backward_block(couple):
        index, log_total = couple
        scores = scores_of(index)
        probs = jnp.where(allowed[None], jnp.exp(scores - log_total), 0.0)
        grad_blk = block_cols(context_grad, index)
        prob_grad = jnp.einsum(
            "qhd,khd->hqk", grad_blk, block_cols(values_all, index), preferred_element_type=wide
        )
        value_part = jnp.einsum(
            "hqk,qhd->khd", probs.astype(narrow), grad_blk, preferred_element_type=wide
        )
        row_inner = jnp.sum(probs * prob_grad, -1, keepdims=True)
        score_low = (probs * (prob_grad - row_inner)).astype(narrow)
        query_part = (
            jnp.einsum(
                "hqk,khd->qhd", score_low, block_cols(keys_all, index), preferred_element_type=wide
            )
            * scale
        )
        key_part = (
            jnp.einsum(
                "hqk,qhd->khd", score_low, block_cols(queries, index), preferred_element_type=wide
            )
            * scale
        )
        return (
            query_part.reshape(row_count, block_width),
            key_part.reshape(length, block_width),
            value_part.reshape(length, block_width),
        )

    query_parts, key_parts, value_parts = lax.map(
        backward_block, (jnp.arange(head_blocks), log_totals)
    )
    query_low = jnp.moveaxis(query_parts, 0, 1).reshape(row_count, width).astype(narrow)
    key_all_grad = jnp.moveaxis(key_parts, 0, 1).reshape(length, width)
    value_all_grad = jnp.moveaxis(value_parts, 0, 1).reshape(length, width)
    key_sum, value_sum = (
        lax.psum_scatter(
            key_all_grad.astype(jnp.bfloat16), "expert", scatter_dimension=0, tiled=True
        ).astype(jnp.float32),
        lax.psum_scatter(
            value_all_grad.astype(jnp.bfloat16), "expert", scatter_dimension=0, tiled=True
        ).astype(jnp.float32),
    )
    key_low = key_sum.astype(narrow)
    value_low = value_sum.astype(narrow)
    querymat_grad = matmul_left(attn_normed, query_low)
    querybias_grad = jnp.sum(query_low.astype(wide), 0)
    keymat_grad = matmul_left(attn_normed, key_low)
    valuemat_grad = matmul_left(attn_normed, value_low)
    valuebias_grad = jnp.sum(value_low.astype(wide), 0)
    attn_norm_grad = (
        matmul_right(query_low, querymat)
        + matmul_right(key_low, keymat)
        + matmul_right(value_low, valuemat)
    )
    _, attn_pull = jax.vjp(norm_rows, inputs, attn_gain, jnp.zeros_like(attn_gain))
    input_part, attngain_grad, attnshift_grad = attn_pull(attn_norm_grad)
    tokens_grad = hidden_grad + input_part
    dense = lax.psum(
        (
            attngain_grad,
            attnshift_grad,
            querymat_grad,
            querybias_grad,
            keymat_grad,
            valuemat_grad,
            valuebias_grad,
            outmat_grad,
            outbias_grad,
        ),
        ("dp", "expert"),
    )
    return (
        result,
        tokens_grad,
        dense[0],
        dense[1],
        dense[2],
        dense[3],
        dense[4],
        dense[5],
        dense[6],
        dense[7],
        dense[8],
        summed[0],
        summed[1],
        summed[2],
        summed[3],
        summed[4],
        summed[5],
        summed[6],
        summed[7],
        summed[8],
        summed[9],
        summed[10],
        summed[11],
        summed[12],
    )


def solution(mesh):
    placed = (
        P(("dp", "expert"), None),
        P(("dp", "expert"), None),
        P("dp", "expert"),
        P("dp", "expert"),
        P(),
        P(),
        P(),
        P(),
        P(),
        P(),
        P(),
        P(),
        P(),
        P("expert", "dp"),
        P("expert", "dp"),
        P("expert", None, "dp"),
        P("expert", "dp"),
        P("expert", "dp", None),
        P("expert", "dp"),
        P("expert", "dp"),
        P("expert", "dp"),
        P("expert", None, "dp"),
        P("expert", "dp"),
        P("expert", "dp", None),
        P("expert", "dp"),
        P("expert", "dp"),
    )
    return jax.shard_map(
        per_device,
        mesh=mesh,
        in_specs=placed,
        out_specs=(
            P(("dp", "expert"), None),
            P(("dp", "expert"), None),
            P(),
            P(),
            P(),
            P(),
            P(),
            P(),
            P(),
            P(),
            P(),
            P("expert", "dp"),
            P("expert", "dp"),
            P("expert", None, "dp"),
            P("expert", "dp"),
            P("expert", "dp", None),
            P("expert", "dp"),
            P("expert", "dp"),
            P("expert", "dp"),
            P("expert", None, "dp"),
            P("expert", "dp"),
            P("expert", "dp", None),
            P("expert", "dp"),
            P("expert", "dp"),
        ),
        check_vma=False,
    )
```

profile of v0, /device:TPU:1, one launch (start us, length us, event | category | flops | bytes accessed | tf_op | source)
XLA Modules:
  0.0 1930.5 jit_solution(8231682968662279679)
XLA Ops:
  31.4 24.1 %all_gather.61 = s32[1,2048]{1,0:T(1,128)S(1)} all-gather(s32[1,256]{1,0:T(1,128)S(1)} %copy-done.57), channel_id=1, replica_groups=mesh['dp'=16,'expert'=8] {'expert'}, dimensions={1}, use_global_device_ids=true | all-gather | bytes 9216 | tf_op jit(solution)/shard_map/all_gather | solution.py:109
  101.3 52.0 %while.28 = (s32[]{:T(128)}, bf16[4,256,256]{1,2,0:T(8,128)(2,1)}, f32[4,4,256,1]{2,1,3,0:T(4,128)}, s32[4]{0:T(128)S(1)}, bf16[2048,1024]{0,1:T(8,128)(2,1)}, /...) while((s32[]{:T(128)}, bf16[4,256,256]{1,2,0:T(8,128)(2,1)}, ...), condition=%wide.region_5.6_spmd.clone, body=%wide.region_2.5_spmd.clone.sunk | while | flops 567802880 | bytes 34384088 | solution.py:147
  167.5 61.5 %all-reduce.9 = (bf16[1024]{0:T(1024)(128)(2,1)S(1)}, bf16[1024]{0:T(1024)(128)(2,1)S(1)}, bf16[1024]{0:T(1024)(128)(2,1)S(1)}, bf16[1024]{0:T(1024)(128)(2,1)S(...) all-reduce(bf16[1024]{0:T(1024)(128)(2,1)S(1)} %dynamic-update-slic, ...), channel_id=1, replica_groups=mesh['dp'=16,'expert'=8] {'dp'}, use_global_device_ids=true, to_apply=%add.2 | all-reduce | flops 7168 | bytes 28672
  229.0 16.8 all_gather.66
  245.9 18.9 all_gather.72
  297.4 27.6 %all-gather.15.cloned.1.call-done = bf16[1,1024,4096]{2,1,0:T(8,128)(2,1)} async-done(((bf16[1,1024,256]{2,1,0:T(8,128)(2,1)}), bf16[1,1024,4096]{2,1,0:T(8,128)(2,1)}) %all-gather.15.cloned.1.call-update) | async-done | bytes 8388624 | tf_op jit(solution)/shard_map/all_gather | solution.py:180
  325.0 16.5 multiply_convert_fusion.1
  341.5 56.5 %all-gather.17.cloned.1.call-done = bf16[1,4096,1024]{2,1,0:T(8,128)(2,1)} async-done(((bf16[1,256,1024]{2,1,0:T(8,128)(2,1)}), bf16[1,4096,1024]{2,1,0:T(8,128)(2,1)}) %all-gather.17.cloned.1.call-update) | async-done | bytes 8388624 | tf_op jit(solution)/shard_map/all_gather | solution.py:182
  467.6 112.3 %while.29 = (s32[]{:T(128)}, bf16[4,256,256]{1,2,0:T(8,128)(2,1)}, bf16[4,2048,256]{1,2,0:T(8,128)(2,1)}, bf16[4,2048,256]{1,2,0:T(8,128)(2,1)}, s32[4]{0:T(128)...) while((s32[]{:T(128)}, bf16[4,256,256]{1,2,0:T(8,128)(2,1)}, ...), condition=%wide.region_33.34_spmd.clone, body=%wide.region_31.33_spmd.clone.sunk | while | flops 1376386048 | bytes 107666040 | solution.py:359
  634.8 18.5 reduce-scatter.36.cloned.1.call-done
  667.8 60.7 %reduce-scatter.46.cloned.1.call-done = bf16[64,1]{1,0:T(8,128)(2,1)} async-done(((bf16[1024,1]{1,0:T(8,128)(2,1)}), bf16[64,1]{1,0:T(8,128)(2,1)}) %reduce-scatter.46.cloned.1.call-update) | async-done | bytes 144
  729.9 73.3 %reduce-scatter.48.cloned.1.call-done = bf16[64,1]{1,0:T(8,128)(2,1)} async-done(((bf16[1024,1]{1,0:T(8,128)(2,1)}), bf16[64,1]{1,0:T(8,128)(2,1)}) %reduce-scatter.48.cloned.1.call-update) | async-done | bytes 144
  804.5 73.2 %reduce-scatter.52.cloned.1.call-done = bf16[64,1]{1,0:T(8,128)(2,1)} async-done(((bf16[1024,1]{1,0:T(8,128)(2,1)}), bf16[64,1]{1,0:T(8,128)(2,1)}) %reduce-scatter.52.cloned.1.call-update) | async-done | bytes 144
  879.0 73.3 %reduce-scatter.54.cloned.1.call-done = bf16[64,1]{1,0:T(8,128)(2,1)} async-done(((bf16[1024,1]{1,0:T(8,128)(2,1)}), bf16[64,1]{1,0:T(8,128)(2,1)}) %reduce-scatter.54.cloned.1.call-update) | async-done | bytes 144
  953.6 73.2 %reduce-scatter.56.cloned.1.call-done = bf16[64,1]{1,0:T(8,128)(2,1)} async-done(((bf16[1024,1]{1,0:T(8,128)(2,1)}), bf16[64,1]{1,0:T(8,128)(2,1)}) %reduce-scatter.56.cloned.1.call-update) | async-done | bytes 144
  1028.2 73.3 %reduce-scatter.60.cloned.1.call-done = bf16[64,1]{1,0:T(8,128)(2,1)} async-done(((bf16[1024,1]{1,0:T(8,128)(2,1)}), bf16[64,1]{1,0:T(8,128)(2,1)}) %reduce-scatter.60.cloned.1.call-update) | async-done | bytes 144
  1102.8 73.0 %reduce-scatter.62.cloned.1.call-done = bf16[64,1]{1,0:T(8,128)(2,1)} async-done(((bf16[1024,1]{1,0:T(8,128)(2,1)}), bf16[64,1]{1,0:T(8,128)(2,1)}) %reduce-scatter.62.cloned.1.call-update) | async-done | bytes 144
  1177.1 74.9 %reduce-scatter.50.cloned.1.call-done = bf16[256,1]{1,0:T(8,128)(2,1)} async-done(((bf16[4096,1]{1,0:T(8,128)(2,1)}), bf16[256,1]{1,0:T(8,128)(2,1)}) %reduce-scatter.50.cloned.1.call-update) | async-done | bytes 528
  1253.5 74.3 %reduce-scatter.58.cloned.1.call-done = bf16[256,1]{1,0:T(8,128)(2,1)} async-done(((bf16[4096,1]{1,0:T(8,128)(2,1)}), bf16[256,1]{1,0:T(8,128)(2,1)}) %reduce-scatter.58.cloned.1.call-update) | async-done | bytes 528
  1341.7 67.4 %all-reduce.7 = (f32[1024]{0:T(1024)}, f32[1024]{0:T(1024)}, f32[1024]{0:T(1024)}, f32[1024]{0:T(1024)}, f32[1024]{0:T(1024)}) all-reduce(f32[1024]{0:T(1024)S(1)} %get-tuple-element.260, f32[1024]{0:T(1024)S(1)} %get-tuple-element.265, f32[1024]{0:T(1024)S(1)} %bitcast.298, ...), channel_id=1, replica_groups=mesh['dp'=16,'expert'=8] {'dp','expert'}, use_global_device_ids=true, to_apply=%region_39.40 | all-reduce | flops 5120 | bytes 40960 | tf_op jit(solution)/shard_map/psum | solution.py:388
  1419.2 85.7 %reduce-scatter.40.cloned.1.call-done = bf16[1,256,1024]{2,1,0:T(8,128)(2,1)} async-done(((bf16[1,4096,1024]{2,1,0:T(8,128)(2,1)}), bf16[1,256,1024]{2,1,0:T(8,128)(2,1)}) %reduce-scatter.40.cloned.1.call-update) | async-done | bytes 524304 | tf_op jit(solution)/shard_map/reduce_scatter | solution.py:295
  1507.1 86.1 %reduce-scatter.42.cloned.1.call-done = bf16[1,1024,256]{2,1,0:T(8,128)(2,1)} async-done(((bf16[1,1024,4096]{2,1,0:T(8,128)(2,1)}), bf16[1,1024,256]{2,1,0:T(8,128)(2,1)}) %reduce-scatter.42.cloned.1.call-update) | async-done | bytes 524304 | tf_op jit(solution)/shard_map/reduce_scatter | solution.py:307
  1595.2 86.1 %reduce-scatter.44.cloned.1.call-done = bf16[1,256,1024]{2,1,0:T(8,128)(2,1)} async-done(((bf16[1,4096,1024]{2,1,0:T(8,128)(2,1)}), bf16[1,256,1024]{2,1,0:T(8,128)(2,1)}) %reduce-scatter.44.cloned.1.call-update) | async-done | bytes 524304 | tf_op jit(solution)/shard_map/reduce_scatter | solution.py:313
  1683.5 225.4 %all-reduce.12.cloned.1.call-done = (f32[1024,1024]{1,0:T(8,128)}, f32[1024,1024]{1,0:T(8,128)}, f32[1024,1024]{1,0:T(8,128)}, f32[1024,1024]{1,0:T(8,128)}) async-done(((f32[1024,1024]{1,0:T(8,128)}, f32[1024,1024]{1,0:T(8,128)}, f32[1024,1024]{1,0:T(8,128)}, f32[1024,1024]{1,0:T(8,128)}), (f32[1024,1024]{1,0:T(8,128)}, f32[1024,1024]{1,0:T(8,128)}, f32[1024,1024]{1,0:T(8,128)}, ...) | async-done | bytes 16777232 | tf_op jit(solution)/shard_map/psum | solution.py:388
  (572 shorter events, 467.8 us)
Async XLA Ops:
  7.2 80.4 %all-gather.7.cloned.1.call-start = ((), (), s32[]{:S(2)}) async-start(), calls=%async_computation.19 | async-start | bytes 4718592 | tf_op jit(solution)/shard_map/all_gather | solution.py:105
  14.7 79.4 %all-gather.9.cloned.1.call-start = ((), (), s32[]{:S(2)}) async-start(), calls=%async_computation.20 | async-start | bytes 4718592 | tf_op jit(solution)/shard_map/all_gather | solution.py:104
  17.9 254.8 %all-gather.11.cloned.1.call-start = ((), (), s32[]{:S(2)}) async-start(), calls=%async_computation.21 | async-start | bytes 8912896 | tf_op jit(solution)/shard_map/all_gather | solution.py:174
  18.7 270.2 %all-gather.13.cloned.1.call-start = ((), (), s32[]{:S(2)}) async-start(), calls=%async_computation.22 | async-start | bytes 8912896 | tf_op jit(solution)/shard_map/all_gather | solution.py:176
  19.2 305.7 %all-gather.15.cloned.1.call-start = ((), (), s32[]{:S(2)}) async-start(), calls=%async_computation.23 | async-start | bytes 8912896 | tf_op jit(solution)/shard_map/all_gather | solution.py:180
  23.9 136.3 %all-to-all-start.2 = ((bf16[8,48,1024]{2,1,0:T(8,128)(2,1)}), bf16[8,48,1024]{2,1,0:T(8,128)(2,1)S(1)}, u32[]{:S(2)}, u32[]{:S(2)}) async-start(bf16[8,48,1024]{2,1,0:T(8,128)(2,1)} %bitcast.286), calls=%async_computation.2 | async-start | bytes 1572864 | tf_op jit(solution)/shard_map/all_to_all | solution.py:219
  30.9 367.1 %all-gather.17.cloned.1.call-start = ((), (), s32[]{:S(2)}) async-start(), calls=%async_computation.24 | async-start | bytes 8912896 | tf_op jit(solution)/shard_map/all_gather | solution.py:182
  160.3 109.1 %all-to-all-start = ((bf16[8,48,1024]{2,1,0:T(8,128)(2,1)}), bf16[8,48,1024]{2,1,0:T(8,128)(2,1)}, u32[]{:S(2)}, u32[]{:S(2)}) async-start(bf16[8,48,1024]{2,1,0:T(8,128)(2,1)} %bitcast.287), calls=%async_computation | async-start | bytes 1572864 | tf_op jit(solution)/shard_map/all_to_all | solution.py:169
  449.8 181.1 %reduce-scatter.34.cloned.1.call-start = ((), (), s32[]{:S(2)}) async-start(), calls=%async_computation.25 | async-start | bytes 4718592 | tf_op jit(solution)/shard_map/reduce_scatter | solution.py:366
  580.9 147.7 %reduce-scatter.46.cloned.1.call-start = ((), (), s32[]{:S(2)}) async-start(), calls=%async_computation.31 | async-start | bytes 278528
  581.9 221.3 %reduce-scatter.48.cloned.1.call-start = ((), (), s32[]{:S(2)}) async-start(), calls=%async_computation.32 | async-start | bytes 278528
  582.8 294.8 %reduce-scatter.52.cloned.1.call-start = ((), (), s32[]{:S(2)}) async-start(), calls=%async_computation.34 | async-start | bytes 278528
  583.8 368.5 %reduce-scatter.54.cloned.1.call-start = ((), (), s32[]{:S(2)}) async-start(), calls=%async_computation.35 | async-start | bytes 278528
  584.8 442.0 %reduce-scatter.56.cloned.1.call-start = ((), (), s32[]{:S(2)}) async-start(), calls=%async_computation.36 | async-start | bytes 278528
  585.8 515.7 %reduce-scatter.60.cloned.1.call-start = ((), (), s32[]{:S(2)}) async-start(), calls=%async_computation.38 | async-start | bytes 278528
  586.8 589.0 %reduce-scatter.62.cloned.1.call-start = ((), (), s32[]{:S(2)}) async-start(), calls=%async_computation.39 | async-start | bytes 278528
  587.8 664.2 %reduce-scatter.50.cloned.1.call-start = ((), (), s32[]{:S(2)}) async-start(), calls=%async_computation.33 | async-start | bytes 1114112
  589.5 738.3 %reduce-scatter.58.cloned.1.call-start = ((), (), s32[]{:S(2)}) async-start(), calls=%async_computation.37 | async-start | bytes 1114112
  591.1 826.0 %reduce-scatter.38.cloned.1.call-start = ((), (), s32[]{:S(2)}) async-start(), calls=%async_computation.27 | async-start | bytes 8912896 | tf_op jit(solution)/shard_map/reduce_scatter | solution.py:289
  598.8 906.1 %reduce-scatter.40.cloned.1.call-start = ((), (), s32[]{:S(2)}) async-start(), calls=%async_computation.28 | async-start | bytes 8912896 | tf_op jit(solution)/shard_map/reduce_scatter | solution.py:295
  607.1 986.0 %reduce-scatter.42.cloned.1.call-start = ((), (), s32[]{:S(2)}) async-start(), calls=%async_computation.29 | async-start | bytes 8912896 | tf_op jit(solution)/shard_map/reduce_scatter | solution.py:307
  615.7 1065.7 %reduce-scatter.44.cloned.1.call-start = ((), (), s32[]{:S(2)}) async-start(), calls=%async_computation.30 | async-start | bytes 8912896 | tf_op jit(solution)/shard_map/reduce_scatter | solution.py:313
  624.0 1284.9 %all-reduce.12.cloned.1.call-start = ((), (), s32[]{:S(2)}) async-start(), calls=%async_computation.40 | async-start | bytes 33554432 | tf_op jit(solution)/shard_map/psum | solution.py:388
  660.6 668.6 %all-to-all-start.1 = ((bf16[8,48,1024]{2,1,0:T(8,128)(2,1)}), bf16[8,48,1024]{2,1,0:T(8,128)(2,1)S(1)}, u32[]{:S(2)}, u32[]{:S(2)}) async-start(bf16[8,48,1024]{2,1,0:T(8,128)(2,1)} %bitcast.288), calls=%async_computation.1 | async-start | bytes 1572864 | tf_op jit(solution)/shard_map/all_to_all | solution.py:212
  (122 other events, 2431.7 us)
Sparse Core Ops, SparseCore 0:
  14.8 44.4 all-gather.6
  61.6 32.2 all-gather.8
  95.9 76.6 all-gather.10
  174.6 71.5 all-gather.12
  248.1 76.8 all-gather.14
  327.0 70.8 all-gather.16
  580.1 33.1 reduce-scatter.33
  616.3 37.0 reduce-scatter.35
  656.5 71.9 reduce-scatter.45
  731.9 71.2 reduce-scatter.47
  806.3 71.2 reduce-scatter.51
  881.0 71.2 reduce-scatter.53
  955.5 71.3 reduce-scatter.55
  1030.2 71.2 reduce-scatter.59
  1104.5 71.2 reduce-scatter.61
  1179.8 72.1 reduce-scatter.49
  1255.6 72.0 reduce-scatter.57
  1331.4 85.6 reduce-scatter.37
  1420.9 83.9 reduce-scatter.39
  1508.6 84.5 reduce-scatter.41
  1596.9 84.3 reduce-scatter.43
  1690.0 218.8 all-reduce.11
where the time goes:
time: 1940 us; the launch traced here: 1930 us
  waiting for transfers between devices  1260 us (65%)
  matrix products  222 us (11%)
  blocking collectives  198 us (10%)
  local copies, waits for them, and re-layouts  118 us (6%)
  other arithmetic  86.7 us (4%)
  starting transfers between devices  25 us (1%)
    unnamed x31, waiting for transfers between devices  652 us
    psum x1, waiting for transfers between devices, per_device(): lax.psum((attngain_grad, attnshift_grad, querymat_grad, querybias_grad, k...  225 us
    reduce_scatter x1, waiting for transfers between devices, per_device(): lax.psum_scatter(bterms[2].astype(jnp.bfloat16), 'dp', scatter_dimension=...  86.1 us
    reduce_scatter x1, waiting for transfers between devices, per_device(): lax.psum_scatter(bterms[0].astype(jnp.bfloat16), 'dp', scatter_dimension=...  86.1 us
    reduce_scatter x1, waiting for transfers between devices, per_device(): lax.psum_scatter(fterms[2].astype(jnp.bfloat16), 'dp', scatter_dimension=...  85.7 us
    psum x1, blocking collectives, per_device(): lax.psum((attngain_grad, attnshift_grad, querymat_grad, querybias_grad, k...  67.4 us
    unnamed x1, blocking collectives  61.5 us
    dot_general x8, matrix products, matmul(): return jnp.dot(left, right, preferred_element_type=jnp.float32)  60.1 us
  transfers between devices with their start and end apart: 26, of which 18 were waited for; matrix products, arithmetic and copies ran while one was open for 12% of the time, Pallas kernels for 0%

commit v1 on v0

v1 whole, which is shorter than its diff:
```python
import jax
import jax.numpy as jnp
from jax import lax
from jax.experimental import pallas as pl
from jax.experimental.pallas import tpu as pltpu
from jax.sharding import Mesh, PartitionSpec as P

HEADS = 16
HEAD_DIM = 64
EPSILON = 1e-05
MASKED = -1e30

GROUP = ("z", "c")
DATA = ("x", "y")
EVERY = ("x", "y", "z", "c")

wide = jnp.float32
narrow = jnp.bfloat16


def matmul(left, right):
    return jnp.dot(left, right, preferred_element_type=wide)


def matmul_left(left, right):
    return lax.dot_general(left, right, (((0,), (0,)), ((), ())), preferred_element_type=wide)


def matmul_right(left, right):
    return lax.dot_general(left, right, (((1,), (1,)), ((), ())), preferred_element_type=wide)


def norm_parts(stream):
    center = stream - jnp.mean(stream, -1, keepdims=True)
    inverse = lax.rsqrt(jnp.mean(center * center, -1, keepdims=True) + EPSILON)
    return center * inverse, inverse


def norm_back(scaled, xhat, inverse):
    return (
        scaled
        - jnp.mean(scaled, -1, keepdims=True)
        - xhat * jnp.mean(scaled * xhat, -1, keepdims=True)
    ) * inverse


def gelu_pair(value):
    cdf = 0.5 + 0.5 * lax.erf(value * (0.5**0.5))
    pdf = jnp.exp(-0.5 * value * value) * 0.3989422804014327
    return value * cdf, cdf + value * pdf


def shift_by(value, axis, step):
    return lax.ppermute(value, axis, [(i, (i + step) % 4) for i in range(4)])


def share_rows(rows, axis):
    return jnp.concatenate(
        [rows, shift_by(rows, axis, 1), shift_by(rows, axis, 3), shift_by(rows, axis, 2)], 0
    )


def sum_rows(partial, axis):
    own, back, ahead, away = jnp.split(partial.astype(narrow), 4, 0)
    got = (shift_by(back, axis, 3), shift_by(ahead, axis, 1), shift_by(away, axis, 2))
    return own.astype(wide) + sum(part.astype(wide) for part in got)


def exchange(blocks, axes):
    return lax.all_to_all(blocks, axes, 0, 0, tiled=True)


def to_everyone(block, axes, count):
    return exchange(jnp.broadcast_to(block[None], (count,) + block.shape), axes)


def head_rows(matrix, head):
    rows = lax.broadcasted_iota(jnp.int32, matrix.shape, 0) // HEAD_DIM
    return jnp.where(rows == head, matrix, jnp.zeros_like(matrix))


def head_lanes(matrix, head):
    lanes = lax.broadcasted_iota(jnp.int32, matrix.shape, 1) // HEAD_DIM
    return jnp.where(lanes == head, matrix, jnp.zeros_like(matrix))


def turn(matrix):
    return jnp.transpose(matrix.astype(wide), (1, 0)).astype(matrix.dtype)


def mask_of(segcol_ref, segrow_ref, i, j, diagonal):
    same = segcol_ref[j] == segrow_ref[i]
    if diagonal:
        size = same.shape
        same = same & (
            lax.broadcasted_iota(jnp.int32, size, 0) <= lax.broadcasted_iota(jnp.int32, size, 1)
        )
    return same


def attend_kernel(low_ref, qkv_ref, segcol_ref, segrow_ref, ctx_ref, full_ref, lse_ref, vals_ref):
    blocks, size, _ = qkv_ref.shape
    for j in range(blocks):
        turned = turn(qkv_ref[j, :, 256:384])
        for head in range(2):
            vals_ref[j, head, 0:64, :] = turned[head * 64 : head * 64 + 64]
            vals_ref[j, head, 64:80, :] = jnp.ones((16, size), narrow)
    for i in range(blocks):
        query = turn((qkv_ref[i, :, 0:128].astype(wide) * HEAD_DIM**-0.5).astype(narrow))
        queries = [head_rows(query, head) for head in range(2)]

        def step(j, carry, diagonal):
            keys = qkv_ref[j, :, 128:256]
            mask = mask_of(segcol_ref, segrow_ref, i, j, diagonal)
            out = []
            for head in range(2):
                scores = jnp.where(mask, matmul(keys, queries[head]), MASKED)
                top = jnp.max(scores, 0, keepdims=True)
                if carry is not None:
                    top = jnp.maximum(top, carry[2 * head])
                probs = jnp.exp(scores - top).astype(narrow)
                total = matmul(vals_ref[j, head], probs)
                if carry is not None:
                    total = total + carry[2 * head + 1] * jnp.exp(carry[2 * head] - top)
                out += [top, total]
            return tuple(out)

        carry = step(i, None, True)
        if i > 0:
            carry = lax.fori_loop(low_ref[i], i, lambda j, c: step(j, c, False), carry)
        parts = []
        for head in range(2):
            top, total = carry[2 * head], carry[2 * head + 1]
            parts.append(total[0:64] / total[64:65])
            lse_ref[i, head : head + 1, :] = top + jnp.log(total[64:65])
        full = jnp.concatenate(parts, 0)
        full_ref[i] = full
        ctx_ref[i] = jnp.transpose(full, (1, 0)).astype(narrow)


def attend(low, qkv, segcol, segrow):
    blocks, size, _ = qkv.shape
    vmem = pl.BlockSpec(memory_space=pltpu.VMEM)
    return pl.pallas_call(
        attend_kernel,
        out_shape=(
            jax.ShapeDtypeStruct((blocks, size, 128), narrow),
            jax.ShapeDtypeStruct((blocks, 128, size), wide),
            jax.ShapeDtypeStruct((blocks, 8, size), wide),
        ),
        in_specs=[pl.BlockSpec(memory_space=pltpu.SMEM), vmem, vmem, vmem],
        out_specs=(vmem, vmem, vmem),
        scratch_shapes=[pltpu.VMEM((blocks, 2, 80, size), narrow)],
        compiler_params=pltpu.CompilerParams(vmem_limit_bytes=40 << 20),
        name="attend",
    )(low, qkv, segcol, segrow)


def attend_back_kernel(
    low_ref, qkv_ref, grad_ref, full_ref, lse_ref, segcol_ref, segrow_ref,
    out_ref, keys_ref, dk_ref, dv_ref,
):
    blocks, size, _ = qkv_ref.shape
    for j in range(blocks):
        keys_ref[j] = turn(qkv_ref[j, :, 128:256])
    dk_ref[...] = jnp.zeros_like(dk_ref)
    dv_ref[...] = jnp.zeros_like(dv_ref)
    for i in range(blocks):
        query = (qkv_ref[i, :, 0:128].astype(wide) * HEAD_DIM**-0.5).astype(narrow)
        query_t = turn(query)
        grad = grad_ref[i]
        grad_t = turn(grad)
        inner = grad_t.astype(wide) * full_ref[i]
        queries_t = [head_rows(query_t, head) for head in range(2)]
        grads_t = [head_rows(grad_t, head) for head in range(2)]
        inners = [
            jnp.sum(inner[head * 64 : head * 64 + 64], 0, keepdims=True) for head in range(2)
        ]
        lses = [lse_ref[i, head : head + 1, :] for head in range(2)]
        query_pair = jnp.concatenate([head_lanes(query, head) for head in range(2)], 0)
        grad_pair = jnp.concatenate([head_lanes(grad, head) for head in range(2)], 0)

        def step(j, carry, diagonal):
            keys = qkv_ref[j, :, 128:256]
            vals = qkv_ref[j, :, 256:384]
            mask = mask_of(segcol_ref, segrow_ref, i, j, diagonal)
            lows, score_lows, out = [], [], []
            for head in range(2):
                scores = matmul(keys, queries_t[head])
                probs = jnp.where(mask, jnp.exp(scores - lses[head]), 0.0)
                prob_grad = matmul(vals, grads_t[head])
                score_low = (probs * (prob_grad - inners[head])).astype(narrow)
                lows.append(probs.astype(narrow))
                score_lows.append(score_low)
                part = matmul(keys_ref[j, head * 64 : head * 64 + 64, :], score_low)
                out.append(part if carry is None else carry[head] + part)
            dv_ref[j] += matmul(jnp.concatenate(lows, 1), grad_pair)
            dk_ref[j] += matmul(jnp.concatenate(score_lows, 1), query_pair)
            return tuple(out)

        carry = step(i, None, True)
        if i > 0:
            carry = lax.fori_loop(low_ref[i], i, lambda j, c: step(j, c, False), carry)
        dq = jnp.concatenate(carry, 0) * HEAD_DIM**-0.5
        out_ref[i, :, 0:128] = jnp.transpose(dq, (1, 0)).astype(narrow)
    for j in range(blocks):
        out_ref[j, :, 128:256] = dk_ref[j].astype(narrow)
        out_ref[j, :, 256:384] = dv_ref[j].astype(narrow)


def attend_back(low, qkv, grad, full, lse, segcol, segrow):
    blocks, size, _ = qkv.shape
    vmem = pl.BlockSpec(memory_space=pltpu.VMEM)
    return pl.pallas_call(
        attend_back_kernel,
        out_shape=jax.ShapeDtypeStruct((blocks, size, 384), narrow),
        in_specs=[pl.BlockSpec(memory_space=pltpu.SMEM)] + [vmem] * 6,
        out_specs=vmem,
        scratch_shapes=[
            pltpu.VMEM((blocks, 128, size), narrow),
            pltpu.VMEM((blocks, size, 128), wide),
            pltpu.VMEM((blocks, size, 128), wide),
        ],
        compiler_params=pltpu.CompilerParams(vmem_limit_bytes=40 << 20),
        name="attend_back",
    )(low, qkv, grad, full, lse, segcol, segrow)


def per_device(
    tokens, cotangent, segments, routes,
    attngain, attnshift, querymat, querybias, keymat, valuemat, valuebias, outmat, outbias,
    frontgain, frontshift, frontexpand, frontlift, frontreduce, frontoffset,
    backgain, backshift, backexpand, backlift, backreduce, backoffset, centroid,
):
    rows, width = tokens.shape
    experts = 8
    capacity = rows // experts + rows // (2 * experts)
    slots = experts * capacity
    mine = lax.axis_index(GROUP)
    x_at, y_at = lax.axis_index("x"), lax.axis_index("y")

    plans = to_everyone(jnp.concatenate([segments, routes], 0), GROUP, experts)
    seg_all, route_all = plans[:, 0], plans[:, 1]
    small_own = jnp.concatenate(
        [
            frontgain[0], frontshift[0], frontoffset[0], backgain[0], backshift[0], backoffset[0],
            centroid[0], frontlift[0], backlift[0], jnp.zeros((64,), narrow),
        ]
    )
    small = to_everyone(small_own.reshape(8, 128), DATA, 16).reshape(16, 1024).astype(wide)
    front_gain, front_shift, front_offset, back_gain, back_shift, back_offset, centre = (
        small[:, i * 64 : i * 64 + 64].reshape(1, width) for i in range(7)
    )
    lifts = small[:, 448:960].reshape(4, 4, 512)
    front_lift = lax.dynamic_index_in_dim(lifts, y_at, 1, False)[:, :256].reshape(1, 1024)
    back_lift = lax.dynamic_index_in_dim(lifts, x_at, 0, False)[:, 256:].reshape(1, 1024)

    front_expand = lax.all_gather(frontexpand[0], "x", axis=0)
    front_shrink = lax.all_gather(frontreduce[0], "x", axis=0, tiled=True)
    back_expand = lax.all_gather(backexpand[0], "y", axis=0)
    back_shrink = lax.all_gather(backreduce[0], "y", axis=0, tiled=True)
    front_expand = jnp.transpose(front_expand, (1, 0, 2)).reshape(width, 1024)
    back_expand = jnp.transpose(back_expand, (1, 0, 2)).reshape(width, 1024)

    route = routes[0]
    picks = (route[:, None] == jnp.arange(experts)[None, :]).astype(narrow)
    lower = (jnp.arange(rows)[:, None] > jnp.arange(rows)[None, :]).astype(narrow)
    rank = jnp.sum(matmul(lower, picks) * picks.astype(wide), 1).astype(jnp.int32)
    send_index = route * capacity + rank
    sender = (jnp.arange(slots)[:, None] == send_index[None, :]).astype(narrow)
    counts = jnp.sum((route_all == mine).astype(jnp.int32), 1)
    ahead = jnp.arange(experts)[:, None] > jnp.arange(experts)[None, :]
    starts = jnp.sum(jnp.where(ahead, counts[None, :], 0), 1)
    place = jnp.arange(capacity)[None, :]
    spots = jnp.where(place < counts[:, None], starts[:, None] + place, -1).reshape(-1)
    taker = (jnp.arange(rows)[:, None] == spots[None, :]).astype(narrow)

    def to_experts(row_data):
        packed = matmul(sender, row_data).astype(narrow).reshape(experts, capacity, width)
        return matmul(taker, exchange(packed, GROUP).reshape(slots, width))

    def to_tokens(row_data):
        packed = matmul_left(taker, row_data).astype(narrow).reshape(experts, capacity, width)
        return matmul_left(sender, exchange(packed, GROUP).reshape(slots, width))

    ct_rows = to_experts(cotangent)

    inputs = tokens.astype(wide)
    attn_gain = attngain.astype(wide)
    attn_xhat, attn_inverse = norm_parts(inputs)
    attn_normed = (attn_xhat * attn_gain + attnshift.astype(wide)).astype(narrow)
    query = (matmul(attn_normed, querymat) + querybias.astype(wide)).astype(narrow)
    key = matmul(attn_normed, keymat).astype(narrow)
    value = (matmul(attn_normed, valuemat) + valuebias.astype(wide)).astype(narrow)
    split = jnp.stack([part.reshape(rows, experts, 128) for part in (query, key, value)], 2)
    qkv = exchange(jnp.transpose(split, (1, 0, 2, 3)).reshape(experts, rows, 384), GROUP)
    normed_all = lax.all_gather(attn_normed, GROUP, axis=0, tiled=True)
    segcol, segrow = seg_all[:, :, None], seg_all[:, None, :]
    low = jnp.sum((seg_all[None, :, -1] < seg_all[:, None, 0]).astype(jnp.int32), 1)
    ctx, full, lse = attend(low, qkv, segcol, segrow)
    context = jnp.transpose(exchange(ctx, GROUP), (1, 0, 2)).reshape(rows, width)
    hidden = inputs + matmul(context, outmat) + outbias.astype(wide)

    stream = to_experts(hidden.astype(narrow))
    gate = jax.nn.sigmoid(jnp.sum(stream * centre, -1, keepdims=True))
    gated = gate * ct_rows
    back_branch = gated.astype(narrow)
    back_branches = share_rows(back_branch, "x")
    front_xhat, front_inverse = norm_parts(stream)
    front_normed = (front_xhat * front_gain + front_shift).astype(narrow)
    front_rows = share_rows(front_normed, "y")
    front_act, front_slope = gelu_pair(matmul(front_rows, front_expand) + front_lift)
    front_act = front_act.astype(narrow)
    front_out = sum_rows(matmul(front_act, front_shrink), "y") + front_offset
    middle = stream + front_out
    back_xhat, back_inverse = norm_parts(middle)
    back_normed = (back_xhat * back_gain + back_shift).astype(narrow)
    back_rows = share_rows(back_normed, "x")
    back_act, back_slope = gelu_pair(matmul(back_rows, back_expand) + back_lift)
    back_act = back_act.astype(narrow)
    back_pre_grad = (back_slope * matmul_right(back_branches, back_shrink)).astype(narrow)
    back_norm_grad = sum_rows(matmul_right(back_pre_grad, back_expand), "x")
    middle_grad = norm_back(back_norm_grad * back_gain, back_xhat, back_inverse)
    front_branch = (gated + middle_grad).astype(narrow)
    front_branches = share_rows(front_branch, "y")
    front_pre_grad = (front_slope * matmul_right(front_branches, front_shrink)).astype(narrow)
    front_norm_grad = sum_rows(matmul_right(front_pre_grad, front_expand), "y")
    first_grad = norm_back(front_norm_grad * front_gain, front_xhat, front_inverse)
    back_out = sum_rows(matmul(back_act, back_shrink), "x") + back_offset
    branches = front_out + back_out
    logit_grad = jnp.sum(ct_rows * branches, -1, keepdims=True) * gate * (1.0 - gate)
    sent_grad = (logit_grad * centre + middle_grad + first_grad).astype(narrow)

    returned = (gate * branches).astype(narrow)
    result = (hidden + to_tokens(returned)).astype(narrow)
    hidden_grad = cotangent.astype(wide) + to_tokens(sent_grad)
    out_low = hidden_grad.astype(narrow)
    context_grad = matmul_right(out_low, outmat).astype(narrow)
    grads = exchange(jnp.transpose(context_grad.reshape(rows, experts, 128), (1, 0, 2)), GROUP)

    def scatter(normed_rows, pre_grad, act, branch_rows, axis):
        expand_grad = matmul_left(normed_rows, pre_grad).astype(narrow).reshape(width, 4, 256)
        expand_grad = lax.psum_scatter(
            jnp.transpose(expand_grad, (1, 0, 2)), axis, scatter_dimension=0, tiled=True
        )
        shrink_grad = lax.psum_scatter(
            matmul_left(act, branch_rows).astype(narrow), axis, scatter_dimension=0, tiled=True
        )
        return expand_grad.astype(wide), shrink_grad.astype(wide)[None]

    back_expand_grad, back_shrink_grad = scatter(
        back_rows, back_pre_grad, back_act, back_branches, "y"
    )
    front_expand_grad, front_shrink_grad = scatter(
        front_rows, front_pre_grad, front_act, front_branches, "x"
    )
    sums = jnp.stack(
        [
            jnp.sum(front_norm_grad * front_xhat, 0),
            jnp.sum(front_norm_grad, 0),
            jnp.sum(front_branch.astype(wide), 0),
            jnp.sum(back_norm_grad * back_xhat, 0),
            jnp.sum(back_norm_grad, 0),
            jnp.sum(back_branch.astype(wide), 0),
            jnp.sum(logit_grad * stream, 0),
        ]
    ).reshape(7, 16, 64)
    front_lift_sum = jnp.sum(front_pre_grad.astype(wide), 0).reshape(4, 1, 256)
    back_lift_sum = jnp.sum(back_pre_grad.astype(wide), 0).reshape(1, 4, 256)
    fours = jnp.arange(4)
    front_lift_sums = jnp.where(fours[None, :, None] == y_at, front_lift_sum, 0.0)
    back_lift_sums = jnp.where(fours[:, None, None] == x_at, back_lift_sum, 0.0)
    packed = jnp.concatenate(
        [
            jnp.transpose(sums, (1, 0, 2)).reshape(16, 448),
            front_lift_sums.reshape(16, 256),
            back_lift_sums.reshape(16, 256),
            jnp.zeros((16, 64), wide),
        ],
        1,
    )
    summed = jnp.sum(exchange(packed.reshape(16, 8, 128), DATA), 0).reshape(1, 1024)
    (
        front_gain_grad, front_shift_grad, front_offset_grad,
        back_gain_grad, back_shift_grad, back_offset_grad, centroid_grad,
    ) = (summed[:, i * 64 : i * 64 + 64] for i in range(7))
    front_lift_grad, back_lift_grad = summed[:, 448:704], summed[:, 704:960]

    dqkv = attend_back(low, qkv, grads, full, lse, segcol, segrow)
    own = jnp.transpose(exchange(dqkv, GROUP).reshape(experts, rows, 3, 128), (2, 1, 0, 3))
    dquery, dkey, dvalue = (own[i].reshape(rows, width) for i in range(3))
    attn_norm_grad = (
        matmul_right(dquery, querymat) + matmul_right(dkey, keymat) + matmul_right(dvalue, valuemat)
    )
    tokens_grad = hidden_grad + norm_back(attn_norm_grad * attn_gain, attn_xhat, attn_inverse)

    dqkv_rows = dqkv.reshape(experts * rows, 384)
    three = exchange(matmul_left(normed_all, dqkv_rows).astype(narrow).reshape(16, 64, 384), DATA)
    three = jnp.sum(three.astype(wide), 0).astype(narrow)
    out_part = matmul_left(context, out_low).astype(narrow).reshape(experts, 128, width)
    out_part = jnp.sum(exchange(out_part, GROUP).astype(wide), 0).astype(narrow)
    out_part = exchange(out_part.reshape(16, 8, width), DATA)
    out_part = jnp.sum(out_part.astype(wide), 0).astype(narrow)
    slices = jnp.concatenate([three.reshape(192, 128), out_part.reshape(64, 128)], 0)
    everything = lax.all_gather(slices, EVERY, axis=0).reshape(16, 8, 256, 128)
    mats = everything[:, :, :192].reshape(16, 8, 64, 3, 128)
    mats = jnp.transpose(mats, (3, 0, 2, 1, 4)).reshape(3, width, width).astype(wide)
    outmat_grad = jnp.transpose(everything[:, :, 192:].reshape(16, 8, 8, width), (1, 0, 2, 3))
    outmat_grad = outmat_grad.reshape(width, width).astype(wide)

    vectors = jnp.stack(
        [
            jnp.sum(out_low.astype(wide), 0),
            jnp.sum(attn_norm_grad * attn_xhat, 0),
            jnp.sum(attn_norm_grad, 0),
            jnp.sum(dquery.astype(wide), 0),
            jnp.sum(dvalue.astype(wide), 0),
        ]
    ).reshape(5, 8, 128)
    vectors = jnp.sum(exchange(jnp.transpose(vectors, (1, 0, 2)), GROUP), 0)
    vectors = jnp.transpose(vectors.reshape(5, 16, 8), (1, 0, 2)).reshape(16, 40)
    vectors = jnp.sum(exchange(vectors, DATA), 0)
    vectors = to_everyone(to_everyone(vectors, DATA, 16), GROUP, experts)
    vectors = jnp.transpose(vectors.reshape(8, 16, 5, 8), (2, 0, 1, 3)).reshape(5, width)
    outbias_grad, attngain_grad, attnshift_grad, querybias_grad, valuebias_grad = vectors
    return (
        result, tokens_grad, attngain_grad, attnshift_grad,
        mats[0], querybias_grad, mats[1], mats[2], valuebias_grad, outmat_grad, outbias_grad,
        front_gain_grad, front_shift_grad, front_expand_grad, front_lift_grad,
        front_shrink_grad, front_offset_grad,
        back_gain_grad, back_shift_grad, back_expand_grad, back_lift_grad,
        back_shrink_grad, back_offset_grad, centroid_grad,
    )


def solution(mesh):
    grid = Mesh(mesh.devices.reshape(4, 4, 4, 2), EVERY)
    rows, plan, full = P(EVERY, None), P(DATA, GROUP), P()
    vector, expand, shrink = P(GROUP, DATA), P(GROUP, None, DATA), P(GROUP, DATA, None)
    sublayer = (vector, vector, expand, vector, shrink, vector)
    return jax.shard_map(
        per_device,
        mesh=grid,
        in_specs=(rows, rows, plan, plan) + (full,) * 9 + sublayer * 2 + (vector,),
        out_specs=(rows, rows) + (full,) * 9 + sublayer * 2 + (vector,),
        check_vma=False,
    )
```

time: 1940 us -> 757 us (0.39)
  waiting for transfers between devices: 1260 us -> 301 us
  blocking collectives: 198 us -> 0 us
  matrix products: 222 us -> 110 us
  starting transfers between devices: 25 us -> 132 us
  other arithmetic: 86.7 us -> 41.6 us
  Pallas kernels: 0 us -> 33.3 us
    unnamed x31 -> x10, waiting for transfers between devices: 652 us -> 2.74 us
    reduce_scatter x6 -> x4, waiting for transfers between devices: 284 us -> 0.01 us  [the longest x2 0.01 us: scatter(): lax.psum_scatter(jnp.transpose(expand_grad, (1, 0, 2)), axis, scatter_dim...]
    psum x1 -> x0, waiting for transfers between devices: 225 us -> none  [per_device(): lax.psum((attngain_grad, attnshift_grad, querymat_grad, querybias_grad, k...]
    ppermute x0 -> x24, waiting for transfers between devices: none -> 183 us  [shift_by(): return lax.ppermute(value, axis, [(i, (i + step) % 4) for i in range(4)])]
    all_to_all x4 -> x18, waiting for transfers between devices: 12.1 us -> 115 us  [exchange(): return lax.all_to_all(blocks, axes, 0, 0, tiled=True)]
    dot_general x36 -> x13, matrix products: 140 us -> 42.5 us  [matmul(): return jnp.dot(left, right, preferred_element_type=wide)]
    all_gather x6, waiting for transfers between devices: 84.1 us -> 0.05 us  [the longest x1 0.02 us: per_device(): front_expand = lax.all_gather(frontexpand[0], 'x', axis=0)]
    all_to_all x4 -> x18, starting transfers between devices: 23.5 us -> 101 us  [exchange(): return lax.all_to_all(blocks, axes, 0, 0, tiled=True)]
  transfers between devices with their start and end apart: 26 -> 52, of which waited for: 18 -> 34; matrix products, arithmetic and copies ran while one was open for 12% -> 25% of each run, Pallas kernels for 0% -> 4%
where the time goes in v1:
time: 757 us; the launch traced here: 746 us
  waiting for transfers between devices  301 us (40%)
  starting transfers between devices  132 us (17%)
  local copies, waits for them, and re-layouts  112 us (15%)
  matrix products  110 us (15%)
  other arithmetic  41.6 us (5%)
  Pallas kernels  33.3 us (4%)
  between operations  15.7 us (2%)
    ppermute x24, waiting for transfers between devices, shift_by(): return lax.ppermute(value, axis, [(i, (i + step) % 4) for i in range(4)])  183 us
    all_to_all x18, waiting for transfers between devices, exchange(): return lax.all_to_all(blocks, axes, 0, 0, tiled=True)  115 us
    all_to_all x18, starting transfers between devices, exchange(): return lax.all_to_all(blocks, axes, 0, 0, tiled=True)  101 us
    dot_general x13, matrix products, matmul(): return jnp.dot(left, right, preferred_element_type=wide)  42.5 us
    dot_general x10, matrix products, matmul_left(): lax.dot_general(left, right, (((0,), (0,)), ((), ())), preferred_element_...  41.4 us
    ppermute x24, starting transfers between devices, shift_by(): return lax.ppermute(value, axis, [(i, (i + step) % 4) for i in range(4)])  29 us
    dot_general x8, matrix products, matmul_right(): lax.dot_general(left, right, (((1,), (1,)), ((), ())), preferred_element_...  26.4 us
    unnamed x157, local copies, waits for them, and re-layouts  26.3 us
  transfers between devices with their start and end apart: 52, of which 34 were waited for; matrix products, arithmetic and copies ran while one was open for 25% of the time, Pallas kernels for 4%

profile of v1, /device:TPU:1, one launch (start us, length us, event | category | flops | bytes accessed | tf_op | source)
XLA Modules:
  0.0 745.9 jit_solution(17309342629885523990)
XLA Ops:
  42.8 19.7 %all-to-all-done.1.qkv_ref = bf16[8,256,384]{2,1,0:T(8,128)(2,1)} async-done(((bf16[8,256,384]{2,1,0:T(8,128)(2,1)}), bf16[8,256,384]{2,1,0:T(8,128)(2,1)}, u32[]{:S(2)}, u32[]{:S(2)}) %all-to-all-start.1) | async-done | bytes 1572896 | tf_op jit(solution)/shard_map/all_to_all | solution.py:70
  62.5 15.9 %attend.1 = (bf16[8,256,128]{2,1,0:T(8,128)(2,1)S(1)}, f32[8,128,256]{2,1,0:T(8,128)S(1)}, f32[8,8,256]{2,1,0:T(8,128)S(1)}) custom-call(s32[8]{0:T(128)S(1)} %convert_reduce_fusion.8.low_ref, bf16[8,256,384]{2,1,0:T(8,128)(2,1)} %all-to-all-done.1.qkv_ref, s32[8,256,1]{2,1,0:T(8,128)S(1)} %copy.110.segcol_ref, s32[8,1,256]{2,1,0:T(1,128)S(1)} %get-tuple-element.95.segrow_ref), custom_call_target="tpu_custom_call" | custom-call | tf_op jit(solution)/shard_map/attend/pallas_call | solution.py:144
  85.6 9.1 %all-to-all-done.2 = bf16[8,256,128]{2,1,0:T(8,128)(2,1)} async-done(((bf16[8,256,128]{2,1,0:T(8,128)(2,1)}), bf16[8,256,128]{2,1,0:T(8,128)(2,1)}, u32[]{:S(2)}, u32[]{:S(2)}) %all-to-all-start.2) | async-done | bytes 524320 | tf_op jit(solution)/shard_map/all_to_all | solution.py:70
  116.3 11.2 %all-to-all-done.3 = bf16[8,48,1024]{2,1,0:T(8,128)(2,1)} async-done(((bf16[8,48,1024]{2,1,0:T(8,128)(2,1)}), bf16[8,48,1024]{2,1,0:T(8,128)(2,1)}, u32[]{:S(2)}, u32[]{:S(2)}) %all-to-all-start.3) | async-done | bytes 786464 | tf_op jit(solution)/shard_map/all_to_all | solution.py:70
  139.4 18.1 %collective-permute-done = bf16[256,1024]{1,0:T(8,128)(2,1)} collective-permute-done((bf16[256,1024]{1,0:T(8,128)(2,1)}, bf16[256,1024]{1,0:T(8,128)(2,1)}, u32[]{:S(2)}, u32[]{:S(2)}) %collective-permute-start) | collective-permute-done | bytes 524320 | tf_op jit(solution)/shard_map/ppermute | solution.py:54
  157.6 13.7 %collective-permute-done.2 = bf16[256,1024]{1,0:T(8,128)(2,1)} collective-permute-done((bf16[256,1024]{1,0:T(8,128)(2,1)}, bf16[256,1024]{1,0:T(8,128)(2,1)}, u32[]{:S(2)}, u32[]{:S(2)}) %collective-permute-start.2) | collective-permute-done | bytes 524320 | tf_op jit(solution)/shard_map/ppermute | solution.py:54
  188.0 10.4 %collective-permute-done.3 = bf16[256,1024]{1,0:T(8,128)(2,1)} collective-permute-done((bf16[256,1024]{1,0:T(8,128)(2,1)}, bf16[256,1024]{1,0:T(8,128)(2,1)}, u32[]{:S(2)}, u32[]{:S(2)}) %collective-permute-start.3) | collective-permute-done | bytes 524320 | tf_op jit(solution)/shard_map/ppermute | solution.py:54
  201.3 9.1 %collective-permute-done.5 = bf16[256,1024]{1,0:T(8,128)(2,1)} collective-permute-done((bf16[256,1024]{1,0:T(8,128)(2,1)}, bf16[256,1024]{1,0:T(8,128)(2,1)}, u32[]{:S(2)}, u32[]{:S(2)}) %collective-permute-start.5) | collective-permute-done | bytes 524320 | tf_op jit(solution)/shard_map/ppermute | solution.py:54
  255.9 8.7 %collective-permute-done.10 = bf16[256,1024]{1,0:T(8,128)(2,1)} collective-permute-done((bf16[256,1024]{1,0:T(8,128)(2,1)}, bf16[256,1024]{1,0:T(8,128)(2,1)}, u32[]{:S(2)}, u32[]{:S(2)}) %collective-permute-start.10) | collective-permute-done | bytes 524320 | tf_op jit(solution)/shard_map/ppermute | solution.py:54
  264.6 9.5 %collective-permute-done.11 = bf16[256,1024]{1,0:T(8,128)(2,1)} collective-permute-done((bf16[256,1024]{1,0:T(8,128)(2,1)}, bf16[256,1024]{1,0:T(8,128)(2,1)}, u32[]{:S(2)}, u32[]{:S(2)}) %collective-permute-start.11) | collective-permute-done | bytes 524320 | tf_op jit(solution)/shard_map/ppermute | solution.py:54
  289.4 9.8 %collective-permute-done.12 = bf16[256,1024]{1,0:T(8,128)(2,1)S(1)} collective-permute-done((bf16[256,1024]{1,0:T(8,128)(2,1)S(1)}, bf16[256,1024]{1,0:T(8,128)(2,1)S(1)}, u32[]{:S(2)}, u32[]{:S(2)}) %collective-permute-start.12) | collective-permute-done | bytes 524320 | tf_op jit(solution)/shard_map/ppermute | solution.py:54
  299.2 12.8 %collective-permute-done.14 = bf16[256,1024]{1,0:T(8,128)(2,1)S(1)} collective-permute-done((bf16[256,1024]{1,0:T(8,128)(2,1)S(1)}, bf16[256,1024]{1,0:T(8,128)(2,1)S(1)}, u32[]{:S(2)}, u32[]{:S(2)}) %collective-permute-start.14) | collective-permute-done | bytes 524320 | tf_op jit(solution)/shard_map/ppermute | solution.py:54
  341.8 9.8 %collective-permute-done.15 = bf16[256,1024]{1,0:T(8,128)(2,1)S(1)} collective-permute-done((bf16[256,1024]{1,0:T(8,128)(2,1)S(1)}, bf16[256,1024]{1,0:T(8,128)(2,1)S(1)}, u32[]{:S(2)}, u32[]{:S(2)}) %collective-permute-start.15) | collective-permute-done | bytes 524320 | tf_op jit(solution)/shard_map/ppermute | solution.py:54
  351.6 11.5 %collective-permute-done.17 = bf16[256,1024]{1,0:T(8,128)(2,1)S(1)} collective-permute-done((bf16[256,1024]{1,0:T(8,128)(2,1)S(1)}, bf16[256,1024]{1,0:T(8,128)(2,1)S(1)}, u32[]{:S(2)}, u32[]{:S(2)}) %collective-permute-start.17) | collective-permute-done | bytes 524320 | tf_op jit(solution)/shard_map/ppermute | solution.py:54
  370.0 11.0 %collective-permute-done.18 = bf16[256,1024]{1,0:T(8,128)(2,1)S(1)} collective-permute-done((bf16[256,1024]{1,0:T(8,128)(2,1)S(1)}, bf16[256,1024]{1,0:T(8,128)(2,1)S(1)}, u32[]{:S(2)}, u32[]{:S(2)}) %collective-permute-start.18) | collective-permute-done | bytes 524320 | tf_op jit(solution)/shard_map/ppermute | solution.py:54
  387.7 18.4 %collective-permute-done.20 = bf16[256,1024]{1,0:T(8,128)(2,1)S(1)} collective-permute-done((bf16[256,1024]{1,0:T(8,128)(2,1)S(1)}, bf16[256,1024]{1,0:T(8,128)(2,1)S(1)}, u32[]{:S(2)}, u32[]{:S(2)}) %collective-permute-start.20) | collective-permute-done | bytes 524320 | tf_op jit(solution)/shard_map/ppermute | solution.py:54
  437.7 13.1 %collective-permute-done.23 = bf16[256,1024]{1,0:T(8,128)(2,1)S(1)} collective-permute-done((bf16[256,1024]{1,0:T(8,128)(2,1)S(1)}, bf16[256,1024]{1,0:T(8,128)(2,1)S(1)}, u32[]{:S(2)}, u32[]{:S(2)}) %collective-permute-start.23) | collective-permute-done | bytes 524320 | tf_op jit(solution)/shard_map/ppermute | solution.py:54
  454.5 8.9 %all-to-all-start.7 = ((bf16[8,48,1024]{2,1,0:T(8,128)(2,1)}), bf16[8,48,1024]{2,1,0:T(8,128)(2,1)}, u32[]{:S(2)}, u32[]{:S(2)}) async-start(bf16[8,48,1024]{2,1,0:T(8,128)(2,1)} %bitcast.218), calls=%async_computation.7 | async-start | bytes 1572864 | tf_op jit(solution)/shard_map/all_to_all | solution.py:70
  505.2 17.4 %attend_back.1 = bf16[8,256,384]{2,1,0:T(8,128)(2,1)S(1)} custom-call(s32[8]{0:T(128)S(1)} %convert_reduce_fusion.8.low_ref, bf16[8,256,384]{2,1,0:T(8,128)(2,1)} %all-to-all-done.1.qkv_ref, bf16[8,256,128]{2,1,0:T(8,128)(2,1)} %all-to-all-done.8.grad_ref, f32[8,128,256]{2,1,0:T(8,128)S(1)} %copy-done.3, f32[8,8,256]{2,1,0:T(8,128)S(1)} %get-tuple-element.29.lse_ref, ...), custom_call_target="tpu_custom_call" | custom-call | tf_op jit(solution)/shard_map/attend_back/pallas_call | solution.py:214
  537.7 10.0 %all-to-all-done.14 = bf16[16,64,384]{2,1,0:T(8,128)(2,1)S(1)} async-done(((bf16[16,64,384]{2,1,0:T(8,128)(2,1)}), bf16[16,64,384]{2,1,0:T(8,128)(2,1)S(1)}, u32[]{:S(2)}, u32[]{:S(2)}) %all-to-all-start.14) | async-done | bytes 786464 | tf_op jit(solution)/shard_map/all_to_all | solution.py:70
  569.8 18.9 %all-to-all-done.9 = bf16[8,256,384]{2,1,0:T(8,128)(2,1)} async-done(((bf16[8,256,384]{2,1,0:T(8,128)(2,1)}), bf16[8,256,384]{2,1,0:T(8,128)(2,1)}, u32[]{:S(2)}, u32[]{:S(2)}) %all-to-all-start.9) | async-done | bytes 1572896 | tf_op jit(solution)/shard_map/all_to_all | solution.py:70
  675.3 9.0 %slice_convert_fusion = f32[16,8,192,128]{3,2,1,0:T(8,128)} fusion(bf16[16,8,256,128]{3,2,1,0:T(8,128)(2,1)} %bitcast.191), kind=kLoop, calls=%fused_computation | loop fusion | flops 3145728 | bytes 18874368 | tf_op jit(solution)/shard_map/convert_element_type | solution.py:407
  688.5 19.2 %copy.124 = f32[16,8,192,128]{3,1,2,0:T(8,128)} copy(f32[16,8,192,128]{3,2,1,0:T(8,128)} %slice_convert_fusion) | data formatting | bytes 25165824 | tf_op jit(solution)/shard_map/convert_element_type | solution.py:407
  707.7 9.7 %fusion.80 = (f32[1,16,64,8,128]{4,3,0,2,1:T(8,128)}, f32[1,16,64,8,128]{4,3,0,2,1:T(8,128)}, f32[1,16,64,8,128]{4,3,0,2,1:T(8,128)}) fusion(f32[3,16,64,8,128]{4,3,0,2,1:T(8,128)} %bitcast.183), kind=kLoop, calls=%fused_computation.191 | loop fusion | bytes 25165824 | tf_op jit(solution)/shard_map/slice | solution.py:428
  (424 shorter events, 425.2 us)
Async XLA Ops:
  7.3 128.2 %all-gather.10.cloned.1.call-start = ((), (), s32[]{:S(2)}) async-start(), calls=%async_computation.22 | async-start | bytes 2621440 | tf_op jit(solution)/shard_map/all_gather | solution.py:258
  8.0 170.4 %all-gather.16.cloned.1.call-start = ((), (), s32[]{:S(2)}) async-start(), calls=%async_computation.29 | async-start | bytes 2621440 | tf_op jit(solution)/shard_map/all_gather | solution.py:259
  10.1 26.8 %all-to-all-start = ((s32[8,2,256]{2,1,0:T(2,128)}), s32[8,2,256]{2,1,0:T(2,128)S(1)}, u32[]{:S(2)}, u32[]{:S(2)}) async-start(s32[8,2,256]{2,1,0:T(2,128)} %broadcast_in_dim.149), calls=%async_computation | async-start | bytes 32768 | tf_op jit(solution)/shard_map/all_to_all | solution.py:70
  16.9 212.2 %all-gather.12.cloned.1.call-start = ((), (), s32[]{:S(2)}) async-start(), calls=%async_computation.23 | async-start | bytes 2621440 | tf_op jit(solution)/shard_map/all_gather | solution.py:260
  36.9 25.6 %all-to-all-start.1 = ((bf16[8,256,384]{2,1,0:T(8,128)(2,1)}), bf16[8,256,384]{2,1,0:T(8,128)(2,1)}, u32[]{:S(2)}, u32[]{:S(2)}) async-start(bf16[8,256,384]{2,1,0:T(8,128)(2,1)} %copy.109), calls=%async_computation.1 | async-start | bytes 3145728 | tf_op jit(solution)/shard_map/all_to_all | solution.py:70
  115.2 130.6 %all-gather.18.cloned.1.call-start = ((), (), s32[]{:S(2)}) async-start(), calls=%async_computation.30 | async-start | bytes 2621440 | tf_op jit(solution)/shard_map/all_gather | solution.py:261
  115.7 407.9 %all-gather.14.cloned.1.call-start = ((), (), s32[]{:S(2)}) async-start(), calls=%async_computation.24 | async-start | bytes 4718592 | tf_op jit(solution)/shard_map/all_gather | solution.py:297
  131.3 26.2 %collective-permute-start = (bf16[256,1024]{1,0:T(8,128)(2,1)}, bf16[256,1024]{1,0:T(8,128)(2,1)}, u32[]{:S(2)}, u32[]{:S(2)}) collective-permute-start(bf16[256,1024]{1,0:T(8,128)(2,1)} %add_convert_fusion.3), channel_id=1, source_target_pairs={{0,8},{8,16},{16,24},{24,0},{1,9},{9,17},{17,25},{25,1},{2,10},{10... | collective-permute-start | bytes 1572872 | tf_op jit(solution)/shard_map/ppermute | solution.py:54
  132.3 25.3 %collective-permute-start.1 = (bf16[256,1024]{1,0:T(8,128)(2,1)}, bf16[256,1024]{1,0:T(8,128)(2,1)}, u32[]{:S(2)}, u32[]{:S(2)}) collective-permute-start(bf16[256,1024]{1,0:T(8,128)(2,1)} %add_convert_fusion.3), channel_id=1, source_target_pairs={{0,24},{8,0},{16,8},{24,16},{1,25},{9,1},{17,9},{25,17},{2,26},{10... | collective-permute-start | bytes 1572872 | tf_op jit(solution)/shard_map/ppermute | solution.py:54
  134.0 37.2 %collective-permute-start.2 = (bf16[256,1024]{1,0:T(8,128)(2,1)}, bf16[256,1024]{1,0:T(8,128)(2,1)}, u32[]{:S(2)}, u32[]{:S(2)}) collective-permute-start(bf16[256,1024]{1,0:T(8,128)(2,1)} %add_convert_fusion.3), channel_id=1, source_target_pairs={{0,16},{8,24},{16,0},{24,8},{1,17},{9,25},{17,1},{25,9},{2,18},{10... | collective-permute-start | bytes 1572872 | tf_op jit(solution)/shard_map/ppermute | solution.py:54
  186.9 23.5 %collective-permute-start.5 = (bf16[256,1024]{1,0:T(8,128)(2,1)}, bf16[256,1024]{1,0:T(8,128)(2,1)}, u32[]{:S(2)}, u32[]{:S(2)}) collective-permute-start(bf16[256,1024]{1,0:T(8,128)(2,1)} %get-tuple-element.74), channel_id=1, source_target_pairs={{0,16},{8,24},{16,0},{24,8},{1,17},{9,25},{17,1},{25,9},{2,18},{10... | collective-permute-start | bytes 1572872 | tf_op jit(solution)/shard_map/ppermute | solution.py:54
  220.2 35.8 %all-to-all-start.6 = ((bf16[8,48,1024]{2,1,0:T(8,128)(2,1)}), bf16[8,48,1024]{2,1,0:T(8,128)(2,1)}, u32[]{:S(2)}, u32[]{:S(2)}) async-start(bf16[8,48,1024]{2,1,0:T(8,128)(2,1)} %bitcast.202), calls=%async_computation.6 | async-start | bytes 1572864 | tf_op jit(solution)/shard_map/all_to_all | solution.py:70
  228.6 438.3 %reduce-scatter.9.cloned.1.call-start = ((), (), s32[]{:S(2)}) async-start(), calls=%async_computation.27 | async-start | bytes 2621440 | tf_op jit(solution)/shard_map/reduce_scatter | solution.py:343
  255.3 23.8 %collective-permute-start.9 = (bf16[256,1024]{1,0:T(8,128)(2,1)}, bf16[256,1024]{1,0:T(8,128)(2,1)}, u32[]{:S(2)}, u32[]{:S(2)}) collective-permute-start(bf16[256,1024]{1,0:T(8,128)(2,1)} %get-tuple-element.70), channel_id=1, source_target_pairs={{0,96},{32,0},{64,32},{96,64},{1,97},{33,1},{65,33},{97,65},{2,98}... | collective-permute-start | bytes 1572872 | tf_op jit(solution)/shard_map/ppermute | solution.py:54
  288.1 23.9 %collective-permute-start.14 = (bf16[256,1024]{1,0:T(8,128)(2,1)S(1)}, bf16[256,1024]{1,0:T(8,128)(2,1)S(1)}, u32[]{:S(2)}, u32[]{:S(2)}) collective-permute-start(bf16[256,1024]{1,0:T(8,128)(2,1)S(1)} %get-tuple-element.50), channel_id=1, source_target_pairs={{0,64},{32,96},{64,0},{96,32},{1,65},{33,97},{65,1},{97,33},{2,66}... | collective-permute-start | bytes 1572872 | tf_op jit(solution)/shard_map/ppermute | solution.py:54
  328.6 340.4 %reduce-scatter.11.cloned.1.call-start = ((), (), s32[]{:S(2)}) async-start(), calls=%async_computation.28 | async-start | bytes 2621440 | tf_op jit(solution)/shard_map/reduce_scatter | solution.py:346
  334.6 336.5 %reduce-scatter.5.cloned.1.call-start = ((), (), s32[]{:S(2)}) async-start(), calls=%async_computation.25 | async-start | bytes 2621440 | tf_op jit(solution)/shard_map/reduce_scatter | solution.py:343
  340.9 22.2 %collective-permute-start.17 = (bf16[256,1024]{1,0:T(8,128)(2,1)S(1)}, bf16[256,1024]{1,0:T(8,128)(2,1)S(1)}, u32[]{:S(2)}, u32[]{:S(2)}) collective-permute-start(bf16[256,1024]{1,0:T(8,128)(2,1)S(1)} %get-tuple-element.68), channel_id=1, source_target_pairs={{0,64},{32,96},{64,0},{96,32},{1,65},{33,97},{65,1},{97,33},{2,66}... | collective-permute-start | bytes 1572872 | tf_op jit(solution)/shard_map/ppermute | solution.py:54
  368.7 37.5 %collective-permute-start.20 = (bf16[256,1024]{1,0:T(8,128)(2,1)S(1)}, bf16[256,1024]{1,0:T(8,128)(2,1)S(1)}, u32[]{:S(2)}, u32[]{:S(2)}) collective-permute-start(bf16[256,1024]{1,0:T(8,128)(2,1)S(1)} %get-tuple-element.52), channel_id=1, source_target_pairs={{0,16},{8,24},{16,0},{24,8},{1,17},{9,25},{17,1},{25,9},{2,18},{10... | collective-permute-start | bytes 1572872 | tf_op jit(solution)/shard_map/ppermute | solution.py:54
  429.5 21.4 %collective-permute-start.23 = (bf16[256,1024]{1,0:T(8,128)(2,1)S(1)}, bf16[256,1024]{1,0:T(8,128)(2,1)S(1)}, u32[]{:S(2)}, u32[]{:S(2)}) collective-permute-start(bf16[256,1024]{1,0:T(8,128)(2,1)S(1)} %get-tuple-element.65), channel_id=1, source_target_pairs={{0,16},{8,24},{16,0},{24,8},{1,17},{9,25},{17,1},{25,9},{2,18},{10... | collective-permute-start | bytes 1572872 | tf_op jit(solution)/shard_map/ppermute | solution.py:54
  463.4 209.8 %reduce-scatter.7.cloned.1.call-start = ((), (), s32[]{:S(2)}) async-start(), calls=%async_computation.26 | async-start | bytes 2621440 | tf_op jit(solution)/shard_map/reduce_scatter | solution.py:346
  498.8 31.6 %all-to-all-start.15 = ((bf16[8,128,1024]{2,1,0:T(8,128)(2,1)}), bf16[8,128,1024]{2,1,0:T(8,128)(2,1)}, u32[]{:S(2)}, u32[]{:S(2)}) async-start(bf16[8,128,1024]{2,1,0:T(8,128)(2,1)} %bitcast.190), calls=%async_computation.15 | async-start | bytes 4194304 | tf_op jit(solution)/shard_map/all_to_all | solution.py:70
  551.4 123.9 %all-gather.20.cloned.1.call-start = ((), (), s32[]{:S(2)}) async-start(), calls=%async_computation.31 | async-start | bytes 8454144 | tf_op jit(solution)/shard_map/all_gather | solution.py:405
  559.6 29.1 %all-to-all-start.9 = ((bf16[8,256,384]{2,1,0:T(8,128)(2,1)}), bf16[8,256,384]{2,1,0:T(8,128)(2,1)}, u32[]{:S(2)}, u32[]{:S(2)}) async-start(bf16[8,256,384]{2,1,0:T(8,128)(2,1)} %copy-done.1), calls=%async_computation.9 | async-start | bytes 3145728 | tf_op jit(solution)/shard_map/all_to_all | solution.py:70
  (100 other events, 1619.1 us)
Sparse Core Ops, SparseCore 0:
  9.8 33.9 all-gather.9
  45.5 30.8 all-gather.15
  78.0 31.0 all-gather.11
  117.3 43.5 all-gather.17
  187.9 34.4 all-gather.13
  328.7 30.9 reduce-scatter.8
  362.2 47.2 reduce-scatter.10
  422.8 32.7 reduce-scatter.4
  469.8 28.6 reduce-scatter.6
  559.6 76.1 all-gather.19

commit v2 on v1

v2 whole, which is shorter than its diff:
```python
import jax
import jax.numpy as jnp
from jax import lax
from jax.experimental import pallas as pl
from jax.experimental.pallas import tpu as pltpu
from jax.sharding import Mesh, PartitionSpec as P

HEADS = 16
HEAD_DIM = 64
EPSILON = 1e-05
MASKED = -1e30

GROUP = ("z", "c")
DATA = ("x", "y1", "y2")
COLUMN = ("y1", "y2")
EVERY = DATA + GROUP

wide = jnp.float32
narrow = jnp.bfloat16


def matmul(left, right):
    return jnp.dot(left, right, preferred_element_type=wide)


def matmul_left(left, right):
    return lax.dot_general(left, right, (((0,), (0,)), ((), ())), preferred_element_type=wide)


def matmul_right(left, right):
    return lax.dot_general(left, right, (((1,), (1,)), ((), ())), preferred_element_type=wide)


def norm_parts(stream):
    center = stream - jnp.mean(stream, -1, keepdims=True)
    inverse = lax.rsqrt(jnp.mean(center * center, -1, keepdims=True) + EPSILON)
    return center * inverse, inverse


def norm_back(scaled, xhat, inverse):
    return (
        scaled
        - jnp.mean(scaled, -1, keepdims=True)
        - xhat * jnp.mean(scaled * xhat, -1, keepdims=True)
    ) * inverse


def gelu_pair(value):
    cdf = 0.5 + 0.5 * lax.erf(value * (0.5**0.5))
    pdf = jnp.exp(-0.5 * value * value) * 0.3989422804014327
    return value * cdf, cdf + value * pdf


def swap(value, axis):
    return lax.ppermute(value, axis, [(0, 1), (1, 0)])


def shift_by(value, step):
    return lax.ppermute(value, "x", [(i, (i + step) % 4) for i in range(4)])


def share_two(rows):
    return jnp.concatenate([rows, swap(rows, "y2")], 0)


def share_four(rows):
    return jnp.concatenate([rows] + [shift_by(rows, step) for step in (1, 3, 2)], 0)


def return_four(partial):
    _, back, ahead, away = jnp.split(partial, 4, 0)
    return shift_by(back, 3), shift_by(ahead, 1), shift_by(away, 2)


def total(own, got):
    return own.astype(wide) + sum(part.astype(wide) for part in got)


def after(first, *later):
    later = lax.optimization_barrier((first,) + later)[1:]
    return later if len(later) > 1 else later[0]


def exchange(blocks, axes):
    return lax.all_to_all(blocks, axes, 0, 0, tiled=True)


def to_everyone(block, axes, count):
    return exchange(jnp.broadcast_to(block[None], (count,) + block.shape), axes)


def head_rows(matrix, head):
    rows = lax.broadcasted_iota(jnp.int32, matrix.shape, 0) // HEAD_DIM
    return jnp.where(rows == head, matrix, jnp.zeros_like(matrix))


def head_lanes(matrix, head):
    lanes = lax.broadcasted_iota(jnp.int32, matrix.shape, 1) // HEAD_DIM
    return jnp.where(lanes == head, matrix, jnp.zeros_like(matrix))


def turn(matrix):
    return jnp.transpose(matrix.astype(wide), (1, 0)).astype(matrix.dtype)


def mask_of(segcol_ref, segrow_ref, i, j, diagonal):
    same = segcol_ref[j] == segrow_ref[i]
    if diagonal:
        size = same.shape
        same = same & (
            lax.broadcasted_iota(jnp.int32, size, 0) <= lax.broadcasted_iota(jnp.int32, size, 1)
        )
    return same


def project_kernel(
    tokens_ref, gain_ref, shift_ref, query_ref, key_ref, value_ref, query_bias_ref, value_bias_ref,
    out_ref, xhat_ref, normed_ref,
):
    @pl.when(pl.program_id(0) == 0)
    def _():
        xhat, _ = norm_parts(tokens_ref[...].astype(wide))
        xhat_ref[...] = xhat.astype(narrow)
        normed = xhat * gain_ref[...].astype(wide) + shift_ref[...].astype(wide)
        normed_ref[...] = normed.astype(narrow)

    normed = normed_ref[...]
    query = matmul(normed, query_ref[...]) + query_bias_ref[...].astype(wide)
    value = matmul(normed, value_ref[...]) + value_bias_ref[...].astype(wide)
    out_ref[0, :, 0:128] = query.astype(narrow)
    out_ref[0, :, 128:256] = matmul(normed, key_ref[...]).astype(narrow)
    out_ref[0, :, 256:384] = value.astype(narrow)


def project(tokens, gain, shift, querymat, querybias, keymat, valuemat, valuebias):
    rows, width = tokens.shape
    all_rows = pl.BlockSpec((rows, width), lambda e: (0, 0))
    line = pl.BlockSpec((1, width), lambda e: (0, 0))
    mat, bias = pl.BlockSpec((width, 128), lambda e: (0, e)), pl.BlockSpec((1, 128), lambda e: (0, e))
    return pl.pallas_call(
        project_kernel,
        grid=(8,),
        out_shape=(
            jax.ShapeDtypeStruct((8, rows, 384), narrow),
            jax.ShapeDtypeStruct((rows, width), narrow),
        ),
        in_specs=[all_rows, line, line, mat, mat, mat, bias, bias],
        out_specs=(pl.BlockSpec((1, rows, 384), lambda e: (e, 0, 0)), all_rows),
        scratch_shapes=[pltpu.VMEM((rows, width), narrow)],
        compiler_params=pltpu.CompilerParams(vmem_limit_bytes=32 << 20),
        name="project",
    )(tokens, gain, shift, querymat, keymat, valuemat, querybias, valuebias)


def join_kernel(ctx_ref, outmat_ref, tokens_ref, bias_ref, sender_ref, hidden_ref, packed_ref, context_ref):
    @pl.when(pl.program_id(0) == 0)
    def _():
        for e in range(8):
            context_ref[:, e * 128 : e * 128 + 128] = ctx_ref[e]

    hidden = tokens_ref[...].astype(wide) + bias_ref[...].astype(wide)
    hidden = hidden + matmul(context_ref[...], outmat_ref[...])
    hidden_ref[...] = hidden
    packed_ref[...] = matmul(sender_ref[...], hidden.astype(narrow)).astype(narrow)


def join(ctx, outmat, tokens, outbias, sender):
    rows, width = tokens.shape
    slots = sender.shape[0]
    strip = lambda height: pl.BlockSpec((height, 256), lambda n: (0, n))
    return pl.pallas_call(
        join_kernel,
        grid=(4,),
        out_shape=(
            jax.ShapeDtypeStruct((rows, width), wide),
            jax.ShapeDtypeStruct((slots, width), narrow),
            jax.ShapeDtypeStruct((rows, width), narrow),
        ),
        in_specs=[
            pl.BlockSpec((8, rows, 128), lambda n: (0, 0, 0)),
            strip(width), strip(rows), strip(1),
            pl.BlockSpec((slots, rows), lambda n: (0, 0)),
        ],
        out_specs=(strip(rows), strip(slots), pl.BlockSpec((rows, width), lambda n: (0, 0))),
        compiler_params=pltpu.CompilerParams(vmem_limit_bytes=32 << 20),
        name="join",
    )(ctx, outmat, tokens, outbias, sender)


def hidden_back_kernel(blocks_ref, getter_ref, cotangent_ref, outmat_ref, hidden_ref, grads_ref, low_ref):
    @pl.when(pl.program_id(0) == 0)
    def _():
        hidden = cotangent_ref[...].astype(wide) + matmul(getter_ref[...], blocks_ref[...])
        hidden_ref[...] = hidden
        low_ref[...] = hidden.astype(narrow)

    grads = matmul_right(low_ref[...], outmat_ref[...]).astype(narrow)
    grads_ref[0] = grads[:, 0:128]
    grads_ref[1] = grads[:, 128:256]


def hidden_back(blocks, getter, cotangent, outmat):
    rows, width = cotangent.shape
    slots = getter.shape[1]
    all_rows = pl.BlockSpec((rows, width), lambda e: (0, 0))
    return pl.pallas_call(
        hidden_back_kernel,
        grid=(4,),
        out_shape=(
            jax.ShapeDtypeStruct((rows, width), wide),
            jax.ShapeDtypeStruct((8, rows, 128), narrow),
            jax.ShapeDtypeStruct((rows, width), narrow),
        ),
        in_specs=[
            pl.BlockSpec((slots, width), lambda e: (0, 0)),
            pl.BlockSpec((rows, slots), lambda e: (0, 0)),
            all_rows,
            pl.BlockSpec((256, width), lambda e: (e, 0)),
        ],
        out_specs=(all_rows, pl.BlockSpec((2, rows, 128), lambda e: (e, 0, 0)), all_rows),
        compiler_params=pltpu.CompilerParams(vmem_limit_bytes=32 << 20),
        name="hidden_back",
    )(blocks, getter, cotangent, outmat)


def attend_kernel(low_ref, qkv_ref, segcol_ref, segrow_ref, ctx_ref, full_ref, lse_ref, vals_ref):
    blocks, size, _ = qkv_ref.shape
    for j in range(blocks):
        turned = turn(qkv_ref[j, :, 256:384])
        for head in range(2):
            vals_ref[j, head, 0:64, :] = turned[head * 64 : head * 64 + 64]
            vals_ref[j, head, 64:80, :] = jnp.ones((16, size), narrow)
    for i in range(blocks):
        query = turn((qkv_ref[i, :, 0:128].astype(wide) * HEAD_DIM**-0.5).astype(narrow))
        queries = [head_rows(query, head) for head in range(2)]

        def step(j, carry, diagonal):
            keys = qkv_ref[j, :, 128:256]
            mask = mask_of(segcol_ref, segrow_ref, i, j, diagonal)
            out = []
            for head in range(2):
                scores = jnp.where(mask, matmul(keys, queries[head]), MASKED)
                top = jnp.max(scores, 0, keepdims=True)
                if carry is not None:
                    top = jnp.maximum(top, carry[2 * head])
                probs = jnp.exp(scores - top).astype(narrow)
                total = matmul(vals_ref[j, head], probs)
                if carry is not None:
                    total = total + carry[2 * head + 1] * jnp.exp(carry[2 * head] - top)
                out += [top, total]
            return tuple(out)

        carry = step(i, None, True)
        if i > 0:
            carry = lax.fori_loop(low_ref[i], i, lambda j, c: step(j, c, False), carry)
        parts = []
        for head in range(2):
            top, total = carry[2 * head], carry[2 * head + 1]
            parts.append(total[0:64] / total[64:65])
            lse_ref[i, head : head + 1, :] = top + jnp.log(total[64:65])
        full = jnp.concatenate(parts, 0)
        full_ref[i] = full
        ctx_ref[i] = jnp.transpose(full, (1, 0)).astype(narrow)


def attend(low, qkv, segcol, segrow):
    blocks, size, _ = qkv.shape
    vmem = pl.BlockSpec(memory_space=pltpu.VMEM)
    return pl.pallas_call(
        attend_kernel,
        out_shape=(
            jax.ShapeDtypeStruct((blocks, size, 128), narrow),
            jax.ShapeDtypeStruct((blocks, 128, size), wide),
            jax.ShapeDtypeStruct((blocks, 8, size), wide),
        ),
        in_specs=[pl.BlockSpec(memory_space=pltpu.SMEM), vmem, vmem, vmem],
        out_specs=(vmem, vmem, vmem),
        scratch_shapes=[pltpu.VMEM((blocks, 2, 80, size), narrow)],
        compiler_params=pltpu.CompilerParams(vmem_limit_bytes=40 << 20),
        name="attend",
    )(low, qkv, segcol, segrow)


def attend_back_kernel(
    low_ref, qkv_ref, grad_ref, full_ref, lse_ref, segcol_ref, segrow_ref, xhat_ref,
    out_ref, three_ref, sums_ref, keys_ref, dk_ref, dv_ref,
):
    blocks, size, _ = qkv_ref.shape
    for j in range(blocks):
        keys_ref[j] = turn(qkv_ref[j, :, 128:256])
    dk_ref[...] = jnp.zeros_like(dk_ref)
    dv_ref[...] = jnp.zeros_like(dv_ref)
    for i in range(blocks):
        query = (qkv_ref[i, :, 0:128].astype(wide) * HEAD_DIM**-0.5).astype(narrow)
        query_t = turn(query)
        grad = grad_ref[i]
        grad_t = turn(grad)
        inner = grad_t.astype(wide) * full_ref[i]
        queries_t = [head_rows(query_t, head) for head in range(2)]
        grads_t = [head_rows(grad_t, head) for head in range(2)]
        inners = [
            jnp.sum(inner[head * 64 : head * 64 + 64], 0, keepdims=True) for head in range(2)
        ]
        lses = [lse_ref[i, head : head + 1, :] for head in range(2)]
        query_pair = jnp.concatenate([head_lanes(query, head) for head in range(2)], 0)
        grad_pair = jnp.concatenate([head_lanes(grad, head) for head in range(2)], 0)

        def step(j, carry, diagonal):
            keys = qkv_ref[j, :, 128:256]
            vals = qkv_ref[j, :, 256:384]
            mask = mask_of(segcol_ref, segrow_ref, i, j, diagonal)
            lows, score_lows, out = [], [], []
            for head in range(2):
                scores = matmul(keys, queries_t[head])
                probs = jnp.where(mask, jnp.exp(scores - lses[head]), 0.0)
                prob_grad = matmul(vals, grads_t[head])
                score_low = (probs * (prob_grad - inners[head])).astype(narrow)
                lows.append(probs.astype(narrow))
                score_lows.append(score_low)
                part = matmul(keys_ref[j, head * 64 : head * 64 + 64, :], score_low)
                out.append(part if carry is None else carry[head] + part)
            dv_ref[j] += matmul(jnp.concatenate(lows, 1), grad_pair)
            dk_ref[j] += matmul(jnp.concatenate(score_lows, 1), query_pair)
            return tuple(out)

        carry = step(i, None, True)
        if i > 0:
            carry = lax.fori_loop(low_ref[i], i, lambda j, c: step(j, c, False), carry)
        dq = jnp.concatenate(carry, 0) * HEAD_DIM**-0.5
        out_ref[i, :, 0:128] = jnp.transpose(dq, (1, 0)).astype(narrow)
    for j in range(blocks):
        out_ref[j, :, 128:256] = dk_ref[j].astype(narrow)
        out_ref[j, :, 256:384] = dv_ref[j].astype(narrow)
    for part in range(4):
        height = slice(part * 256, part * 256 + 256)
        three = sum(matmul(xhat_ref[j, height, :], out_ref[j]) for j in range(blocks))
        for d in range(4):
            for i in range(3):
                three_ref[part * 4 + d, i * 64 : i * 64 + 64, :] = three[
                    d * 64 : d * 64 + 64, i * 128 : i * 128 + 128
                ].astype(narrow)
    sums_ref[...] = sum(jnp.sum(out_ref[j].astype(wide), 0, keepdims=True) for j in range(blocks))


def attend_back(low, qkv, grad, full, lse, segcol, segrow, xhat):
    blocks, size, _ = qkv.shape
    vmem = pl.BlockSpec(memory_space=pltpu.VMEM)
    return pl.pallas_call(
        attend_back_kernel,
        out_shape=(
            jax.ShapeDtypeStruct((blocks, size, 384), narrow),
            jax.ShapeDtypeStruct((16, 192, 128), narrow),
            jax.ShapeDtypeStruct((1, 384), wide),
        ),
        in_specs=[pl.BlockSpec(memory_space=pltpu.SMEM)] + [vmem] * 7,
        out_specs=(vmem, vmem, vmem),
        scratch_shapes=[
            pltpu.VMEM((blocks, 128, size), narrow),
            pltpu.VMEM((blocks, size, 128), wide),
            pltpu.VMEM((blocks, size, 128), wide),
        ],
        compiler_params=pltpu.CompilerParams(vmem_limit_bytes=40 << 20),
        name="attend_back",
    )(low, qkv, grad, full, lse, segcol, segrow, xhat)


def unpack_kernel(
    all_ref, bias_ref, gain_ref, shift_ref, query_ref, key_ref, value_ref,
    dquery_ref, dkey_ref, dvalue_ref, dout_ref, vector_ref,
):
    mats = ((query_ref, dquery_ref), (key_ref, dkey_ref), (value_ref, dvalue_ref))
    for d in range(all_ref.shape[0]):
        height = slice(d * 64, d * 64 + 64)
        gain, shift = gain_ref[d].astype(wide), shift_ref[d].astype(wide)
        gain_sum = shift_sum = jnp.zeros((64, 128), wide)
        for e in range(8):
            lanes = slice(e * 128, e * 128 + 128)
            for i, (mat_ref, grad_ref) in enumerate(mats):
                part = all_ref[d, e, i * 64 : i * 64 + 64, :].astype(wide)
                bias = bias_ref[i : i + 1, lanes]
                mat = mat_ref[height, lanes].astype(wide)
                grad_ref[height, lanes] = gain * part + shift * bias
                gain_sum = gain_sum + mat * part
                shift_sum = shift_sum + mat * bias
            for i in range(8):
                dout_ref[e, d, :, i * 128 : i * 128 + 128] = all_ref[
                    d, e, 192 + i * 8 : 200 + i * 8, :
                ].astype(wide)
        vector_ref[d, :, 0:1] = jnp.sum(gain_sum, 1, keepdims=True)
        vector_ref[d, :, 1:2] = jnp.sum(shift_sum, 1, keepdims=True)


def unpack(everything, biases, gain, shift, querymat, keymat, valuemat, step=2):
    width = querymat.shape[0]
    column = pl.BlockSpec((step, 64, 1), lambda d: (d, 0, 0))
    strip = pl.BlockSpec((step * 64, width), lambda d: (d, 0))
    square = jax.ShapeDtypeStruct((width, width), wide)
    return pl.pallas_call(
        unpack_kernel,
        grid=(16 // step,),
        out_shape=(
            square, square, square,
            jax.ShapeDtypeStruct((8, 16, 8, width), wide),
            jax.ShapeDtypeStruct((16, 64, 2), wide),
        ),
        in_specs=[
            pl.BlockSpec((step, 8, 264, 128), lambda d: (d, 0, 0, 0)),
            pl.BlockSpec((3, width), lambda d: (0, 0)),
            column, column, strip, strip, strip,
        ],
        out_specs=(
            strip, strip, strip,
            pl.BlockSpec((8, step, 8, width), lambda d: (0, d, 0, 0)),
            pl.BlockSpec((step, 64, 2), lambda d: (d, 0, 0)),
        ),
        compiler_params=pltpu.CompilerParams(vmem_limit_bytes=32 << 20),
        name="unpack",
    )(everything, biases, gain, shift, querymat, keymat, valuemat)


def per_device(
    tokens, cotangent, segments, routes,
    attngain, attnshift, querymat, querybias, keymat, valuemat, valuebias, outmat, outbias,
    frontgain, frontshift, frontexpand, frontlift, frontreduce, frontoffset,
    backgain, backshift, backexpand, backlift, backreduce, backoffset, centroid,
):
    rows, width = tokens.shape
    experts = 8
    capacity = rows // experts + rows // (2 * experts)
    slots = experts * capacity
    mine = lax.axis_index(GROUP)
    x_at, y1_at, y2_at = (lax.axis_index(axis) for axis in DATA)

    plans = to_everyone(jnp.concatenate([segments, routes], 0), GROUP, experts)
    small_own = jnp.concatenate(
        [
            frontgain[0], frontshift[0], frontoffset[0], backgain[0], backshift[0], backoffset[0],
            centroid[0], frontlift[0], backlift[0], jnp.zeros((64,), narrow),
        ]
    )
    small = small_own.reshape(8, 128)

    def reduced(matrix, axes):
        return lax.psum_scatter(matrix, axes, scatter_dimension=0, tiled=True)

    def gathered(matrix, axes):
        return lax.all_gather(matrix, axes, axis=0, tiled=True)

    front_expand, front_shrink = frontexpand[0].T, frontreduce[0]
    front_pair = swap(jnp.concatenate([front_expand, front_shrink], 0), "y1")
    front_expands, front_shrinks = [gathered(front_expand, "x")], [gathered(front_shrink, "x")]

    route = routes[0]
    picks = (route[:, None] == jnp.arange(experts)[None, :]).astype(narrow)
    lower = (jnp.arange(rows)[:, None] > jnp.arange(rows)[None, :]).astype(narrow)
    rank = jnp.sum(matmul(lower, picks) * picks.astype(wide), 1).astype(jnp.int32)
    send_index = route * capacity + rank
    sender = (jnp.arange(slots)[:, None] == send_index[None, :]).astype(narrow)
    def pack(row_data):
        return matmul(sender, row_data).astype(narrow).reshape(experts, capacity, width)

    def unpack_rows(blocks):
        return matmul(taker, blocks.reshape(slots, width)).astype(narrow)

    def pack_back(row_data):
        return matmul_left(taker, row_data).astype(narrow).reshape(experts, capacity, width)

    def unpack_back(blocks):
        return matmul_left(sender, blocks.reshape(slots, width))

    line = lambda vector: vector.reshape(1, width)
    split, xhat_low = project(
        tokens, line(attngain), line(attnshift),
        querymat, line(querybias), keymat, valuemat, line(valuebias),
    )
    split, plans = lax.optimization_barrier((split, plans))
    seg_all, route_all = plans[:, 0], plans[:, 1]
    qkv = exchange(split, GROUP)
    small = to_everyone(after(qkv, small), DATA, 16)
    counts = jnp.sum((route_all == mine).astype(jnp.int32), 1)
    ahead = jnp.arange(experts)[:, None] > jnp.arange(experts)[None, :]
    starts = jnp.sum(jnp.where(ahead, counts[None, :], 0), 1)
    place = jnp.arange(capacity)[None, :]
    spots = jnp.where(place < counts[:, None], starts[:, None] + place, -1).reshape(-1)
    taker = (jnp.arange(rows)[:, None] == spots[None, :]).astype(narrow)

    segcol, segrow = seg_all[:, :, None], seg_all[:, None, :]
    low = jnp.sum((seg_all[None, :, -1] < seg_all[:, None, 0]).astype(jnp.int32), 1)
    ctx, full, lse = attend(low, qkv, segcol, segrow)
    ctx, small = lax.optimization_barrier((ctx, small))
    front_pair, back_expand, back_shrink = after(ctx, front_pair, backexpand[0].T, backreduce[0])
    front_expands.append(gathered(front_pair[:256], "x"))
    front_shrinks.append(gathered(front_pair[256:], "x"))
    back_expand, back_shrink = gathered(back_expand, COLUMN), gathered(back_shrink, COLUMN)
    small = small.reshape(16, 1024).astype(wide)
    front_gain, front_shift, front_offset, back_gain, back_shift, back_offset, centre = (
        small[:, i * 64 : i * 64 + 64].reshape(1, width) for i in range(7)
    )
    lifts = small[:, 448:960].reshape(4, 2, 2, 512)
    front_lift = lax.dynamic_index_in_dim(lifts, y2_at, 2, False)[:, :, :256]
    front_lift = jnp.where(y1_at == 0, front_lift, front_lift[:, ::-1])
    front_lift = jnp.transpose(front_lift, (1, 0, 2)).reshape(2, 1, 1024)
    back_lift = lax.dynamic_index_in_dim(lifts, x_at, 0, False)[:, :, 256:].reshape(1, 1024)
    hidden, blocks, context = join(exchange(ctx, GROUP), outmat, tokens, line(outbias), sender)
    xhat_all = lax.all_gather(after(blocks, xhat_low).T, GROUP, axis=0)

    stream = unpack_rows(exchange(blocks.reshape(experts, capacity, width), GROUP)).astype(wide)
    front_xhat, front_inverse = norm_parts(stream)
    front_normed = share_two((front_xhat * front_gain + front_shift).astype(narrow))
    gate = jax.nn.sigmoid(jnp.sum(stream * centre, -1, keepdims=True))
    ct_blocks = exchange(pack(after(front_normed, cotangent)), GROUP)
    front_acts, front_slopes = [], []
    for expand, lift in zip(front_expands, front_lift):
        act, slope = gelu_pair(matmul_right(front_normed, expand) + lift)
        front_acts.append(act.astype(narrow))
        front_slopes.append(slope)
    front_part = sum(matmul(act, shrink) for act, shrink in zip(front_acts, front_shrinks))
    front_part, ct_blocks = lax.optimization_barrier((front_part, ct_blocks))
    ct_rows = unpack_rows(ct_blocks).astype(wide)
    gated = gate * ct_rows
    back_branch = gated.astype(narrow)
    front_got, back_branches = lax.optimization_barrier(
        (swap(front_part[rows:].astype(narrow), "y2"), share_four(back_branch))
    )
    front_out = front_part[:rows] + front_got.astype(wide) + front_offset
    middle = stream + front_out
    back_xhat, back_inverse = norm_parts(middle)
    back_normed = share_four((back_xhat * back_gain + back_shift).astype(narrow))
    back_act, back_slope = gelu_pair(matmul_right(back_normed, back_expand) + back_lift)
    back_act = back_act.astype(narrow)
    back_pre_grad = (back_slope * matmul_right(back_branches, back_shrink)).astype(narrow)
    back_part = matmul(back_pre_grad, back_expand).astype(narrow)
    act_late, normed_late, back_pre_late = after(back_part, back_act, back_normed, back_pre_grad)
    back_grads = [matmul_left(act_late, back_branches), matmul_left(back_pre_late, normed_late)]
    back_grads = [part.astype(narrow) for part in back_grads]
    *back_got, shrink_part, expand_part = lax.optimization_barrier(
        (*return_four(back_part), *back_grads)
    )
    back_grads = [reduced(part, COLUMN) for part in (shrink_part, expand_part)]
    back_norm_grad = total(back_part[:rows], back_got)
    middle_grad = norm_back(back_norm_grad * back_gain, back_xhat, back_inverse)
    front_branch = (gated + middle_grad).astype(narrow)
    out_part = matmul(after(front_branch, back_act), back_shrink).astype(narrow)
    branch_got, out_part = lax.optimization_barrier((swap(front_branch, "y2"), out_part))
    front_branches = jnp.concatenate([front_branch, branch_got], 0)
    front_pre_grads = [
        (slope * matmul_right(front_branches, shrink)).astype(narrow)
        for slope, shrink in zip(front_slopes, front_shrinks)
    ]
    front_part = sum(matmul(grad, expand) for grad, expand in zip(front_pre_grads, front_expands))
    front_low = front_part[rows:].astype(narrow)
    front_acts = after(front_low, *front_acts)
    front_shrink_part = [matmul_left(act, front_branches).astype(narrow) for act in front_acts]
    front_got, out_got, front_shrink_part = lax.optimization_barrier(
        (swap(front_low, "y2"), return_four(out_part), front_shrink_part)
    )
    front_shrink_part = [reduced(part, "x") for part in front_shrink_part]
    front_norm_grad = front_part[:rows] + front_got.astype(wide)
    first_grad = norm_back(front_norm_grad * front_gain, front_xhat, front_inverse)
    branches = front_out + total(out_part[:rows], out_got) + back_offset
    logit_grad = jnp.sum(ct_rows * branches, -1, keepdims=True) * gate * (1.0 - gate)
    sent_grad = (logit_grad * centre + middle_grad + first_grad).astype(narrow)

    sent_blocks = pack_back(sent_grad)
    normed_late, *front_pre_late = after(sent_blocks, front_normed, *front_pre_grads)
    front_expand_part = [matmul_left(grad, normed_late).astype(narrow) for grad in front_pre_late]
    sent_blocks, front_expand_part, back_grads = lax.optimization_barrier(
        (exchange(sent_blocks, GROUP), front_expand_part, back_grads)
    )
    front_expand_part = [reduced(part, "x") for part in front_expand_part]
    getter = (send_index[:, None] == jnp.arange(slots)[None, :]).astype(narrow)
    hidden_grad, context_grad, out_low = hidden_back(
        sent_blocks.reshape(slots, width), getter, cotangent, outmat
    )
    grads = exchange(context_grad, GROUP)
    context, out_late = after(context_grad, context, out_low)
    out_part = matmul_left(context, out_late).astype(narrow).reshape(experts, 128, width)
    grads, out_part = lax.optimization_barrier((grads, out_part))
    out_part = exchange(out_part, GROUP)
    grads, xhat_all, front_shrink_part = lax.optimization_barrier((grads, xhat_all, front_shrink_part))

    dqkv, three, sums = attend_back(low, qkv, grads, full, lse, segcol, segrow, xhat_all)

    out_part = jnp.sum(out_part.astype(wide), 0).astype(narrow).reshape(16, 8, 8, 128)
    biases = jnp.concatenate(
        [
            sums.reshape(16, 24),
            jnp.sum(out_low.astype(wide), 0).reshape(16, 64),
        ],
        1,
    ).astype(narrow)
    expert_sums = jnp.stack(
        [
            jnp.sum(front_norm_grad * front_xhat, 0),
            jnp.sum(front_norm_grad, 0),
            jnp.sum(front_branch.astype(wide), 0),
            jnp.sum(back_norm_grad * back_xhat, 0),
            jnp.sum(back_norm_grad, 0),
            jnp.sum(back_branch.astype(wide), 0),
            jnp.sum(logit_grad * stream, 0),
        ]
    ).reshape(7, 16, 64)
    front_lifts = jnp.stack([jnp.sum(grad.astype(wide), 0).reshape(4, 256) for grad in front_pre_late], 1)
    front_lifts = jnp.where(y1_at == 0, front_lifts, front_lifts[:, ::-1])
    front_lifts = jnp.where(jnp.arange(2)[:, None] == y2_at, front_lifts[:, :, None], 0.0)
    back_lifts = jnp.sum(back_pre_late.astype(wide), 0).reshape(1, 4, 256)
    back_lifts = jnp.where(jnp.arange(4)[:, None, None] == x_at, back_lifts, 0.0)
    packed = jnp.concatenate(
        [
            jnp.transpose(expert_sums, (1, 0, 2)).reshape(16, 448),
            front_lifts.reshape(16, 256),
            back_lifts.reshape(16, 256),
            jnp.zeros((16, 64), wide),
        ],
        1,
    )
    slices = jnp.concatenate(
        [
            three,
            jnp.transpose(out_part, (0, 2, 1, 3)).reshape(16, 64, 128),
            jnp.pad(biases[:, None], ((0, 0), (0, 7), (0, 40))),
            packed.reshape(16, 8, 128).astype(narrow),
        ],
        1,
    )
    front_swap = swap(front_shrink_part[1], "y1")
    slices, front_swap, front_expand_part = lax.optimization_barrier(
        (exchange(slices, DATA), front_swap, front_expand_part)
    )
    slices = jnp.sum(slices.astype(wide), 0)
    summed = slices[264:].reshape(1, 1024)
    slices = slices[:264].astype(narrow)
    everything = lax.all_gather(slices, EVERY, axis=0).reshape(16, 8, 264, 128)
    biases = everything[:, :, 256, :88].astype(wide)
    outbias_grad = jnp.sum(biases[:, :, 24:], 1).reshape(width)
    biases = jnp.transpose(biases[:, :, :24], (1, 0, 2)).reshape(8, 3, 128)
    biases = jnp.transpose(biases, (1, 0, 2)).reshape(3, width)
    query_grad, key_grad, value_grad, outmat_grad, vectors = unpack(
        everything, biases, attngain.reshape(16, 64, 1), attnshift.reshape(16, 64, 1),
        querymat, keymat, valuemat,
    )
    outmat_grad = outmat_grad.reshape(width, width)
    attngain_grad, attnshift_grad = vectors[:, :, 0].reshape(width), vectors[:, :, 1].reshape(width)
    querybias_grad, _, valuebias_grad = biases

    dqkv, returned, front_expand_own, other = after(
        slices, dqkv, pack_back((gate * branches).astype(narrow)), *front_expand_part
    )
    own, returned, other = lax.optimization_barrier(
        (exchange(dqkv, GROUP), exchange(returned, GROUP), swap(other, "y1"))
    )
    own = jnp.transpose(own.reshape(experts, rows, 3, 128), (2, 1, 0, 3))
    dquery, dkey, dvalue = (own[i].reshape(rows, width) for i in range(3))
    attn_norm_grad = (
        matmul_right(dquery, querymat) + matmul_right(dkey, keymat) + matmul_right(dvalue, valuemat)
    )
    attn_xhat, attn_inverse = norm_parts(tokens.astype(wide))
    tokens_grad = hidden_grad + norm_back(
        attn_norm_grad * attngain.astype(wide), attn_xhat, attn_inverse
    )
    result = (hidden + unpack_back(returned)).astype(narrow)
    back_shrink_grad, back_expand_grad = (grad.astype(wide) for grad in back_grads)
    front_shrink_grad = front_shrink_part[0].astype(wide) + front_swap.astype(wide)
    front_expand_grad = front_expand_own.astype(wide) + other.astype(wide)
    back_shrink_grad, front_shrink_grad = back_shrink_grad[None], front_shrink_grad[None]
    back_expand_grad, front_expand_grad = back_expand_grad.T[None], front_expand_grad.T[None]
    (
        front_gain_grad, front_shift_grad, front_offset_grad,
        back_gain_grad, back_shift_grad, back_offset_grad, centroid_grad,
    ) = (summed[:, i * 64 : i * 64 + 64] for i in range(7))
    front_lift_grad, back_lift_grad = summed[:, 448:704], summed[:, 704:960]

    return (
        result, tokens_grad, attngain_grad, attnshift_grad,
        query_grad, querybias_grad, key_grad, value_grad, valuebias_grad, outmat_grad, outbias_grad,
        front_gain_grad, front_shift_grad, front_expand_grad, front_lift_grad,
        front_shrink_grad, front_offset_grad,
        back_gain_grad, back_shift_grad, back_expand_grad, back_lift_grad,
        back_shrink_grad, back_offset_grad, centroid_grad,
    )


def solution(mesh):
    grid = Mesh(mesh.devices.reshape(4, 2, 2, 4, 2), EVERY)
    rows, plan, full = P(EVERY, None), P(DATA, GROUP), P()
    vector, expand, shrink = P(GROUP, DATA), P(GROUP, None, DATA), P(GROUP, DATA, None)
    sublayer = (vector, vector, expand, vector, shrink, vector)
    return jax.shard_map(
        per_device,
        mesh=grid,
        in_specs=(rows, rows, plan, plan) + (full,) * 9 + sublayer * 2 + (vector,),
        out_specs=(rows, rows) + (full,) * 9 + sublayer * 2 + (vector,),
        check_vma=False,
    )
```

time: 757 us -> 620 us (0.82)
  waiting for transfers between devices: 301 us -> 226 us
  local copies, waits for them, and re-layouts: 112 us -> 77.1 us
  starting transfers between devices: 132 us -> 99.1 us
  Pallas kernels: 33.3 us -> 55.5 us
  matrix products: 110 us -> 89.7 us
    all_to_all x18 -> x12, waiting for transfers between devices: 115 us -> 55.8 us  [exchange(): return lax.all_to_all(blocks, axes, 0, 0, tiled=True)]
    ppermute x24 -> x19, waiting for transfers between devices: 183 us -> 129 us  [the longest x12 67.4 us: shift_by(): return lax.ppermute(value, 'x', [(i, (i + step) % 4) for i in range(4)])]
    all_to_all x18 -> x12, starting transfers between devices: 101 us -> 66.2 us  [exchange(): return lax.all_to_all(blocks, axes, 0, 0, tiled=True)]
    convert_element_type x4 -> x0, local copies, waits for them, and re-layouts: 30.9 us -> none  [the longest x1 19.2 us: per_device(): jnp.transpose(mats, (3, 0, 2, 1, 4)).reshape(3, width, width).astype(wide)]
    all_gather x6 -> x8, waiting for transfers between devices: 0.05 us -> 30.4 us  [the longest x6 18.3 us: gathered(): return lax.all_gather(matrix, axes, axis=0, tiled=True)]
    pallas_call x1 -> x5, Pallas kernels: 17.4 us -> 39.8 us  [the longest x1 18.8 us: attend_back(): pl.pallas_call(attend_back_kernel, out_shape=(jax.ShapeDtypeStruct((block...]
    dot_general x13 -> x10, matrix products: 42.5 us -> 23.1 us  [matmul(): return jnp.dot(left, right, preferred_element_type=wide)]
    unnamed x157 -> x209, local copies, waits for them, and re-layouts: 26.3 us -> 44.7 us
  transfers between devices with their start and end apart: 52 -> 45, of which waited for: 34 -> 25; matrix products, arithmetic and copies ran while one was open for 25% -> 25% of each run, Pallas kernels for 4% -> 8%
where the time goes in v2:
time: 620 us; the launch traced here: 610 us
  waiting for transfers between devices  226 us (36%)
  starting transfers between devices  99.1 us (16%)
  matrix products  89.7 us (14%)
  local copies, waits for them, and re-layouts  77.1 us (12%)
  Pallas kernels  55.5 us (9%)
  other arithmetic  45.3 us (7%)
  between operations  17.3 us (3%)
    ppermute x12, waiting for transfers between devices, shift_by(): return lax.ppermute(value, 'x', [(i, (i + step) % 4) for i in range(4)])  67.4 us
    all_to_all x12, starting transfers between devices, exchange(): return lax.all_to_all(blocks, axes, 0, 0, tiled=True)  66.2 us
    ppermute x7, waiting for transfers between devices, swap(): return lax.ppermute(value, axis, [(0, 1), (1, 0)])  61.2 us
    all_to_all x12, waiting for transfers between devices, exchange(): return lax.all_to_all(blocks, axes, 0, 0, tiled=True)  55.8 us
    unnamed x209, local copies, waits for them, and re-layouts  44.7 us
    dot_general x10, matrix products, matmul_left(): lax.dot_general(left, right, (((0,), (0,)), ((), ())), preferred_element_...  35 us
    dot_general x9, matrix products, matmul_right(): lax.dot_general(left, right, (((1,), (1,)), ((), ())), preferred_element_...  31.5 us
    dot_general x10, matrix products, matmul(): return jnp.dot(left, right, preferred_element_type=wide)  23.1 us
  transfers between devices with their start and end apart: 45, of which 25 were waited for; matrix products, arithmetic and copies ran while one was open for 25% of the time, Pallas kernels for 8%

profile of v2, /device:TPU:1, one launch (start us, length us, event | category | flops | bytes accessed | tf_op | source)
XLA Modules:
  0.0 609.6 jit_solution(10218160559739485228)
XLA Ops:
  11.5 6.8 %all-to-all-start = ((s32[8,2,256]{2,1,0:T(2,128)}), s32[8,2,256]{2,1,0:T(2,128)S(1)}, u32[]{:S(2)}, u32[]{:S(2)}) async-start(s32[8,2,256]{2,1,0:T(2,128)} %broadcast_in_dim.137), calls=%async_computation | async-start | bytes 32768 | tf_op jit(solution)/shard_map/all_to_all | solution.py:85
  27.1 7.5 %project.1 = (bf16[8,256,384]{2,1,0:T(8,128)(2,1)}, bf16[256,1024]{1,0:T(8,128)(2,1)}) custom-call(bf16[256,1024]{1,0:T(8,128)(2,1)S(1)} %copy-done.8, bf16[1,1024]{1,0:T(2,128)(2,1)S(1)} %reshape.381.gain_ref, bf16[1,1024]{1,0:T(2,128)(2,1)S(1)} %reshape.382.shift_ref, bf16[1024,1024]{1,0:T(8,128)(2,1)S(1)} %copy-done.2, bf16[1024,1024]{1,0:T(8,128)(2,1)S(1)} %copy-done.5, ...), custom_call_target="tpu_custom_call" | custom-call | tf_op jit(solution)/shard_map/project/pallas_call | solution.py:140
  44.4 16.0 %all-to-all-done.1.qkv_ref = bf16[8,256,384]{2,1,0:T(8,128)(2,1)S(1)} async-done(((bf16[8,256,384]{2,1,0:T(8,128)(2,1)}), bf16[8,256,384]{2,1,0:T(8,128)(2,1)S(1)}, u32[]{:S(2)}, u32[]{:S(2)}) %all-to-all-start.1) | async-done | bytes 1572896 | tf_op jit(solution)/shard_map/all_to_all | solution.py:85
  68.3 15.7 %attend.1 = (bf16[8,256,128]{2,1,0:T(8,128)(2,1)}, f32[8,128,256]{2,1,0:T(8,128)S(1)}, f32[8,8,256]{2,1,0:T(8,128)S(1)}) custom-call(s32[8]{0:T(128)S(1)} %convert_reduce_fusion.6.low_ref, bf16[8,256,384]{2,1,0:T(8,128)(2,1)S(1)} %all-to-all-done.1.qkv_ref, s32[8,256,1]{2,1,0:T(8,128)S(1)} %copy.70.segcol_ref, s32[8,1,256]{2,1,0:T(1,128)S(1)} %get-tuple-element.302.segrow_ref), custom_call_target="tpu_custom_call" | custom-call | tf_op jit(solution)/shard_map/attend/pallas_call | solution.py:269
  94.6 8.7 %all-to-all-done.3.ctx_ref = bf16[8,256,128]{2,1,0:T(8,128)(2,1)S(1)} async-done(((bf16[8,256,128]{2,1,0:T(8,128)(2,1)}), bf16[8,256,128]{2,1,0:T(8,128)(2,1)S(1)}, u32[]{:S(2)}, u32[]{:S(2)}) %all-to-all-start.3) | async-done | bytes 524320 | tf_op jit(solution)/shard_map/all_to_all | solution.py:85
  118.2 8.9 %all-to-all-done.4 = bf16[8,48,1024]{2,1,0:T(8,128)(2,1)S(1)} async-done(((bf16[8,48,1024]{2,1,0:T(8,128)(2,1)}), bf16[8,48,1024]{2,1,0:T(8,128)(2,1)S(1)}, u32[]{:S(2)}, u32[]{:S(2)}) %all-to-all-start.4) | async-done | bytes 786464 | tf_op jit(solution)/shard_map/all_to_all | solution.py:85
  135.0 11.6 %collective-permute-done = bf16[256,1024]{1,0:T(8,128)(2,1)} collective-permute-done((bf16[256,1024]{1,0:T(8,128)(2,1)}, bf16[256,1024]{1,0:T(8,128)(2,1)}, u32[]{:S(2)}, u32[]{:S(2)}) %collective-permute-start) | collective-permute-done | bytes 524320 | tf_op jit(solution)/shard_map/ppermute | solution.py:55
  170.4 13.6 %all-gather.22.cloned.1.call-done = bf16[1,1024,1024]{2,1,0:T(8,128)(2,1)} async-done(((bf16[1,256,1024]{2,1,0:T(8,128)(2,1)}), bf16[1,1024,1024]{2,1,0:T(8,128)(2,1)}) %all-gather.22.cloned.1.call-update) | async-done | bytes 2097168 | tf_op jit(solution)/shard_map/all_gather | solution.py:447
  198.7 8.7 %collective-permute-done.3 = bf16[256,1024]{1,0:T(8,128)(2,1)} collective-permute-done((bf16[256,1024]{1,0:T(8,128)(2,1)}, bf16[256,1024]{1,0:T(8,128)(2,1)}, u32[]{:S(2)}, u32[]{:S(2)}) %collective-permute-start.3) | collective-permute-done | bytes 524320 | tf_op jit(solution)/shard_map/ppermute | solution.py:59
  207.5 9.4 %collective-permute-done.5 = bf16[256,1024]{1,0:T(8,128)(2,1)} collective-permute-done((bf16[256,1024]{1,0:T(8,128)(2,1)}, bf16[256,1024]{1,0:T(8,128)(2,1)}, u32[]{:S(2)}, u32[]{:S(2)}) %collective-permute-start.5) | collective-permute-done | bytes 524320 | tf_op jit(solution)/shard_map/ppermute | solution.py:59
  228.1 8.6 %collective-permute-done.6 = bf16[256,1024]{1,0:T(8,128)(2,1)} collective-permute-done((bf16[256,1024]{1,0:T(8,128)(2,1)}, bf16[256,1024]{1,0:T(8,128)(2,1)}, u32[]{:S(2)}, u32[]{:S(2)}) %collective-permute-start.6) | collective-permute-done | bytes 524320 | tf_op jit(solution)/shard_map/ppermute | solution.py:59
  237.0 11.2 %collective-permute-done.8 = bf16[256,1024]{1,0:T(8,128)(2,1)} collective-permute-done((bf16[256,1024]{1,0:T(8,128)(2,1)}, bf16[256,1024]{1,0:T(8,128)(2,1)}, u32[]{:S(2)}, u32[]{:S(2)}) %collective-permute-start.8) | collective-permute-done | bytes 524320 | tf_op jit(solution)/shard_map/ppermute | solution.py:59
  248.2 7.1 %multiply_convert_fusion = (bf16[1024,1024]{1,0:T(8,128)(2,1)}, f32[1024,1024]{1,0:T(8,128)}) fusion(f32[1024]{0:T(1024)S(1)} %bitcast.186, bf16[1024,1024]{0,1:T(8,128)(2,1)} %all-gather.18.cloned.1.call-done, bf16[256,1024]{1,0:T(8,128)(2,1)} %collective-permute-done.8, bf16[256,1024]{1,0:T(8,128)(2,1)} %collective-permute-done.7, ...), kind=kOutput, calls=%fused_computation.8 | convolution fusion | flops 2162163712 | bytes 10489856 | tf_op jit(solution)/shard_map/dot_general | solution.py:31
  292.6 12.2 %collective-permute-done.11 = bf16[256,1024]{1,0:T(8,128)(2,1)} collective-permute-done((bf16[256,1024]{1,0:T(8,128)(2,1)}, bf16[256,1024]{1,0:T(8,128)(2,1)}, u32[]{:S(2)}, u32[]{:S(2)}) %collective-permute-start.11) | collective-permute-done | bytes 524320 | tf_op jit(solution)/shard_map/ppermute | solution.py:59
  313.8 14.2 %collective-permute-done.12 = bf16[256,1024]{1,0:T(8,128)(2,1)S(1)} collective-permute-done((bf16[256,1024]{1,0:T(8,128)(2,1)S(1)}, bf16[256,1024]{1,0:T(8,128)(2,1)S(1)}, u32[]{:S(2)}, u32[]{:S(2)}) %collective-permute-start.12) | collective-permute-done | bytes 524320 | tf_op jit(solution)/shard_map/ppermute | solution.py:55
  358.8 8.3 %collective-permute-done.16 = bf16[256,1024]{1,0:T(8,128)(2,1)} collective-permute-done((bf16[256,1024]{1,0:T(8,128)(2,1)}, bf16[256,1024]{1,0:T(8,128)(2,1)}, u32[]{:S(2)}, u32[]{:S(2)}) %collective-permute-start.16) | collective-permute-done | bytes 524320 | tf_op jit(solution)/shard_map/ppermute | solution.py:59
  376.8 10.2 %all-to-all-start.6 = ((bf16[8,48,1024]{2,1,0:T(8,128)(2,1)}), bf16[8,48,1024]{2,1,0:T(8,128)(2,1)S(1)}, u32[]{:S(2)}, u32[]{:S(2)}) async-start(bf16[8,48,1024]{2,1,0:T(8,128)(2,1)} %bitcast.160), calls=%async_computation.6 | async-start | bytes 1572864 | tf_op jit(solution)/shard_map/all_to_all | solution.py:85
  443.7 18.8 %attend_back.1 = (bf16[8,256,384]{2,1,0:T(8,128)(2,1)}, bf16[16,192,128]{2,1,0:T(8,128)(2,1)S(1)}, f32[1,384]{1,0:T(1,128)S(1)}) custom-call(s32[8]{0:T(128)S(1)} %convert_reduce_fusion.6.low_ref, bf16[8,256,384]{2,1,0:T(8,128)(2,1)S(1)} %all-to-all-done.1.qkv_ref, bf16[8,256,128]{2,1,0:T(8,128)(2,1)S(1)} %all-to-all-done.7.grad_ref, ...), custom_call_target="tpu_custom_call" | custom-call | tf_op jit(solution)/shard_map/attend_back/pallas_call | solution.py:348
  473.1 23.8 %collective-permute-done.17 = bf16[256,1024]{1,0:T(8,128)(2,1)S(1)} collective-permute-done((bf16[256,1024]{1,0:T(8,128)(2,1)S(1)}, bf16[256,1024]{1,0:T(8,128)(2,1)S(1)}, u32[]{:S(2)}, u32[]{:S(2)}) %collective-permute-start.17) | collective-permute-done | bytes 524320 | tf_op jit(solution)/shard_map/ppermute | solution.py:55
  496.9 7.4 %reduce-scatter.17.cloned.1.call-done = bf16[256,1024]{1,0:T(8,128)(2,1)} async-done(((bf16[1024,1024]{1,0:T(8,128)(2,1)}), bf16[256,1024]{1,0:T(8,128)(2,1)}) %reduce-scatter.17.cloned.1.call-update) | async-done | bytes 524304 | tf_op jit(solution)/shard_map/reduce_scatter | solution.py:444
  513.9 11.4 %all-to-all-done.11 = bf16[8,48,1024]{2,1,0:T(8,128)(2,1)S(1)} async-done(((bf16[8,48,1024]{2,1,0:T(8,128)(2,1)}), bf16[8,48,1024]{2,1,0:T(8,128)(2,1)S(1)}, u32[]{:S(2)}, u32[]{:S(2)}) %all-to-all-start.11) | async-done | bytes 786464 | tf_op jit(solution)/shard_map/all_to_all | solution.py:85
  542.7 11.1 %collective-permute-done.18 = bf16[256,1024]{1,0:T(8,128)(2,1)} collective-permute-done((bf16[256,1024]{1,0:T(8,128)(2,1)}, bf16[256,1024]{1,0:T(8,128)(2,1)}, u32[]{:S(2)}, u32[]{:S(2)}) %collective-permute-start.18) | collective-permute-done | bytes 524320 | tf_op jit(solution)/shard_map/ppermute | solution.py:55
  570.0 12.0 %all-gather.26.cloned.1.call-done = bf16[33792,128]{1,0:T(8,128)(2,1)} async-done(((bf16[264,128]{1,0:T(8,128)(2,1)}), bf16[33792,128]{1,0:T(8,128)(2,1)}) %all-gather.26.cloned.1.call-update) | async-done | bytes 8650768 | tf_op jit(solution)/shard_map/all_gather | solution.py:633
  589.9 8.7 %unpack.1 = (f32[1024,1024]{1,0:T(8,128)}, f32[1024,1024]{1,0:T(8,128)}, f32[1024,1024]{1,0:T(8,128)}, f32[8,16,8,1024]{3,2,1,0:T(8,128)}, f32[16,64,2]{2,1,0:T(8,128)S(1)}) custom-call(bf16[16,8,264,128]{3,2,1,0:T(8,128)(2,1)S(1)} %bitcast.143, f32[3,1024]{1,0:T(4,128)S(1)} %bitcast.146, bf16[16,64,1]{2,1,0:T(8,128)(2,1)S(1)} %reshape.417.gain_ref, ...), custom_call_target="tpu_custom_call" | custom-call | tf_op jit(solution)/shard_map/unpack/pallas_call | solution.py:398
  (461 shorter events, 320.5 us)
Async XLA Ops:
  8.0 147.7 %all-gather.12.cloned.1.call-start = ((), (), s32[]{:S(2)}) async-start(), calls=%async_computation.18 | async-start | bytes 2621440 | tf_op jit(solution)/shard_map/all_gather | solution.py:447
  11.5 23.1 %all-to-all-start = ((s32[8,2,256]{2,1,0:T(2,128)}), s32[8,2,256]{2,1,0:T(2,128)S(1)}, u32[]{:S(2)}, u32[]{:S(2)}) async-start(s32[8,2,256]{2,1,0:T(2,128)} %broadcast_in_dim.137), calls=%async_computation | async-start | bytes 32768 | tf_op jit(solution)/shard_map/all_to_all | solution.py:85
  34.7 25.7 %all-to-all-start.1 = ((bf16[8,256,384]{2,1,0:T(8,128)(2,1)}), bf16[8,256,384]{2,1,0:T(8,128)(2,1)S(1)}, u32[]{:S(2)}, u32[]{:S(2)}) async-start(bf16[8,256,384]{2,1,0:T(8,128)(2,1)} %get-tuple-element.105), calls=%async_computation.1 | async-start | bytes 3145728 | tf_op jit(solution)/shard_map/all_to_all | solution.py:85
  40.6 44.4 %collective-permute-start.1 = (bf16[512,1024]{1,0:T(8,128)(2,1)}, bf16[512,1024]{1,0:T(8,128)(2,1)}, u32[]{:S(2)}, u32[]{:S(2)}) collective-permute-start(bf16[512,1024]{1,0:T(8,128)(2,1)} %pad_maximum_fusion.4), channel_id=1, source_target_pairs={{0,16},{16,0},{1,17},{17,1},{2,18},{18,2},{3,19},{19,3},{4,20},{20... | collective-permute-start | bytes 3145736 | tf_op jit(solution)/shard_map/ppermute | solution.py:55
  61.0 24.0 %all-to-all-start.2 = ((bf16[16,8,128]{2,1,0:T(8,128)(2,1)}), bf16[16,8,128]{2,1,0:T(8,128)(2,1)S(1)}, u32[]{:S(2)}, u32[]{:S(2)}) async-start(bf16[16,8,128]{2,1,0:T(8,128)(2,1)} %broadcast_in_dim.139), calls=%async_computation.2 | async-start | bytes 65536 | tf_op jit(solution)/shard_map/all_to_all | solution.py:85
  67.7 93.0 %all-gather.14.cloned.1.call-start = ((), (), s32[]{:S(2)}) async-start(), calls=%async_computation.19 | async-start | bytes 2621440 | tf_op jit(solution)/shard_map/all_gather | solution.py:447
  87.3 78.6 %all-gather.16.cloned.1.call-start = ((), (), s32[]{:S(2)}) async-start(), calls=%async_computation.20 | async-start | bytes 2621440 | tf_op jit(solution)/shard_map/all_gather | solution.py:447
  88.0 95.9 %all-gather.22.cloned.1.call-start = ((), (), s32[]{:S(2)}) async-start(), calls=%async_computation.29 | async-start | bytes 2621440 | tf_op jit(solution)/shard_map/all_gather | solution.py:447
  88.6 139.5 %all-gather.18.cloned.1.call-start = ((), (), s32[]{:S(2)}) async-start(), calls=%async_computation.21 | async-start | bytes 2621440 | tf_op jit(solution)/shard_map/all_gather | solution.py:447
  114.9 145.2 %all-gather.20.cloned.1.call-start = ((), (), s32[]{:S(2)}) async-start(), calls=%async_computation.22 | async-start | bytes 2621440 | tf_op jit(solution)/shard_map/all_gather | solution.py:447
  150.2 38.9 %all-to-all-start.5 = ((bf16[8,48,1024]{2,1,0:T(8,128)(2,1)}), bf16[8,48,1024]{2,1,0:T(8,128)(2,1)}, u32[]{:S(2)}, u32[]{:S(2)}) async-start(bf16[8,48,1024]{2,1,0:T(8,128)(2,1)} %bitcast.152), calls=%async_computation.5 | async-start | bytes 1572864 | tf_op jit(solution)/shard_map/all_to_all | solution.py:85
  155.8 243.5 %reduce-scatter.7.cloned.1.call-start = ((), (), s32[]{:S(2)}) async-start(), calls=%async_computation.23 | async-start | bytes 2621440 | tf_op jit(solution)/shard_map/reduce_scatter | solution.py:444
  279.5 25.3 %collective-permute-start.11 = (bf16[256,1024]{1,0:T(8,128)(2,1)}, bf16[256,1024]{1,0:T(8,128)(2,1)}, u32[]{:S(2)}, u32[]{:S(2)}) collective-permute-start(bf16[256,1024]{1,0:T(8,128)(2,1)} %get-tuple-element.283), channel_id=1, source_target_pairs={{0,64},{32,96},{64,0},{96,32},{1,65},{33,97},{65,1},{97,33},{2,66}... | collective-permute-start | bytes 1572872 | tf_op jit(solution)/shard_map/ppermute | solution.py:59
  304.8 94.4 %reduce-scatter.9.cloned.1.call-start = ((), (), s32[]{:S(2)}) async-start(), calls=%async_computation.24 | async-start | bytes 2621440 | tf_op jit(solution)/shard_map/reduce_scatter | solution.py:444
  305.6 126.8 %all-gather.24.cloned.1.call-start = ((), (), s32[]{:S(2)}) async-start(), calls=%async_computation.30 | async-start | bytes 4718592 | tf_op jit(solution)/shard_map/all_gather | solution.py:505
  306.1 132.9 %reduce-scatter.11.cloned.1.call-start = ((), (), s32[]{:S(2)}) async-start(), calls=%async_computation.25 | async-start | bytes 2621440 | tf_op jit(solution)/shard_map/reduce_scatter | solution.py:444
  367.1 71.9 %reduce-scatter.13.cloned.1.call-start = ((), (), s32[]{:S(2)}) async-start(), calls=%async_computation.26 | async-start | bytes 2621440 | tf_op jit(solution)/shard_map/reduce_scatter | solution.py:444
  386.9 109.9 %reduce-scatter.15.cloned.1.call-start = ((), (), s32[]{:S(2)}) async-start(), calls=%async_computation.27 | async-start | bytes 2621440 | tf_op jit(solution)/shard_map/reduce_scatter | solution.py:444
  399.3 105.0 %reduce-scatter.17.cloned.1.call-start = ((), (), s32[]{:S(2)}) async-start(), calls=%async_computation.28 | async-start | bytes 2621440 | tf_op jit(solution)/shard_map/reduce_scatter | solution.py:444
  423.8 38.8 %all-to-all-start.8 = ((bf16[8,128,1024]{2,1,0:T(8,128)(2,1)}), bf16[8,128,1024]{2,1,0:T(8,128)(2,1)}, u32[]{:S(2)}, u32[]{:S(2)}) async-start(bf16[8,128,1024]{2,1,0:T(8,128)(2,1)} %bitcast.148), calls=%async_computation.12 | async-start | bytes 4194304 | tf_op jit(solution)/shard_map/all_to_all | solution.py:85
  465.8 31.1 %all-to-all-start.9 = ((bf16[16,272,128]{2,1,0:T(8,128)(2,1)}), bf16[16,272,128]{2,1,0:T(8,128)(2,1)S(1)}, u32[]{:S(2)}, u32[]{:S(2)}) async-start(bf16[16,272,128]{2,1,0:T(8,128)(2,1)} %pad_maximum_fusion.2), calls=%async_computation.13 | async-start | bytes 2228224 | tf_op jit(solution)/shard_map/all_to_all | solution.py:85
  470.1 112.0 %all-gather.26.cloned.1.call-start = ((), (), s32[]{:S(2)}) async-start(), calls=%async_computation.31 | async-start | bytes 8718336 | tf_op jit(solution)/shard_map/all_gather | solution.py:633
  470.1 26.7 %collective-permute-start.17 = (bf16[256,1024]{1,0:T(8,128)(2,1)S(1)}, bf16[256,1024]{1,0:T(8,128)(2,1)S(1)}, u32[]{:S(2)}, u32[]{:S(2)}) collective-permute-start(bf16[256,1024]{1,0:T(8,128)(2,1)S(1)} %copy-done.90), channel_id=1, source_target_pairs={{0,16},{16,0},{1,17},{17,1},{2,18},{18,2},{3,19},{19,3},{4,20},{20... | collective-permute-start | bytes 1572872 | tf_op jit(solution)/shard_map/ppermute | solution.py:55
  526.2 28.2 %all-to-all-start.10 = ((bf16[8,256,384]{2,1,0:T(8,128)(2,1)}), bf16[8,256,384]{2,1,0:T(8,128)(2,1)S(1)}, u32[]{:S(2)}, u32[]{:S(2)}) async-start(bf16[8,256,384]{2,1,0:T(8,128)(2,1)} %get-tuple-element.165), calls=%async_computation.16 | async-start | bytes 3145728 | tf_op jit(solution)/shard_map/all_to_all | solution.py:85
  (118 other events, 1175.9 us)
Sparse Core Ops, SparseCore 0:
  11.1 34.0 all-gather.11
  87.4 30.9 all-gather.13
  120.7 30.8 all-gather.15
  153.1 30.8 all-gather.21
  185.4 40.7 all-gather.17
  227.8 32.1 all-gather.19
  304.9 37.1 reduce-scatter.6
  344.7 29.8 reduce-scatter.8
  377.0 29.3 reduce-scatter.10
  408.8 29.3 reduce-scatter.12
  441.2 29.3 reduce-scatter.14
  473.6 30.6 reduce-scatter.16
Sparse Core Ops, SparseCore 1:
  308.3 33.1 all-gather.23
  505.2 76.8 all-gather.25

commit v3 on v2

--- a/solution.py
+++ b/solution.py
@@ -56,20 +56,15 @@
 
 
 def shift_by(value, step):
-    return lax.ppermute(value, "x", [(i, (i + step) % 4) for i in range(4)])
-
-
-def share_two(rows):
-    return jnp.concatenate([rows, swap(rows, "y2")], 0)
+    return lax.ppermute(value, COLUMN, [(i, (i + step) % 4) for i in range(4)])
 
 
 def share_four(rows):
-    return jnp.concatenate([rows] + [shift_by(rows, step) for step in (1, 3, 2)], 0)
-
-
-def return_four(partial):
-    _, back, ahead, away = jnp.split(partial, 4, 0)
-    return shift_by(back, 3), shift_by(ahead, 1), shift_by(away, 2)
+    return [rows] + [shift_by(rows, step) for step in (1, 3, 2)]
+
+
+def return_four(parts):
+    return [shift_by(part, step) for part, step in zip(parts[1:], (3, 1, 2))]
 
 
 def total(own, got):
@@ -111,6 +106,194 @@
             lax.broadcasted_iota(jnp.int32, size, 0) <= lax.broadcasted_iota(jnp.int32, size, 1)
         )
     return same
+
+
+EXPAND = pl.BlockSpec((1, 256, 1024), lambda k: (k, 0, 0))
+SHRINK = pl.BlockSpec((1, 256, 1024), lambda k: (k, 1, 0))
+COLUMNS = pl.BlockSpec((256, 256), lambda k: (0, k))
+WHOLE = pl.BlockSpec((256, 1024), lambda k: (0, 0))
+LINE = pl.BlockSpec((1, 1024), lambda k: (0, 0))
+LIFT = pl.BlockSpec((1, 256), lambda k: (0, k))
+
+
+def first_step(run):
+    pl.when(pl.program_id(0) == 0)(run)
+
+
+def add_up(acc_ref, part_ref, part):
+    k = pl.program_id(0)
+
+    @first_step
+    def _():
+        acc_ref[...] = part
+
+    @pl.when(k > 0)
+    def _():
+        acc_ref[...] += part
+
+    @pl.when(k == pl.num_programs(0) - 1)
+    def _():
+        part_ref[...] = acc_ref[...].astype(part_ref.dtype)
+
+
+def expert_call(kernel, name, in_specs, out_specs, outs, kept, accs, *args):
+    return pl.pallas_call(
+        kernel,
+        grid=(4,),
+        out_shape=[
+            pltpu.HBM((256, 1024), dtype) if i < kept else jax.ShapeDtypeStruct((256, 1024), dtype)
+            for i, dtype in enumerate(outs)
+        ],
+        in_specs=in_specs,
+        out_specs=out_specs,
+        scratch_shapes=[pltpu.VMEM((256, 1024), wide)] * accs,
+        compiler_params=pltpu.CompilerParams(vmem_limit_bytes=16 << 20),
+        name=name,
+    )(*args)
+
+
+def front_forward_kernel(
+    xhat_ref, gain_ref, shift_ref, lift_a_ref, lift_b_ref,
+    expand_a_ref, shrink_a_ref, expand_b_ref, shrink_b_ref,
+    act_a_ref, act_b_ref, slope_a_ref, slope_b_ref, rows_ref, part_ref, acc_ref,
+):
+    @first_step
+    def _():
+        rows = xhat_ref[...].astype(wide) * gain_ref[...] + shift_ref[...]
+        rows_ref[...] = rows.astype(narrow)
+
+    part = 0.0
+    for lift_ref, expand_ref, shrink_ref, act_ref, slope_ref in (
+        (lift_a_ref, expand_a_ref, shrink_a_ref, act_a_ref, slope_a_ref),
+        (lift_b_ref, expand_b_ref, shrink_b_ref, act_b_ref, slope_b_ref),
+    ):
+        act, slope = gelu_pair(matmul_right(rows_ref[...], expand_ref[0]) + lift_ref[...])
+        act = act.astype(narrow)
+        act_ref[...] = act
+        slope_ref[...] = slope
+        part = part + matmul(act, shrink_ref[0])
+    add_up(acc_ref, part_ref, part)
+
+
+def front_forward(xhat, gain, shift, lifts, mats, last):
+    return expert_call(
+        front_forward_kernel, "front_forward",
+        [WHOLE, LINE, LINE, LIFT, LIFT, EXPAND, SHRINK, EXPAND, SHRINK],
+        [COLUMNS] * 4 + [WHOLE] * 2, [narrow, narrow, wide, wide, narrow, last], 5, 1,
+        xhat, gain, shift, lifts[0], lifts[1], mats[0], mats[0], mats[1], mats[1],
+    )
+
+
+def front_backward_kernel(
+    rows_ref, slope_a_ref, slope_b_ref, expand_a_ref, shrink_a_ref, expand_b_ref, shrink_b_ref,
+    grad_a_ref, grad_b_ref, part_ref, acc_ref,
+):
+    part = 0.0
+    for slope_ref, expand_ref, shrink_ref, grad_ref in (
+        (slope_a_ref, expand_a_ref, shrink_a_ref, grad_a_ref),
+        (slope_b_ref, expand_b_ref, shrink_b_ref, grad_b_ref),
+    ):
+        grad = (slope_ref[...] * matmul_right(rows_ref[...], shrink_ref[0])).astype(narrow)
+        grad_ref[...] = grad
+        part = part + matmul(grad, expand_ref[0])
+    add_up(acc_ref, part_ref, part)
+
+
+def front_backward(rows, slopes, mats, last):
+    return expert_call(
+        front_backward_kernel, "front_backward",
+        [WHOLE, COLUMNS, COLUMNS, EXPAND, SHRINK, EXPAND, SHRINK],
+        [COLUMNS] * 2 + [WHOLE], [narrow, narrow, last], 2, 1,
+        rows, pinned(slopes[0]), pinned(slopes[1]), mats[0], mats[0], mats[1], mats[1],
+    )
+
+
+def back_kernel(
+    rows_ref, branch_ref, lift_ref, expand_ref, shrink_ref,
+    act_ref, grad_ref, part_ref, out_ref, part_acc_ref, out_acc_ref,
+):
+    act, slope = gelu_pair(matmul_right(rows_ref[...], expand_ref[0]) + lift_ref[...])
+    act = act.astype(narrow)
+    act_ref[...] = act
+    grad = (slope * matmul_right(branch_ref[...], shrink_ref[0])).astype(narrow)
+    grad_ref[...] = grad
+    add_up(part_acc_ref, part_ref, matmul(grad, expand_ref[0]))
+    add_up(out_acc_ref, out_ref, matmul(act, shrink_ref[0]))
+
+
+def back_both(rows, branch, lift, mats, last):
+    return expert_call(
+        back_kernel, "back_both", [WHOLE, WHOLE, LIFT, EXPAND, SHRINK],
+        [COLUMNS] * 2 + [WHOLE] * 2, [narrow, narrow, last, last], 2, 2,
+        rows, branch, lift, mats, mats,
+    )
+
+
+def mat_grads_kernel(count, sides, *refs):
+    lefts, rights, out_ref = refs[: count * sides], refs[count * sides : -2], refs[-2]
+    for side in range(sides):
+        side_lefts = [lefts[side * count + i][...] for i in range(count)]
+        part = sum(matmul_left(left, right[...]) for left, right in zip(side_lefts, rights))
+        out_ref[0, side] = part.astype(narrow)
+        line = sum(jnp.sum(left.astype(wide), 0, keepdims=True) for left in side_lefts)
+        refs[-1][0, side] = jnp.broadcast_to(line, (8, 256))
+
+
+def mat_grads(lefts, rights):
+    count, sides = len(rights), len(lefts)
+    return pl.pallas_call(
+        lambda *refs: mat_grads_kernel(count, sides, *refs),
+        grid=(4,),
+        out_shape=(
+            pltpu.HBM((4, sides, 256, 1024), narrow),
+            jax.ShapeDtypeStruct((4, sides, 8, 256), wide),
+        ),
+        in_specs=[COLUMNS] * (count * sides) + [WHOLE] * count,
+        out_specs=(
+            pl.BlockSpec((1, sides, 256, 1024), lambda k: (k, 0, 0, 0)),
+            pl.BlockSpec((1, sides, 8, 256), lambda k: (k, 0, 0, 0)),
+        ),
+        compiler_params=pltpu.CompilerParams(vmem_limit_bytes=14 << 20),
+        name="mat_grads",
+    )(*(pinned(part) for side in lefts for part in side), *rights)
+
+
+def sums_kernel(
+    front_grad_ref, front_xhat_ref, front_branch_ref, back_grad_ref, back_xhat_ref, back_branch_ref,
+    logit_grad_ref, stream_ref, out_ref,
+):
+    front_grad, back_grad = front_grad_ref[...], back_grad_ref[...]
+    lines = (
+        front_grad * front_xhat_ref[...], front_grad, front_branch_ref[...].astype(wide),
+        back_grad * back_xhat_ref[...], back_grad, back_branch_ref[...].astype(wide),
+        logit_grad_ref[...] * stream_ref[...],
+    )
+    for i, line in enumerate(lines):
+        out_ref[i : i + 1, :] = jnp.sum(line, 0, keepdims=True)
+    out_ref[7:8, :] = jnp.zeros_like(out_ref[7:8, :])
+
+
+def row_sums(*args):
+    return pl.pallas_call(
+        sums_kernel,
+        out_shape=jax.ShapeDtypeStruct((8, 1024), wide),
+        compiler_params=pltpu.CompilerParams(vmem_limit_bytes=12 << 20),
+        name="row_sums",
+    )(*args)
+
+
+def turn_kernel(in_ref, out_ref):
+    out_ref[...] = turn(in_ref[...])
+
+
+def turned(matrix):
+    return pl.pallas_call(
+        turn_kernel, out_shape=jax.ShapeDtypeStruct(matrix.shape[::-1], matrix.dtype), name="turned"
+    )(matrix)
+
+
+def pinned(value):
+    return pltpu.with_memory_space_constraint(value, pltpu.HBM)
 
 
 def project_kernel(
@@ -147,9 +330,9 @@
         in_specs=[all_rows, line, line, mat, mat, mat, bias, bias],
         out_specs=(pl.BlockSpec((1, rows, 384), lambda e: (e, 0, 0)), all_rows),
         scratch_shapes=[pltpu.VMEM((rows, width), narrow)],
-        compiler_params=pltpu.CompilerParams(vmem_limit_bytes=32 << 20),
+        compiler_params=pltpu.CompilerParams(vmem_limit_bytes=8 << 20),
         name="project",
-    )(tokens, gain, shift, querymat, keymat, valuemat, querybias, valuebias)
+    )(tokens, gain, shift, pinned(querymat), pinned(keymat), pinned(valuemat), querybias, valuebias)
 
 
 def join_kernel(ctx_ref, outmat_ref, tokens_ref, bias_ref, sender_ref, hidden_ref, packed_ref, context_ref):
@@ -182,7 +365,7 @@
             pl.BlockSpec((slots, rows), lambda n: (0, 0)),
         ],
         out_specs=(strip(rows), strip(slots), pl.BlockSpec((rows, width), lambda n: (0, 0))),
-        compiler_params=pltpu.CompilerParams(vmem_limit_bytes=32 << 20),
+        compiler_params=pltpu.CompilerParams(vmem_limit_bytes=10 << 20),
         name="join",
     )(ctx, outmat, tokens, outbias, sender)
 
@@ -218,7 +401,7 @@
             pl.BlockSpec((256, width), lambda e: (e, 0)),
         ],
         out_specs=(all_rows, pl.BlockSpec((2, rows, 128), lambda e: (e, 0, 0)), all_rows),
-        compiler_params=pltpu.CompilerParams(vmem_limit_bytes=32 << 20),
+        compiler_params=pltpu.CompilerParams(vmem_limit_bytes=12 << 20),
         name="hidden_back",
     )(blocks, getter, cotangent, outmat)
 
@@ -276,15 +459,17 @@
         in_specs=[pl.BlockSpec(memory_space=pltpu.SMEM), vmem, vmem, vmem],
         out_specs=(vmem, vmem, vmem),
         scratch_shapes=[pltpu.VMEM((blocks, 2, 80, size), narrow)],
-        compiler_params=pltpu.CompilerParams(vmem_limit_bytes=40 << 20),
+        compiler_params=pltpu.CompilerParams(vmem_limit_bytes=12 << 20),
         name="attend",
     )(low, qkv, segcol, segrow)
 
 
 def attend_back_kernel(
     low_ref, qkv_ref, grad_ref, full_ref, lse_ref, segcol_ref, segrow_ref, xhat_ref,
-    out_ref, three_ref, sums_ref, keys_ref, dk_ref, dv_ref,
+    out_ref, three_ref, sums_ref, keys_ref, dk_ref, dv_ref, held_ref, sem_ref,
 ):
+    fetch = pltpu.make_async_copy(xhat_ref, held_ref, sem_ref)
+    fetch.start()
     blocks, size, _ = qkv_ref.shape
     for j in range(blocks):
         keys_ref[j] = turn(qkv_ref[j, :, 128:256])
@@ -331,9 +516,10 @@
     for j in range(blocks):
         out_ref[j, :, 128:256] = dk_ref[j].astype(narrow)
         out_ref[j, :, 256:384] = dv_ref[j].astype(narrow)
+    fetch.wait()
     for part in range(4):
         height = slice(part * 256, part * 256 + 256)
-        three = sum(matmul(xhat_ref[j, height, :], out_ref[j]) for j in range(blocks))
+        three = sum(matmul(held_ref[j, height, :], out_ref[j]) for j in range(blocks))
         for d in range(4):
             for i in range(3):
                 three_ref[part * 4 + d, i * 64 : i * 64 + 64, :] = three[
@@ -352,14 +538,18 @@
             jax.ShapeDtypeStruct((16, 192, 128), narrow),
             jax.ShapeDtypeStruct((1, 384), wide),
         ),
-        in_specs=[pl.BlockSpec(memory_space=pltpu.SMEM)] + [vmem] * 7,
+        in_specs=[pl.BlockSpec(memory_space=pltpu.SMEM)]
+        + [vmem] * 6
+        + [pl.BlockSpec(memory_space=pltpu.HBM)],
         out_specs=(vmem, vmem, vmem),
         scratch_shapes=[
             pltpu.VMEM((blocks, 128, size), narrow),
             pltpu.VMEM((blocks, size, 128), wide),
             pltpu.VMEM((blocks, size, 128), wide),
+            pltpu.VMEM(xhat.shape, narrow),
+            pltpu.SemaphoreType.DMA,
         ],
-        compiler_params=pltpu.CompilerParams(vmem_limit_bytes=40 << 20),
+        compiler_params=pltpu.CompilerParams(vmem_limit_bytes=20 << 20),
         name="attend_back",
     )(low, qkv, grad, full, lse, segcol, segrow, xhat)
 
@@ -413,7 +603,7 @@
             pl.BlockSpec((8, step, 8, width), lambda d: (0, d, 0, 0)),
             pl.BlockSpec((step, 64, 2), lambda d: (d, 0, 0)),
         ),
-        compiler_params=pltpu.CompilerParams(vmem_limit_bytes=32 << 20),
+        compiler_params=pltpu.CompilerParams(vmem_limit_bytes=14 << 20),
         name="unpack",
     )(everything, biases, gain, shift, querymat, keymat, valuemat)
 
@@ -429,7 +619,7 @@
     capacity = rows // experts + rows // (2 * experts)
     slots = experts * capacity
     mine = lax.axis_index(GROUP)
-    x_at, y1_at, y2_at = (lax.axis_index(axis) for axis in DATA)
+    y1_at, y2_at, y_at = (lax.axis_index(axis) for axis in ("y1", "y2", COLUMN))
 
     plans = to_everyone(jnp.concatenate([segments, routes], 0), GROUP, experts)
     small_own = jnp.concatenate(
@@ -444,11 +634,11 @@
         return lax.psum_scatter(matrix, axes, scatter_dimension=0, tiled=True)
 
     def gathered(matrix, axes):
-        return lax.all_gather(matrix, axes, axis=0, tiled=True)
-
-    front_expand, front_shrink = frontexpand[0].T, frontreduce[0]
-    front_pair = swap(jnp.concatenate([front_expand, front_shrink], 0), "y1")
-    front_expands, front_shrinks = [gathered(front_expand, "x")], [gathered(front_shrink, "x")]
+        return lax.all_gather(matrix, axes, axis=0)
+
+    front_own = jnp.concatenate([frontexpand[0].T, frontreduce[0]], 0)
+    front_other = swap(front_own, "y1")
+    front_mats = [gathered(front_own, "x")]
 
     route = routes[0]
     picks = (route[:, None] == jnp.arange(experts)[None, :]).astype(narrow)
@@ -476,7 +666,12 @@
     split, plans = lax.optimization_barrier((split, plans))
     seg_all, route_all = plans[:, 0], plans[:, 1]
     qkv = exchange(split, GROUP)
+    xhat_turned = turned(xhat_low)
+    qkv, xhat_turned = lax.optimization_barrier((qkv, xhat_turned))
     small = to_everyone(after(qkv, small), DATA, 16)
+    front_other, back_own = after(qkv, front_other, jnp.concatenate([backexpand[0].T, backreduce[0]], 0))
+    front_mats.append(gathered(front_other, "x"))
+    back_mats = gathered(back_own, "x")
     counts = jnp.sum((route_all == mine).astype(jnp.int32), 1)
     ahead = jnp.arange(experts)[:, None] > jnp.arange(experts)[None, :]
     starts = jnp.sum(jnp.where(ahead, counts[None, :], 0), 1)
@@ -487,11 +682,7 @@
     segcol, segrow = seg_all[:, :, None], seg_all[:, None, :]
     low = jnp.sum((seg_all[None, :, -1] < seg_all[:, None, 0]).astype(jnp.int32), 1)
     ctx, full, lse = attend(low, qkv, segcol, segrow)
-    ctx, small = lax.optimization_barrier((ctx, small))
-    front_pair, back_expand, back_shrink = after(ctx, front_pair, backexpand[0].T, backreduce[0])
-    front_expands.append(gathered(front_pair[:256], "x"))
-    front_shrinks.append(gathered(front_pair[256:], "x"))
-    back_expand, back_shrink = gathered(back_expand, COLUMN), gathered(back_shrink, COLUMN)
+    ctx, small, front_mats[0] = lax.optimization_barrier((ctx, small, front_mats[0]))
     small = small.reshape(16, 1024).astype(wide)
     front_gain, front_shift, front_offset, back_gain, back_shift, back_offset, centre = (
         small[:, i * 64 : i * 64 + 64].reshape(1, width) for i in range(7)
@@ -500,88 +691,103 @@
     front_lift = lax.dynamic_index_in_dim(lifts, y2_at, 2, False)[:, :, :256]
     front_lift = jnp.where(y1_at == 0, front_lift, front_lift[:, ::-1])
     front_lift = jnp.transpose(front_lift, (1, 0, 2)).reshape(2, 1, 1024)
-    back_lift = lax.dynamic_index_in_dim(lifts, x_at, 0, False)[:, :, 256:].reshape(1, 1024)
+    back_lift = lax.dynamic_index_in_dim(lifts.reshape(4, 4, 512), y_at, 1, False)[:, 256:]
+    back_lift = back_lift.reshape(1, 1024)
     hidden, blocks, context = join(exchange(ctx, GROUP), outmat, tokens, line(outbias), sender)
-    xhat_all = lax.all_gather(after(blocks, xhat_low).T, GROUP, axis=0)
-
-    stream = unpack_rows(exchange(blocks.reshape(experts, capacity, width), GROUP)).astype(wide)
+
+    blocks = exchange(blocks.reshape(experts, capacity, width), GROUP)
+    stream = unpack_rows(blocks).astype(wide)
     front_xhat, front_inverse = norm_parts(stream)
-    front_normed = share_two((front_xhat * front_gain + front_shift).astype(narrow))
+    xhat_own = front_xhat.astype(narrow)
+    ct_blocks = exchange(pack(after(xhat_own, cotangent)), GROUP)
+    front_side = front_gain, front_shift, front_lift, [pinned(mats) for mats in front_mats]
+    *own_acts, own_slope_a, own_slope_b, front_normed, own_part = front_forward(
+        xhat_own, *front_side, wide
+    )
+    ct_blocks, own_part = lax.optimization_barrier((ct_blocks, own_part))
     gate = jax.nn.sigmoid(jnp.sum(stream * centre, -1, keepdims=True))
-    ct_blocks = exchange(pack(after(front_normed, cotangent)), GROUP)
-    front_acts, front_slopes = [], []
-    for expand, lift in zip(front_expands, front_lift):
-        act, slope = gelu_pair(matmul_right(front_normed, expand) + lift)
-        front_acts.append(act.astype(narrow))
-        front_slopes.append(slope)
-    front_part = sum(matmul(act, shrink) for act, shrink in zip(front_acts, front_shrinks))
-    front_part, ct_blocks = lax.optimization_barrier((front_part, ct_blocks))
     ct_rows = unpack_rows(ct_blocks).astype(wide)
     gated = gate * ct_rows
     back_branch = gated.astype(narrow)
-    front_got, back_branches = lax.optimization_barrier(
-        (swap(front_part[rows:].astype(narrow), "y2"), share_four(back_branch))
-    )
-    front_out = front_part[:rows] + front_got.astype(wide) + front_offset
+    xhat_got, back_branch, own_part = lax.optimization_barrier(
+        (swap(xhat_own, "y2"), back_branch, own_part)
+    )
+    back_branches = share_four(back_branch)
+    *got_acts, got_slope_a, got_slope_b, normed_got, got_part = front_forward(
+        xhat_got, *front_side, narrow
+    )
+    got_part, *back_branches = lax.optimization_barrier((got_part, *back_branches))
+    front_got = swap(got_part, "y2")
+    front_out = own_part + front_got.astype(wide) + front_offset
+    xhat_all = lax.all_gather(after(got_part, xhat_turned), GROUP, axis=0)
     middle = stream + front_out
     back_xhat, back_inverse = norm_parts(middle)
     back_normed = share_four((back_xhat * back_gain + back_shift).astype(narrow))
-    back_act, back_slope = gelu_pair(matmul_right(back_normed, back_expand) + back_lift)
-    back_act = back_act.astype(narrow)
-    back_pre_grad = (back_slope * matmul_right(back_branches, back_shrink)).astype(narrow)
-    back_part = matmul(back_pre_grad, back_expand).astype(narrow)
-    act_late, normed_late, back_pre_late = after(back_part, back_act, back_normed, back_pre_grad)
-    back_grads = [matmul_left(act_late, back_branches), matmul_left(back_pre_late, normed_late)]
-    back_grads = [part.astype(narrow) for part in back_grads]
-    *back_got, shrink_part, expand_part = lax.optimization_barrier(
-        (*return_four(back_part), *back_grads)
-    )
-    back_grads = [reduced(part, COLUMN) for part in (shrink_part, expand_part)]
-    back_norm_grad = total(back_part[:rows], back_got)
+    back_results = [
+        back_both(normed, branch, back_lift, back_mats, last)
+        for normed, branch, last in zip(back_normed, back_branches, (wide, narrow, narrow, narrow))
+    ]
+    back_acts, back_pre_grads, back_parts, out_parts = map(list, zip(*back_results))
+    back_late = after(back_parts[-1], *back_pre_grads)
+    expand_part, back_lifts = mat_grads([back_late], back_normed)
+    *back_got, expand_part, xhat_all = lax.optimization_barrier(
+        (*return_four(back_parts), expand_part, xhat_all)
+    )
+    expand_grad = reduced(expand_part, "x")
+    back_norm_grad = total(back_parts[0], back_got)
     middle_grad = norm_back(back_norm_grad * back_gain, back_xhat, back_inverse)
     front_branch = (gated + middle_grad).astype(narrow)
-    out_part = matmul(after(front_branch, back_act), back_shrink).astype(narrow)
-    branch_got, out_part = lax.optimization_barrier((swap(front_branch, "y2"), out_part))
-    front_branches = jnp.concatenate([front_branch, branch_got], 0)
-    front_pre_grads = [
-        (slope * matmul_right(front_branches, shrink)).astype(narrow)
-        for slope, shrink in zip(front_slopes, front_shrinks)
-    ]
-    front_part = sum(matmul(grad, expand) for grad, expand in zip(front_pre_grads, front_expands))
-    front_low = front_part[rows:].astype(narrow)
-    front_acts = after(front_low, *front_acts)
-    front_shrink_part = [matmul_left(act, front_branches).astype(narrow) for act in front_acts]
-    front_got, out_got, front_shrink_part = lax.optimization_barrier(
-        (swap(front_low, "y2"), return_four(out_part), front_shrink_part)
-    )
-    front_shrink_part = [reduced(part, "x") for part in front_shrink_part]
-    front_norm_grad = front_part[:rows] + front_got.astype(wide)
+    back_acts = after(front_branch, *back_acts)
+    shrink_part, _ = mat_grads([back_acts], back_branches)
+    branch_got, shrink_part, *out_got = lax.optimization_barrier(
+        (swap(front_branch, "y2"), shrink_part, *return_four(out_parts))
+    )
+    back_grads = [reduced(shrink_part, "x"), expand_grad]
+    *got_pre_grads, got_part = front_backward(
+        branch_got, (got_slope_a, got_slope_b), front_side[-1], narrow
+    )
+    *own_pre_grads, own_part = front_backward(
+        front_branch, (own_slope_a, own_slope_b), front_side[-1], wide
+    )
+    late = after(got_part, *own_acts, *got_acts)
+    front_shrink_part, _ = mat_grads(list(zip(late[:2], late[2:])), (front_branch, branch_got))
+    front_got, front_shrink_part = lax.optimization_barrier((swap(got_part, "y2"), front_shrink_part))
+    front_shrink_part = reduced(front_shrink_part, "x")
+    front_norm_grad = own_part + front_got.astype(wide)
     first_grad = norm_back(front_norm_grad * front_gain, front_xhat, front_inverse)
-    branches = front_out + total(out_part[:rows], out_got) + back_offset
+    branches = front_out + total(out_parts[0], out_got) + back_offset
     logit_grad = jnp.sum(ct_rows * branches, -1, keepdims=True) * gate * (1.0 - gate)
     sent_grad = (logit_grad * centre + middle_grad + first_grad).astype(narrow)
 
     sent_blocks = pack_back(sent_grad)
-    normed_late, *front_pre_late = after(sent_blocks, front_normed, *front_pre_grads)
-    front_expand_part = [matmul_left(grad, normed_late).astype(narrow) for grad in front_pre_late]
+    pre_late = after(sent_blocks, *own_pre_grads, *got_pre_grads)
+    front_expand_part, front_lifts = mat_grads(
+        list(zip(pre_late[:2], pre_late[2:])), (front_normed, normed_got)
+    )
     sent_blocks, front_expand_part, back_grads = lax.optimization_barrier(
         (exchange(sent_blocks, GROUP), front_expand_part, back_grads)
     )
-    front_expand_part = [reduced(part, "x") for part in front_expand_part]
+    front_expand_part = reduced(front_expand_part, "x")
     getter = (send_index[:, None] == jnp.arange(slots)[None, :]).astype(narrow)
     hidden_grad, context_grad, out_low = hidden_back(
         sent_blocks.reshape(slots, width), getter, cotangent, outmat
     )
     grads = exchange(context_grad, GROUP)
+    expert_sums = row_sums(
+        *after(
+            context_grad, front_norm_grad, front_xhat, front_branch, back_norm_grad, back_xhat,
+            back_branches[0], logit_grad, stream,
+        )
+    )[:7].reshape(7, 16, 64)
     context, out_late = after(context_grad, context, out_low)
     out_part = matmul_left(context, out_late).astype(narrow).reshape(experts, 128, width)
-    grads, out_part = lax.optimization_barrier((grads, out_part))
+    grads, out_part, expert_sums = lax.optimization_barrier((grads, out_part, expert_sums))
     out_part = exchange(out_part, GROUP)
-    grads, xhat_all, front_shrink_part = lax.optimization_barrier((grads, xhat_all, front_shrink_part))
+    grads, front_shrink_part = lax.optimization_barrier((grads, front_shrink_part))
 
     dqkv, three, sums = attend_back(low, qkv, grads, full, lse, segcol, segrow, xhat_all)
 
-    out_part = jnp.sum(out_part.astype(wide), 0).astype(narrow).reshape(16, 8, 8, 128)
+    out_part = jnp.sum(after(sums, out_part).astype(wide), 0).astype(narrow).reshape(16, 8, 8, 128)
     biases = jnp.concatenate(
         [
             sums.reshape(16, 24),
@@ -589,22 +795,10 @@
         ],
         1,
     ).astype(narrow)
-    expert_sums = jnp.stack(
-        [
-            jnp.sum(front_norm_grad * front_xhat, 0),
-            jnp.sum(front_norm_grad, 0),
-            jnp.sum(front_branch.astype(wide), 0),
-            jnp.sum(back_norm_grad * back_xhat, 0),
-            jnp.sum(back_norm_grad, 0),
-            jnp.sum(back_branch.astype(wide), 0),
-            jnp.sum(logit_grad * stream, 0),
-        ]
-    ).reshape(7, 16, 64)
-    front_lifts = jnp.stack([jnp.sum(grad.astype(wide), 0).reshape(4, 256) for grad in front_pre_late], 1)
+    front_lifts, back_lifts = front_lifts[:, :, 0], back_lifts[:, 0, 0]
     front_lifts = jnp.where(y1_at == 0, front_lifts, front_lifts[:, ::-1])
     front_lifts = jnp.where(jnp.arange(2)[:, None] == y2_at, front_lifts[:, :, None], 0.0)
-    back_lifts = jnp.sum(back_pre_late.astype(wide), 0).reshape(1, 4, 256)
-    back_lifts = jnp.where(jnp.arange(4)[:, None, None] == x_at, back_lifts, 0.0)
+    back_lifts = jnp.where(jnp.arange(4)[:, None] == y_at, back_lifts[:, None], 0.0)
     packed = jnp.concatenate(
         [
             jnp.transpose(expert_sums, (1, 0, 2)).reshape(16, 448),
@@ -623,7 +817,7 @@
         ],
         1,
     )
-    front_swap = swap(front_shrink_part[1], "y1")
+    front_swap = swap(front_shrink_part[0, 1], "y1")
     slices, front_swap, front_expand_part = lax.optimization_barrier(
         (exchange(slices, DATA), front_swap, front_expand_part)
     )
@@ -644,7 +838,7 @@
     querybias_grad, _, valuebias_grad = biases
 
     dqkv, returned, front_expand_own, other = after(
-        slices, dqkv, pack_back((gate * branches).astype(narrow)), *front_expand_part
+        slices, dqkv, pack_back((gate * branches).astype(narrow)), *front_expand_part[0]
     )
     own, returned, other = lax.optimization_barrier(
         (exchange(dqkv, GROUP), exchange(returned, GROUP), swap(other, "y1"))
@@ -659,8 +853,8 @@
         attn_norm_grad * attngain.astype(wide), attn_xhat, attn_inverse
     )
     result = (hidden + unpack_back(returned)).astype(narrow)
-    back_shrink_grad, back_expand_grad = (grad.astype(wide) for grad in back_grads)
-    front_shrink_grad = front_shrink_part[0].astype(wide) + front_swap.astype(wide)
+    back_shrink_grad, back_expand_grad = (grad[0, 0].astype(wide) for grad in back_grads)
+    front_shrink_grad = front_shrink_part[0, 0].astype(wide) + front_swap.astype(wide)
     front_expand_grad = front_expand_own.astype(wide) + other.astype(wide)
     back_shrink_grad, front_shrink_grad = back_shrink_grad[None], front_shrink_grad[None]
     back_expand_grad, front_expand_grad = back_expand_grad.T[None], front_expand_grad.T[None]

time: 620 us -> 551 us (0.89)
  Pallas kernels: 55.5 us -> 146 us
  matrix products: 89.7 us -> 14.7 us
  waiting for transfers between devices: 226 us -> 158 us
  other arithmetic: 45.3 us -> 30.4 us
    pallas_call x0 -> x14, Pallas kernels: none -> 87.1 us  [the longest x8 60.6 us: expert_call(): pl.pallas_call(kernel, grid=(4,), out_shape=[pltpu.HBM((256, 1024), dtype...]
    ppermute x12, waiting for transfers between devices: 67.4 us -> 24 us  [shift_by(): return lax.ppermute(value, COLUMN, [(i, (i + step) % 4) for i in range(4)])]
    dot_general x9 -> x3, matrix products: 31.5 us -> 2.59 us  [matmul_right(): lax.dot_general(left, right, (((1,), (1,)), ((), ())), preferred_element_...]
    dot_general x10 -> x4, matrix products: 35 us -> 7.79 us  [matmul_left(): lax.dot_general(left, right, (((0,), (0,)), ((), ())), preferred_element_...]
    dot_general x10 -> x4, matrix products: 23.1 us -> 4.35 us  [matmul(): return jnp.dot(left, right, preferred_element_type=wide)]
    all_gather x7 -> x4, waiting for transfers between devices: 18.3 us -> 0.04 us  [the longest x3 0.03 us: gathered(): return lax.all_gather(matrix, axes, axis=0)]
    unnamed x209 -> x199, local copies, waits for them, and re-layouts: 44.7 us -> 56.4 us
    all_to_all x12, starting transfers between devices: 66.2 us -> 76.2 us  [exchange(): return lax.all_to_all(blocks, axes, 0, 0, tiled=True)]
  transfers between devices with their start and end apart: 45 -> 40, of which waited for: 25 -> 22; matrix products, arithmetic and copies ran while one was open for 25% -> 11% of each run, Pallas kernels for 8% -> 25%
where the time goes in v3:
time: 551 us; the launch traced here: 540 us
  waiting for transfers between devices  158 us (29%)
  Pallas kernels  146 us (26%)
  starting transfers between devices  104 us (19%)
  local copies, waits for them, and re-layouts  72.3 us (13%)
  other arithmetic  30.4 us (6%)
  between operations  15.2 us (3%)
  matrix products  14.7 us (3%)
    all_to_all x12, starting transfers between devices, exchange(): return lax.all_to_all(blocks, axes, 0, 0, tiled=True)  76.2 us
    pallas_call x8, Pallas kernels, expert_call(): pl.pallas_call(kernel, grid=(4,), out_shape=[pltpu.HBM((256, 1024), dtype...  60.6 us
    ppermute x7, waiting for transfers between devices, swap(): return lax.ppermute(value, axis, [(0, 1), (1, 0)])  60.1 us
    unnamed x199, local copies, waits for them, and re-layouts  56.4 us
    all_to_all x12, waiting for transfers between devices, exchange(): return lax.all_to_all(blocks, axes, 0, 0, tiled=True)  50.8 us
    ppermute x12, waiting for transfers between devices, shift_by(): return lax.ppermute(value, COLUMN, [(i, (i + step) % 4) for i in range(4)])  24 us
    pallas_call x4, Pallas kernels, mat_grads(): pl.pallas_call(lambda *refs: mat_grads_kernel(count, sides, *refs), grid=...  23.7 us
    pallas_call x1, Pallas kernels, attend_back(): pl.pallas_call(attend_back_kernel, out_shape=(jax.ShapeDtypeStruct((block...  19.6 us
  transfers between devices with their start and end apart: 40, of which 22 were waited for; matrix products, arithmetic and copies ran while one was open for 11% of the time, Pallas kernels for 25%

profile of v3, /device:TPU:1, one launch (start us, length us, event | category | flops | bytes accessed | tf_op | source)
XLA Modules:
  0.0 540.1 jit_solution(6136383934470109422)
XLA Ops:
  18.3 8.1 %project.1 = (bf16[8,256,384]{2,1,0:T(8,128)(2,1)S(1)}, bf16[256,1024]{1,0:T(8,128)(2,1)S(1)}) custom-call(bf16[256,1024]{1,0:T(8,128)(2,1)S(1)} %copy-done.7, bf16[1,1024]{1,0:T(2,128)(2,1)S(1)} %reshape.406.gain_ref, bf16[1,1024]{1,0:T(2,128)(2,1)S(1)} %reshape.407.shift_ref, bf16[1024,1024]{1,0:T(8,128)(2,1)} %query_ref.3, bf16[1024,1024]{1,0:T(8,128)(2,1)} %key_ref.3, ...), custom_call_target="tpu_custom_call" | custom-call | tf_op jit(solution)/shard_map/project/pallas_call | solution.py:323
  42.8 11.3 %all-to-all-done.1.qkv_ref = bf16[8,256,384]{2,1,0:T(8,128)(2,1)S(1)} async-done(((bf16[8,256,384]{2,1,0:T(8,128)(2,1)}), bf16[8,256,384]{2,1,0:T(8,128)(2,1)S(1)}, u32[]{:S(2)}, u32[]{:S(2)}) %all-to-all-start.1) | async-done | bytes 1572896 | tf_op jit(solution)/shard_map/all_to_all | solution.py:80
  71.3 15.7 %attend.1 = (bf16[8,256,128]{2,1,0:T(8,128)(2,1)}, f32[8,128,256]{2,1,0:T(8,128)S(1)}, f32[8,8,256]{2,1,0:T(8,128)S(1)}) custom-call(s32[8]{0:T(128)S(1)} %convert_reduce_fusion.2.low_ref, bf16[8,256,384]{2,1,0:T(8,128)(2,1)S(1)} %all-to-all-done.1.qkv_ref, s32[8,256,1]{2,1,0:T(8,128)S(1)} %copy-done.15, s32[8,1,256]{2,1,0:T(1,128)S(1)} %get-tuple-element.436.segrow_ref), custom_call_target="tpu_custom_call" | custom-call | tf_op jit(solution)/shard_map/attend/pallas_call | solution.py:452
  93.9 9.2 %all-to-all-done.3.ctx_ref = bf16[8,256,128]{2,1,0:T(8,128)(2,1)S(1)} async-done(((bf16[8,256,128]{2,1,0:T(8,128)(2,1)}), bf16[8,256,128]{2,1,0:T(8,128)(2,1)S(1)}, u32[]{:S(2)}, u32[]{:S(2)}) %all-to-all-start.3) | async-done | bytes 524320 | tf_op jit(solution)/shard_map/all_to_all | solution.py:80
  115.4 11.7 %all-to-all-done.4 = bf16[8,48,1024]{2,1,0:T(8,128)(2,1)S(1)} async-done(((bf16[8,48,1024]{2,1,0:T(8,128)(2,1)}), bf16[8,48,1024]{2,1,0:T(8,128)(2,1)S(1)}, u32[]{:S(2)}, u32[]{:S(2)}) %all-to-all-start.4) | async-done | bytes 786464 | tf_op jit(solution)/shard_map/all_to_all | solution.py:80
  137.6 8.7 %front_forward.2 = (bf16[256,1024]{1,0:T(8,128)(2,1)}, bf16[256,1024]{1,0:T(8,128)(2,1)}, f32[256,1024]{1,0:T(8,128)}, f32[256,1024]{1,0:T(8,128)}, bf16[256,1024]{1,0:T(8,128)(2,1)}, /*index=5*/f32[256,1024]{1,0:T(8,128)S(1)}) custom-call(bf16[256,1024]{1,0:T(8,128)(2,1)} %get-tuple-element.418.xhat_ref, f32[1,1024]{1,0:T(1,128)S(1)} %reshape.415.gain_ref, ...), custom_call_target="tpu_custom_call" | custom-call | tf_op jit(solution)/shard_map/front_forward/pallas_call | solution.py:140
  154.4 8.6 %front_forward.3 = (bf16[256,1024]{1,0:T(8,128)(2,1)}, bf16[256,1024]{1,0:T(8,128)(2,1)}, f32[256,1024]{1,0:T(8,128)}, f32[256,1024]{1,0:T(8,128)}, bf16[256,102...) custom-call(bf16[256,1024]{1,0:T(8,128)(2,1)} %collective-permute-done.1.xhat_ref, f32[1,1024]{1,0:T(1,128)S(1)} %reshape.415.gain_ref, ...), custom_call_target="tpu_custom_call" | custom-call | tf_op jit(solution)/shard_map/front_forward/pallas_call | solution.py:140
  166.1 10.6 %collective-permute-done.4.branch_ref.refs_7_ = bf16[256,1024]{1,0:T(8,128)(2,1)S(1)} collective-permute-done((bf16[256,1024]{1,0:T(8,128)(2,1)S(1)}, bf16[256,1024]{1,0:T(8,128)(2,1)S(1)}, u32[]{:S(2)}, u32[]{:S(2)}) %collective-permute-start.4) | collective-permute-done | bytes 524320 | tf_op jit(solution)/shard_map/ppermute | solution.py:59
  178.4 11.2 %collective-permute-done.5 = bf16[256,1024]{1,0:T(8,128)(2,1)} collective-permute-done((bf16[256,1024]{1,0:T(8,128)(2,1)}, bf16[256,1024]{1,0:T(8,128)(2,1)}, u32[]{:S(2)}, u32[]{:S(2)}) %collective-permute-start.5) | collective-permute-done | bytes 524320 | tf_op jit(solution)/shard_map/ppermute | solution.py:55
  194.5 8.9 %collective-permute-done.8.rows_ref.refs_6_ = bf16[256,1024]{1,0:T(8,128)(2,1)} collective-permute-done((bf16[256,1024]{1,0:T(8,128)(2,1)}, bf16[256,1024]{1,0:T(8,128)(2,1)}, u32[]{:S(2)}, u32[]{:S(2)}) %collective-permute-start.8) | collective-permute-done | bytes 524320 | tf_op jit(solution)/shard_map/ppermute | solution.py:59
  206.7 7.1 %back_both.6 = (bf16[256,1024]{1,0:T(8,128)(2,1)}, bf16[256,1024]{1,0:T(8,128)(2,1)}, bf16[256,1024]{1,0:T(8,128)(2,1)S(1)}, bf16[256,1024]{1,0:T(8,128)(2,1)}) custom-call(bf16[256,1024]{1,0:T(8,128)(2,1)} %collective-permute-done.8.rows_ref.refs_6_, bf16[256,1024]{1,0:T(8,128)(2,1)S(1)} %copy-done.38, f32[1,1024]{1,0:T(1,128)S(1)} %bitcast.141, ...), custom_call_target="tpu_custom_call" | custom-call | tf_op jit(solution)/shard_map/back_both/pallas_call | solution.py:140
  215.4 7.2 %back_both.5 = (bf16[256,1024]{1,0:T(8,128)(2,1)}, bf16[256,1024]{1,0:T(8,128)(2,1)}, bf16[256,1024]{1,0:T(8,128)(2,1)S(1)}, bf16[256,1024]{1,0:T(8,128)(2,1)}) custom-call(bf16[256,1024]{1,0:T(8,128)(2,1)} %collective-permute-done.6.rows_ref.refs_5_, bf16[256,1024]{1,0:T(8,128)(2,1)S(1)} %copy-done.35, f32[1,1024]{1,0:T(1,128)S(1)} %bitcast.142, ...), custom_call_target="tpu_custom_call" | custom-call | tf_op jit(solution)/shard_map/back_both/pallas_call | solution.py:140
  223.9 7.3 %back_both.7 = (bf16[256,1024]{1,0:T(8,128)(2,1)}, bf16[256,1024]{1,0:T(8,128)(2,1)}, bf16[256,1024]{1,0:T(8,128)(2,1)S(1)}, bf16[256,1024]{1,0:T(8,128)(2,1)}) custom-call(bf16[256,1024]{1,0:T(8,128)(2,1)} %collective-permute-done.10.rows_ref.refs_7_, bf16[256,1024]{1,0:T(8,128)(2,1)S(1)} %copy-done.41, f32[1,1024]{1,0:T(1,128)S(1)} %bitcast.143, ...), custom_call_target="tpu_custom_call" | custom-call | tf_op jit(solution)/shard_map/back_both/pallas_call | solution.py:140
  265.1 10.0 %collective-permute-done.12.rows_ref.refs_5_ = bf16[256,1024]{1,0:T(8,128)(2,1)S(1)} collective-permute-done((bf16[256,1024]{1,0:T(8,128)(2,1)S(1)}, bf16[256,1024]{1,0:T(8,128)(2,1)S(1)}, u32[]{:S(2)}, u32[]{:S(2)}) %collective-permute-start.12) | collective-permute-done | bytes 524320 | tf_op jit(solution)/shard_map/ppermute | solution.py:55
  277.1 7.3 %front_backward.3 = (bf16[256,1024]{1,0:T(8,128)(2,1)}, bf16[256,1024]{1,0:T(8,128)(2,1)}, bf16[256,1024]{1,0:T(8,128)(2,1)S(1)}) custom-call(bf16[256,1024]{1,0:T(8,128)(2,1)S(1)} %copy-done.31, f32[256,1024]{1,0:T(8,128)} %get-tuple-element.228.slope_a_ref, f32[256,1024]{1,0:T(8,128)} %get-tuple-element.229.slope_b_ref, bf16[4,512,1024]{2,1,0:T(8,128)(2,1)} %bitcast.155, ...), custom_call_target="tpu_custom_call" | custom-call | tf_op jit(solution)/shard_map/front_backward/pallas_call | solution.py:140
  294.2 7.4 %front_backward.2 = (bf16[256,1024]{1,0:T(8,128)(2,1)}, bf16[256,1024]{1,0:T(8,128)(2,1)}, f32[256,1024]{1,0:T(8,128)S(1)}) custom-call(bf16[256,1024]{1,0:T(8,128)(2,1)S(1)} %fusion.15.rows_ref.refs_4_.front_branch_ref, f32[256,1024]{1,0:T(8,128)} %get-tuple-element.224.slope_a_ref, f32[256,1024]{1,0:T(8,128)} %get-tuple-element.225.slope_b_ref, ...), custom_call_target="tpu_custom_call" | custom-call | tf_op jit(solution)/shard_map/front_backward/pallas_call | solution.py:140
  307.5 16.1 %all-to-all-start.6 = ((bf16[8,48,1024]{2,1,0:T(8,128)(2,1)}), bf16[8,48,1024]{2,1,0:T(8,128)(2,1)}, u32[]{:S(2)}, u32[]{:S(2)}) async-start(bf16[8,48,1024]{2,1,0:T(8,128)(2,1)} %bitcast.169), calls=%async_computation.6 | async-start | bytes 1572864 | tf_op jit(solution)/shard_map/all_to_all | solution.py:80
  365.2 7.2 %reduce-scatter.9.cloned.1.call-done = bf16[1,2,256,1024]{3,2,1,0:T(8,128)(2,1)} async-done(((bf16[4,2,256,1024]{3,2,1,0:T(8,128)(2,1)}), bf16[1,2,256,1024]{3,2,1,0:T(8,128)(2,1)}) %reduce-scatter.9.cloned.1.call-update) | async-done | bytes 1048592 | tf_op jit(solution)/shard_map/reduce_scatter | solution.py:634
  377.1 19.6 %attend_back.1 = (bf16[8,256,384]{2,1,0:T(8,128)(2,1)}, bf16[16,192,128]{2,1,0:T(8,128)(2,1)S(1)}, f32[1,384]{1,0:T(1,128)S(1)}) custom-call(s32[8]{0:T(128)S(1)} %convert_reduce_fusion.2.low_ref, bf16[8,256,384]{2,1,0:T(8,128)(2,1)S(1)} %copy-done.14, bf16[8,256,128]{2,1,0:T(8,128)(2,1)} %all-to-all-done.7.grad_ref, f32[8,128,256]{2,1,0:T(8,128)S(1)} %copy-done.45, ...), custom_call_target="tpu_custom_call" | custom-call | tf_op jit(solution)/shard_map/attend_back/pallas_call | solution.py:534
  409.2 21.4 %collective-permute-done.17 = bf16[256,1024]{1,0:T(8,128)(2,1)} collective-permute-done((bf16[256,1024]{1,0:T(8,128)(2,1)S(1)}, bf16[256,1024]{1,0:T(8,128)(2,1)}, u32[]{:S(2)}, u32[]{:S(2)}) %collective-permute-start.17) | collective-permute-done | bytes 524320 | tf_op jit(solution)/shard_map/ppermute | solution.py:55
  443.7 11.2 %all-to-all-done.11 = bf16[8,48,1024]{2,1,0:T(8,128)(2,1)S(1)} async-done(((bf16[8,48,1024]{2,1,0:T(8,128)(2,1)}), bf16[8,48,1024]{2,1,0:T(8,128)(2,1)S(1)}, u32[]{:S(2)}, u32[]{:S(2)}) %all-to-all-start.11) | async-done | bytes 786464 | tf_op jit(solution)/shard_map/all_to_all | solution.py:80
  473.5 11.2 %collective-permute-done.18 = bf16[256,1024]{1,0:T(8,128)(2,1)} collective-permute-done((bf16[256,1024]{1,0:T(8,128)(2,1)}, bf16[256,1024]{1,0:T(8,128)(2,1)}, u32[]{:S(2)}, u32[]{:S(2)}) %collective-permute-start.18) | collective-permute-done | bytes 524320 | tf_op jit(solution)/shard_map/ppermute | solution.py:55
  500.2 13.5 %all-gather.19.cloned.1.call-done = bf16[33792,128]{1,0:T(8,128)(2,1)} async-done(((bf16[264,128]{1,0:T(8,128)(2,1)}), bf16[33792,128]{1,0:T(8,128)(2,1)}) %all-gather.19.cloned.1.call-update) | async-done | bytes 8650768 | tf_op jit(solution)/shard_map/all_gather | solution.py:827
  521.6 8.7 %unpack.1 = (f32[1024,1024]{1,0:T(8,128)}, f32[1024,1024]{1,0:T(8,128)}, f32[1024,1024]{1,0:T(8,128)}, f32[8,16,8,1024]{3,2,1,0:T(8,128)}, f32[16,64,2]{2,1,0:T(8,128)S(1)}) custom-call(bf16[16,8,264,128]{3,2,1,0:T(8,128)(2,1)S(1)} %bitcast.139, f32[3,1024]{1,0:T(4,128)S(1)} %bitcast.145, bf16[16,64,1]{2,1,0:T(8,128)(2,1)S(1)} %reshape.454.gain_ref, ...), custom_call_target="tpu_custom_call" | custom-call | tf_op jit(solution)/shard_map/unpack/pallas_call | solution.py:588
  (420 shorter events, 265.7 us)
Async XLA Ops:
  7.3 80.7 %all-gather.11.cloned.1.call-start = ((), (), s32[]{:S(2)}) async-start(), calls=%async_computation.20 | async-start | bytes 5242880 | tf_op jit(solution)/shard_map/all_gather | solution.py:637
  28.4 25.8 %all-to-all-start.1 = ((bf16[8,256,384]{2,1,0:T(8,128)(2,1)}), bf16[8,256,384]{2,1,0:T(8,128)(2,1)S(1)}, u32[]{:S(2)}, u32[]{:S(2)}) async-start(bf16[8,256,384]{2,1,0:T(8,128)(2,1)} %copy-done.43), calls=%async_computation.1 | async-start | bytes 3145728 | tf_op jit(solution)/shard_map/all_to_all | solution.py:80
  33.3 104.3 %all-gather.13.cloned.1.call-start = ((), (), s32[]{:S(2)}) async-start(), calls=%async_computation.21 | async-start | bytes 5242880 | tf_op jit(solution)/shard_map/all_gather | solution.py:637
  33.3 26.4 %collective-permute-start = (bf16[512,1024]{1,0:T(8,128)(2,1)S(1)}, bf16[512,1024]{1,0:T(8,128)(2,1)}, u32[]{:S(2)}, u32[]{:S(2)}) collective-permute-start(bf16[512,1024]{1,0:T(8,128)(2,1)S(1)} %copy-done.62), channel_id=1, source_target_pairs={{0,16},{16,0},{1,17},{17,1},{2,18},{18,2},{3,19},{19,3},{4,20},{20... | collective-permute-start | bytes 3145736 | tf_op jit(solution)/shard_map/ppermute | solution.py:55
  59.7 134.7 %all-gather.15.cloned.1.call-start = ((), (), s32[]{:S(2)}) async-start(), calls=%async_computation.22 | async-start | bytes 5242880 | tf_op jit(solution)/shard_map/all_gather | solution.py:637
  61.8 26.2 %all-to-all-start.2 = ((bf16[16,8,128]{2,1,0:T(8,128)(2,1)}), bf16[16,8,128]{2,1,0:T(8,128)(2,1)S(1)}, u32[]{:S(2)}, u32[]{:S(2)}) async-start(bf16[16,8,128]{2,1,0:T(8,128)(2,1)} %broadcast_in_dim.134), calls=%async_computation.2 | async-start | bytes 65536 | tf_op jit(solution)/shard_map/all_to_all | solution.py:80
  135.5 112.5 %all-gather.17.cloned.1.call-start = ((), (), s32[]{:S(2)}) async-start(), calls=%async_computation.23 | async-start | bytes 4718592 | tf_op jit(solution)/shard_map/all_gather | solution.py:722
  153.3 23.4 %collective-permute-start.4 = (bf16[256,1024]{1,0:T(8,128)(2,1)S(1)}, bf16[256,1024]{1,0:T(8,128)(2,1)S(1)}, u32[]{:S(2)}, u32[]{:S(2)}) collective-permute-start(bf16[256,1024]{1,0:T(8,128)(2,1)S(1)} %get-tuple-element.265.branch_ref.refs_4_.back_branch_ref), channel_id=1, source_target_pairs={{0,16},{8,24},{16,0},{24,8},{1,17},{9,25},{17,1},{25,9},{2,18},{10... | collective-permute-start | bytes 1572872 | tf_op jit(solution)/shard_map/ppermute | solution.py:59
  177.5 158.5 %reduce-scatter.7.cloned.1.call-start = ((), (), s32[]{:S(2)}) async-start(), calls=%async_computation.17 | async-start | bytes 2621440 | tf_op jit(solution)/shard_map/reduce_scatter | solution.py:634
  192.3 23.0 %collective-permute-start.6 = (bf16[256,1024]{1,0:T(8,128)(2,1)}, bf16[256,1024]{1,0:T(8,128)(2,1)}, u32[]{:S(2)}, u32[]{:S(2)}) collective-permute-start(bf16[256,1024]{1,0:T(8,128)(2,1)} %get-tuple-element.414.rows_ref.refs_4_), channel_id=1, source_target_pairs={{0,8},{8,16},{16,24},{24,0},{1,9},{9,17},{17,25},{25,1},{2,10},{10... | collective-permute-start | bytes 1572872 | tf_op jit(solution)/shard_map/ppermute | solution.py:59
  193.8 30.1 %collective-permute-start.10 = (bf16[256,1024]{1,0:T(8,128)(2,1)}, bf16[256,1024]{1,0:T(8,128)(2,1)}, u32[]{:S(2)}, u32[]{:S(2)}) collective-permute-start(bf16[256,1024]{1,0:T(8,128)(2,1)} %get-tuple-element.414.rows_ref.refs_4_), channel_id=1, source_target_pairs={{0,16},{8,24},{16,0},{24,8},{1,17},{9,25},{17,1},{25,9},{2,18},{10... | collective-permute-start | bytes 1572872 | tf_op jit(solution)/shard_map/ppermute | solution.py:59
  213.9 32.6 %collective-permute-start.9 = (bf16[256,1024]{1,0:T(8,128)(2,1)S(1)}, bf16[256,1024]{1,0:T(8,128)(2,1)S(1)}, u32[]{:S(2)}, u32[]{:S(2)}) collective-permute-start(bf16[256,1024]{1,0:T(8,128)(2,1)S(1)} %get-tuple-element.192), channel_id=1, source_target_pairs={{0,8},{8,16},{16,24},{24,0},{1,9},{9,17},{17,25},{25,1},{2,10},{10... | collective-permute-start | bytes 1572872 | tf_op jit(solution)/shard_map/ppermute | solution.py:59
  222.5 23.9 %collective-permute-start.7 = (bf16[256,1024]{1,0:T(8,128)(2,1)S(1)}, bf16[256,1024]{1,0:T(8,128)(2,1)S(1)}, u32[]{:S(2)}, u32[]{:S(2)}) collective-permute-start(bf16[256,1024]{1,0:T(8,128)(2,1)S(1)} %get-tuple-element.190), channel_id=1, source_target_pairs={{0,24},{8,0},{16,8},{24,16},{1,25},{9,1},{17,9},{25,17},{2,26},{10... | collective-permute-start | bytes 1572872 | tf_op jit(solution)/shard_map/ppermute | solution.py:59
  248.0 88.0 %reduce-scatter.5.cloned.1.call-start = ((), (), s32[]{:S(2)}) async-start(), calls=%async_computation.16 | async-start | bytes 2621440 | tf_op jit(solution)/shard_map/reduce_scatter | solution.py:634
  254.4 20.7 %collective-permute-start.12 = (bf16[256,1024]{1,0:T(8,128)(2,1)S(1)}, bf16[256,1024]{1,0:T(8,128)(2,1)S(1)}, u32[]{:S(2)}, u32[]{:S(2)}) collective-permute-start(bf16[256,1024]{1,0:T(8,128)(2,1)S(1)} %fusion.15.rows_ref.refs_4_.front_branch_ref), channel_id=1, source_target_pairs={{0,8},{8,0},{1,9},{9,1},{2,10},{10,2},{3,11},{11,3},{4,12},{12,4},... | collective-permute-start | bytes 1572872 | tf_op jit(solution)/shard_map/ppermute | solution.py:55
  276.0 96.4 %reduce-scatter.9.cloned.1.call-start = ((), (), s32[]{:S(2)}) async-start(), calls=%async_computation.18 | async-start | bytes 5242880 | tf_op jit(solution)/shard_map/reduce_scatter | solution.py:634
  307.5 28.6 %all-to-all-start.6 = ((bf16[8,48,1024]{2,1,0:T(8,128)(2,1)}), bf16[8,48,1024]{2,1,0:T(8,128)(2,1)}, u32[]{:S(2)}, u32[]{:S(2)}) async-start(bf16[8,48,1024]{2,1,0:T(8,128)(2,1)} %bitcast.169), calls=%async_computation.6 | async-start | bytes 1572864 | tf_op jit(solution)/shard_map/all_to_all | solution.py:80
  323.7 109.1 %reduce-scatter.11.cloned.1.call-start = ((), (), s32[]{:S(2)}) async-start(), calls=%async_computation.19 | async-start | bytes 5242880 | tf_op jit(solution)/shard_map/reduce_scatter | solution.py:634
  358.9 37.7 %all-to-all-start.8 = ((bf16[8,128,1024]{2,1,0:T(8,128)(2,1)}), bf16[8,128,1024]{2,1,0:T(8,128)(2,1)}, u32[]{:S(2)}, u32[]{:S(2)}) async-start(bf16[8,128,1024]{2,1,0:T(8,128)(2,1)} %bitcast.167), calls=%async_computation.11 | async-start | bytes 4194304 | tf_op jit(solution)/shard_map/all_to_all | solution.py:80
  399.9 31.7 %all-to-all-start.9 = ((bf16[16,272,128]{2,1,0:T(8,128)(2,1)}), bf16[16,272,128]{2,1,0:T(8,128)(2,1)S(1)}, u32[]{:S(2)}, u32[]{:S(2)}) async-start(bf16[16,272,128]{2,1,0:T(8,128)(2,1)} %pad_maximum_fusion), calls=%async_computation.12 | async-start | bytes 2228224 | tf_op jit(solution)/shard_map/all_to_all | solution.py:80
  405.1 108.6 %all-gather.19.cloned.1.call-start = ((), (), s32[]{:S(2)}) async-start(), calls=%async_computation.24 | async-start | bytes 8718336 | tf_op jit(solution)/shard_map/all_gather | solution.py:827
  406.2 24.4 %collective-permute-start.17 = (bf16[256,1024]{1,0:T(8,128)(2,1)S(1)}, bf16[256,1024]{1,0:T(8,128)(2,1)}, u32[]{:S(2)}, u32[]{:S(2)}) collective-permute-start(bf16[256,1024]{1,0:T(8,128)(2,1)S(1)} %slice_bitcast_fusion.2), channel_id=1, source_target_pairs={{0,16},{16,0},{1,17},{17,1},{2,18},{18,2},{3,19},{19,3},{4,20},{20... | collective-permute-start | bytes 1572872 | tf_op jit(solution)/shard_map/ppermute | solution.py:55
  435.8 19.1 %all-to-all-start.11 = ((bf16[8,48,1024]{2,1,0:T(8,128)(2,1)}), bf16[8,48,1024]{2,1,0:T(8,128)(2,1)S(1)}, u32[]{:S(2)}, u32[]{:S(2)}) async-start(bf16[8,48,1024]{2,1,0:T(8,128)(2,1)} %bitcast.38), calls=%async_computation.15 | async-start | bytes 1572864 | tf_op jit(solution)/shard_map/all_to_all | solution.py:80
  455.7 28.9 %all-to-all-start.10 = ((bf16[8,256,384]{2,1,0:T(8,128)(2,1)}), bf16[8,256,384]{2,1,0:T(8,128)(2,1)S(1)}, u32[]{:S(2)}, u32[]{:S(2)}) async-start(bf16[8,256,384]{2,1,0:T(8,128)(2,1)} %get-tuple-element.286), calls=%async_computation.14 | async-start | bytes 3145728 | tf_op jit(solution)/shard_map/all_to_all | solution.py:80
  (109 other events, 913.8 us)
Sparse Core Ops, SparseCore 0:
  10.9 51.4 all-gather.10
  64.0 48.8 all-gather.12
  115.1 48.4 all-gather.14
  177.7 33.9 all-gather.16
  248.2 42.3 reduce-scatter.6
  293.5 29.3 reduce-scatter.4
  325.9 46.5 reduce-scatter.8
  375.5 57.1 reduce-scatter.10
  435.6 78.0 all-gather.18
